TPU v7x, 32 devices: a whole 2x2x4 slice. The times are simulated.
32 devices in a mesh: parts: 2 (over y), ctx: 4 (over z), width: 2 (over x), sub: 2 (over core).
Axes of the slice: x: 2, y: 2, z: 4, core: 2. Of those that a mesh axis runs over, the one named last changes fastest.
Arguments:
- tokens: bfloat16 [4096, 8192], P(('parts', 'ctx'), 'width'), parts along dimension 0, may hold values from -4 to 4
- norm_gain: float32 [8192], P('width'), may hold values from 0.25 to 1.75
- in_weight: bfloat16 [3, 8192, 2, 2048], P(None, 'width', 'sub', 'ctx'), may hold values from -0.09375 to 0.09375
- short_taps: float32 [3, 3, 2, 2048], P(None, None, 'sub', 'width'), may hold values from -3 to 3
- long_taps: float32 [128, 2, 2048], P(None, 'sub', 'width'), may hold values from -0.5 to 0.5
Outputs:
- output: bfloat16 [4096, 2, 2048], P(('parts', 'ctx'), 'sub', 'width'), parts along dimension 0
There are 2 independent parts, one for each index of `parts`. A program takes and returns all parts, laid end to end along the dimension named above; an argument that names none is the same for every part. Nothing has to cross between parts.
All inputs are finite; a program needn't handle non-finite values.
Results may differ from a plain program's by a relative error of at most 0.025.
Values may be sent and summed in bfloat16 or wider, within the bound.
No kernel may reach another device: no remote copies, remote signals or barrier semaphores. Data moves between devices by JAX's collectives and lax.ppermute only.
A program may use at most 192 MiB of HBM per device.

v0:
```python
import jax
import jax.numpy as jnp
from jax import lax
from jax.sharding import PartitionSpec as P

D = 8192


epsilon = 1e-05


def passed_along(value, axis, steps):
    count = lax.axis_size(axis)
    leading, last = (max(0, -steps), min(count, count - steps))
    return lax.ppermute(value, axis, [(source, source + steps) for source in range(leading, last)])


def short_filter(padded, tap_set):
    widened = padded.astype(jnp.float32)
    length_out = padded.shape[0] - 2
    return (
        tap_set[0] * widened[2:]
        + tap_set[1] * widened[1 : length_out + 1]
        + tap_set[2] * widened[:length_out]
    )


def gate_pair(streams):
    return (streams[:, 0] * streams[:, 1]).astype(jnp.bfloat16)


def medium_filter(extended, long_filter):
    inputs = extended.astype(jnp.float32)[None]
    kernel = long_filter[::-1][:, None, :]
    result = lax.conv_general_dilated(
        inputs,
        kernel,
        (1,),
        "VALID",
        dimension_numbers=("NWC", "WIO", "NWC"),
        feature_group_count=long_filter.shape[1],
        precision=lax.Precision.HIGHEST,
    )
    return result[0]


def shards(tokens, norm_gain, in_weight, short_taps, long_taps):
    values = tokens.astype(jnp.float32)
    power = lax.psum(jnp.sum(values * values, axis=1), "width")
    scaled = (values * lax.rsqrt(power / D + epsilon)[:, None] * norm_gain[None, :]).astype(
        jnp.bfloat16
    )
    partial_sums = jnp.einsum(
        "td,idk->tik",
        scaled,
        lax.all_gather(in_weight, "ctx", axis=3, tiled=True)[:, :, 0, :],
        preferred_element_type=jnp.float32,
    )
    projected = lax.psum_scatter(
        partial_sums.astype(jnp.bfloat16), "width", scatter_dimension=2, tiled=True
    )
    tap_set = short_taps[:, :, 0, :]
    long_filter = long_taps[:, 0, :]
    reach = long_filter.shape[0] - 1
    row_count = projected.shape[0]
    tail_filtered = short_filter(projected[row_count - reach - 2 :, 1:], tap_set[:, 1:])
    tail_gated = gate_pair(tail_filtered)
    before_rows, before_gated = passed_along((projected[row_count - 2 :], tail_gated), "ctx", 1)
    filtered = short_filter(jnp.concatenate([before_rows, projected], axis=0), tap_set)
    extended = jnp.concatenate([before_gated, gate_pair(filtered[:, 1:])], axis=0)
    query = filtered[:, 0]
    convolved = medium_filter(extended, long_filter)
    output = (query * convolved).astype(jnp.bfloat16)
    return output[:, None, :]


def solution(mesh):
    placed = (
        P(("parts", "ctx"), "width"),
        P("width"),
        P(None, "width", "sub", "ctx"),
        P(None, None, "sub", "width"),
        P(None, "sub", "width"),
    )
    return jax.shard_map(
        shards,
        mesh=mesh,
        in_specs=placed,
        out_specs=P(("parts", "ctx"), "sub", "width"),
        check_vma=False,
    )
```

profile of v0, /device:TPU:0, one launch (start us, length us, event | category | flops | bytes accessed | tf_op | source)
XLA Modules:
  0.0 1002.5 jit_solution(10612651653385447560)
XLA Ops:
  6.5 0.0 all-gather.2.cloned.1.call-start
  6.5 0.0 copy-start.3
  6.5 0.7 all-gather.2.cloned.1.call-update
  7.3 0.0 reduce-scatter.2.cloned.1.call-start
  7.3 3.1 fusion.2
  10.4 5.8 psum.7
  16.2 831.5 %all-gather.2.cloned.1.call-done = bf16[3,4096,1,2048]{3,1,0,2:T(8,128)(2,1)} async-done(((bf16[3,4096,1,512]{3,1,0,2:T(8,128)(2,1)}), bf16[3,4096,1,2048]{3,1,0,2:T(8,128)(2,1)}) %all-gather.2.cloned.1.call-update) | async-done | bytes 50331664 | tf_op jit(solution)/shard_map/all_gather | solution.py:56
  847.7 0.0 copy-done.3
  847.7 33.8 %fusion.7 = bf16[512,3,2048]{2,0,1:T(8,128)(2,1)} fusion(bf16[3,4096,1,2048]{3,1,0,2:T(8,128)(2,1)} %all-gather.2.cloned.1.call-done, bf16[512,4096]{1,0:T(8,128)(2,1)} %param.5, f32[4096]{0:T(1024)S(1)} %copy-done.3, f32[512]{0:T(512)S(1)} %add_rsqrt_fusion), kind=kOutput, calls=%fused_computation.12 | convolution fusion | flops 25781338112 | bytes 60835840 | tf_op jit(solution)/shard_map/td,idk->tik/dot_general | solution.py:53
  881.5 0.0 copy-start.2
  881.5 0.0 copy-start.1
  881.5 0.0 reduce-scatter.2.cloned.1.call-update
  881.5 0.7 copy-done.2
  882.3 0.3 copy-done.1
  882.5 0.1 copy.25
  882.6 0.2 rev.3
  882.9 74.0 %reduce-scatter.2.cloned.1.call-done = bf16[512,3,1024]{2,0,1:T(8,128)(2,1)} async-done(((bf16[512,3,2048]{2,0,1:T(8,128)(2,1)}), bf16[512,3,1024]{2,0,1:T(8,128)(2,1)}) %reduce-scatter.2.cloned.1.call-update) | async-done | bytes 3145744 | tf_op jit(solution)/shard_map/reduce_scatter | solution.py:59
  956.9 1.0 slice.86
  957.8 3.4 collective-permute-start
  961.2 1.2 slice_convert_fusion
  962.4 0.3 fusion.19
  962.8 0.1 fusion.23
  962.8 3.6 collective-permute-start.1
  966.4 0.0 collective-permute-done
  966.4 0.0 copy-done
  966.5 0.9 maximum_convert_fusion
  967.4 1.9 fusion.5
  969.3 0.3 fusion.18
  969.6 1.9 collective-permute-done.1
  971.5 0.3 maximum_bitcast_fusion
  971.8 22.5 %fusion.14 = f32[1,512,1024]{2,0,1:T(1,128)S(1)} fusion(bf16[1,639,1024]{2,1,0:T(8,128)(2,1)S(1)} %maximum_bitcast_fusion, f32[128,1,1024]{2,0,1:T(8,128)S(1)} %bitcast.39), kind=kOutput, calls=%fused_computation.17 | convolution fusion | flops 805306368 | bytes 3930112 | tf_op jit(solution)/shard_map/conv_general_dilated | solution.py:35
  994.3 1.4 fusion.17
  (7 shorter events, 0.1 us)
Async XLA Ops:
  6.5 841.1 %all-gather.2.cloned.1.call-start = ((), (), s32[]{:S(2)}) async-start(), calls=%async_computation.1 | async-start | bytes 62914560 | tf_op jit(solution)/shard_map/all_gather | solution.py:56
  6.5 841.1 %copy-start.3 = (f32[4096]{0:T(1024)S(1)}, f32[4096]{0:T(1024)}, u32[]{:S(2)}) copy-start(f32[4096]{0:T(1024)} %param.6) | copy-start | bytes 49156
  7.3 949.6 %reduce-scatter.2.cloned.1.call-start = ((), (), s32[]{:S(2)}) async-start(), calls=%async_computation.2 | async-start | bytes 9437184 | tf_op jit(solution)/shard_map/reduce_scatter | solution.py:59
  881.5 0.8 copy-start.2
  881.5 1.1 copy-start.1
  956.9 9.6 copy-start
  957.8 8.6 collective-permute-start
  962.8 8.7 collective-permute-start.1
Sparse Core Ops, SparseCore 0:
  8.9 838.7 all-gather.1
  881.6 75.2 reduce-scatter.1
where the time goes:
time: 1000 us
  waiting for transfers between devices  908 us (91%)
  matrix products  56.3 us (6%)
  between operations  13.5 us (1%)
    all_gather x1, waiting for transfers between devices, shards(): lax.all_gather(in_weight, 'ctx', axis=3, tiled=True)[:, :, 0, :]  831 us
    reduce_scatter x1, waiting for transfers between devices, shards(): lax.psum_scatter(partial_sums.astype(jnp.bfloat16), 'width', scatter_dime...  74 us
    dot_general x1, matrix products, shards(): jnp.einsum('td,idk->tik', scaled, lax.all_gather(in_weight, 'ctx', axis=3...  33.8 us
    conv_general_dilated x1, matrix products, medium_filter(): lax.conv_general_dilated(inputs, kernel, (1,), 'VALID', dimension_numbers...  22.5 us
  transfers between devices with their start and end apart: 4, of which 3 were waited for; matrix products, arithmetic and copies ran while one was open for 1% of the time, Pallas kernels for 0%

commit v1 on v0

v1 whole, which is shorter than its diff:
```python
import functools

import jax
import jax.numpy as jnp
import numpy as np
from jax import lax
from jax.experimental import pallas as pl
from jax.experimental.pallas import tpu as pltpu
from jax.sharding import PartitionSpec as P

EPSILON = 1e-05
HALO = 144
FFT = 256
STEP = 128
BF16 = jnp.bfloat16
F32 = jnp.float32


def split(matrix):
    high = np.asarray(matrix, np.float32).astype(jnp.bfloat16)
    low = (np.asarray(matrix, np.float32) - high.astype(np.float32)).astype(jnp.bfloat16)
    return high, low


def transforms():
    half = FFT // 2
    n = np.arange(FFT)
    k = np.arange(half)
    angle = 2.0 * np.pi * np.outer(k, n) / FFT
    real, imag = np.cos(angle), -np.sin(angle)
    imag[0] = np.cos(np.pi * n)
    forward = np.concatenate([real, imag], axis=0)
    weight = np.full((half,), 2.0)
    weight[0] = 1.0
    back_real = (weight[:, None] * np.cos(angle)).T / FFT
    back_imag = (-2.0 * np.sin(angle)).T / FFT
    back_imag[:, 0] = np.cos(np.pi * n) / FFT
    inverse = np.concatenate([back_real, back_imag], axis=1)[FFT - STEP :]
    return forward, inverse


def project_kernel(count, *refs):
    scalars, refs = refs[0], refs[1:]
    parts, weights, out = refs[:count], refs[count : 2 * count], refs[2 * count]
    total = jnp.dot(parts[0][...], weights[0][0], preferred_element_type=F32)
    for part, weight in zip(parts[1:], weights[1:]):
        total = total + jnp.dot(part[...], weight[0], preferred_element_type=F32)
    out[0] = total.astype(BF16)


def project(parts, weight, sub, column, kept):
    count = len(parts)
    rows, depth = parts[0].shape
    streams = weight.shape[0]
    if kept % 128 and kept != weight.shape[2]:
        weight = lax.dynamic_slice_in_dim(weight, column * kept, kept, 2)
        column = column * 0
    scalars = jnp.stack([sub, column]).astype(jnp.int32)

    def weight_spec(offset):
        return pl.BlockSpec(
            (1, depth, kept), lambda i, s: (i, lax.rem(s[0] + offset, count), s[1])
        )

    return pl.pallas_call(
        functools.partial(project_kernel, count),
        out_shape=jax.ShapeDtypeStruct((streams, rows, kept), BF16),
        grid_spec=pltpu.PrefetchScalarGridSpec(
            num_scalar_prefetch=1,
            grid=(streams,),
            in_specs=[pl.BlockSpec((rows, depth), lambda i, s: (0, 0)) for _ in parts]
            + [weight_spec(o) for o in range(count)],
            out_specs=pl.BlockSpec((1, rows, kept), lambda i, s: (i, 0, 0)),
        ),
        compiler_params=pltpu.CompilerParams(
            dimension_semantics=("arbitrary",), vmem_limit_bytes=24 << 20
        ),
        cost_estimate=pl.CostEstimate(
            flops=2 * rows * depth * count * streams * kept,
            bytes_accessed=2 * (rows * depth * count + depth * count * streams * kept + rows * streams * kept),
            transcendentals=0,
        ),
        name="project",
    )(scalars, *parts, *[weight] * count)


def filter_kernel(plan, terms, rows, *refs):
    flag, refs = refs[0], refs[1:]
    pieces = []
    for _ in plan:
        pieces.append(refs[:terms])
        refs = refs[terms:]
    near, far, short, spec_a, spec_b, spec_c, fh, fl, gh, gl, out, held, query, gated = refs
    tile = 64
    at = 0
    for (first, count, scale, scale_first, masked), sources in zip(plan, pieces):
        scales = (near, far)[scale]
        for low in range(0, count, tile):
            size = min(tile, count - low)
            factor = scales[0, scale_first + low : scale_first + low + size, :]
            if masked:
                factor = factor * flag[1].astype(F32)
            for stream in range(3):
                total = sources[0][stream, first + low : first + low + size, :].astype(F32)
                for source in sources[1:]:
                    total = total + source[stream, first + low : first + low + size, :].astype(F32)
                value = (total * factor).astype(BF16).astype(F32)
                held[stream, at + low : at + low + size, :] = value
        at += count

    def short_filter(stream, row, size):
        taps = [short[j, stream][None, :] for j in range(3)]
        return sum(taps[j] * held[stream, row - j : row - j + size, :] for j in range(3))

    lead = HALO - STEP
    for low in range(0, STEP + rows, tile):
        value = short_filter(1, lead + low, tile) * short_filter(2, lead + low, tile)
        gated[low : low + tile, :] = value.astype(BF16)
    for low in range(0, rows, tile):
        query[low : low + tile, :] = short_filter(0, HALO + low, tile)
    half = FFT // 2
    starts = [min(s, rows - STEP) for s in range(0, rows, STEP)]
    for start in starts:
        window = gated[start : start + FFT, :]
        spectrum = jnp.dot(fh[...], window, preferred_element_type=F32)
        spectrum = spectrum + jnp.dot(fl[...], window, preferred_element_type=F32)
        upper, lower = spectrum[:half], spectrum[half:]
        product = jnp.concatenate(
            [upper * spec_a[...] - lower * spec_b[...], upper * spec_b[...] + lower * spec_c[...]], axis=0
        )
        high = product.astype(BF16)
        rest = (product - high.astype(F32)).astype(BF16)
        result = jnp.dot(gh[...], high, preferred_element_type=F32)
        result = result + jnp.dot(gh[...], rest, preferred_element_type=F32)
        result = result + jnp.dot(gl[...], high, preferred_element_type=F32)
        out[start : start + STEP, :] = (result * query[start : start + STEP, :]).astype(BF16)


def filter_rows(plan, pieces, scales, index, follows, short, spectra, matrices, rows):
    terms = len(pieces[0])
    streams, _, kept = pieces[0][0].shape
    before = lax.rem(index + scales.shape[0] - 1, scales.shape[0])
    scalars = jnp.stack([index, follows, before]).astype(jnp.int32)
    arrays = [array for piece in pieces for array in piece]
    whole = lambda array: pl.BlockSpec(array.shape, lambda i, s, n=array.ndim: (0,) * n)
    scale_block = (1,) + scales.shape[1:]
    reach = HALO + rows
    constants = [short, *spectra, *matrices]
    return pl.pallas_call(
        functools.partial(filter_kernel, plan, terms, rows),
        out_shape=jax.ShapeDtypeStruct((rows, kept), BF16),
        grid_spec=pltpu.PrefetchScalarGridSpec(
            num_scalar_prefetch=1,
            grid=(1,),
            in_specs=[whole(a) for a in arrays]
            + [
                pl.BlockSpec(scale_block, lambda i, s: (s[0], 0, 0)),
                pl.BlockSpec(scale_block, lambda i, s: (s[2], 0, 0)),
            ]
            + [whole(c) for c in constants],
            out_specs=pl.BlockSpec((rows, kept), lambda i, s: (0, 0)),
            scratch_shapes=[
                pltpu.VMEM((streams, reach, kept), F32),
                pltpu.VMEM((rows, kept), F32),
                pltpu.VMEM((STEP + rows, kept), BF16),
            ],
        ),
        compiler_params=pltpu.CompilerParams(vmem_limit_bytes=24 << 20),
        cost_estimate=pl.CostEstimate(
            flops=2 * 5 * FFT * FFT * kept * (rows // STEP + 1),
            bytes_accessed=sum(a.size * 2 for a in arrays) + 2 * rows * kept,
            transcendentals=0,
        ),
        name="filter",
    )(scalars, *arrays, scales, scales, *constants)


def shards(tokens, norm_gain, in_weight, short_taps, long_taps):
    steps, across, cores = (lax.axis_size(a) for a in ("ctx", "width", "sub"))
    z, x, sub = (lax.axis_index(a) for a in ("ctx", "width", "sub"))
    rows, features = tokens.shape
    weight = in_weight[:, :, 0, :]
    panel = weight.shape[2]
    kept = panel // across
    group = steps // across
    owner = z // group
    depth = features // cores
    mid, small, late = rows // 2, 48, 192

    power = jnp.sum(tokens.astype(F32) ** 2, axis=1)

    def scaled_part(first, count, offset):
        column = lax.rem(sub + offset, cores) * depth
        block = lax.dynamic_slice(tokens, (first, column), (count, depth)).astype(F32)
        gain = lax.dynamic_slice(norm_gain, (column,), (depth,))
        return (block * gain[None, :]).astype(BF16)

    ring = [(i, (i + 1) % steps) for i in range(steps)]
    forward = lambda block: lax.ppermute(block, "ctx", ring)

    def all_parts(block):
        swaps = [[((c + o) % cores, c) for c in range(cores)] for o in range(1, cores)]
        return [block] + [lax.ppermute(block, "sub", swap) for swap in swaps]

    def partials(parts):
        received = []
        for w in range(1, across):
            block = project(parts, weight, sub, lax.rem(x + w, across), kept)
            received.append(lax.ppermute(block, "width", [(i, (i + w) % across) for i in range(across)]))
        return [project(parts, weight, sub, x, kept)] + received

    halves = [(mid, rows - mid), (0, mid)]
    last = [(mid, rows - mid), (small, mid - small), (0, small)]
    moving = [scaled_part(first, count, 0) for first, count in halves]
    table = {}
    for (first, count), block in zip(halves, moving):
        table[0, first] = partials([block] + [scaled_part(first, count, o) for o in range(1, cores)])
    gathered = lax.all_gather(power, ("ctx", "width"), axis=0).reshape(steps, across, rows).sum(axis=1)
    scales = lax.rsqrt(gathered / (features * across) + EPSILON)[:, :, None]

    for step in range(1, steps):
        if step < steps - 1:
            moving = [forward(block) for block in moving]
            spans = halves
        else:
            upper, lower = moving
            moving = [forward(upper), forward(lower[small:]), forward(lower[:small])]
            spans = last
        for (first, count), block in zip(spans, moving):
            table[step, first] = partials(all_parts(block))

    def taps_of(taps):
        offset = lambda v: lax.rem(z, group) * panel + v * kept
        cut = lambda v: lax.dynamic_slice_in_dim(taps, offset(v), kept, taps.ndim - 1)
        result = cut(x)
        for w in range(1, across):
            other = lax.ppermute(cut(lax.rem(x + w, across)), "width", [(i, (i + w) % across) for i in range(across)])
            result = jnp.where(lax.rem(owner + w, across) == x, other, result)
        return result

    short = taps_of(short_taps[:, :, 0, :])
    long = taps_of(long_taps[:, 0, :])
    forward_dft, inverse_dft = transforms()
    spectrum = jnp.dot(
        jnp.asarray(forward_dft[:, : long.shape[0]], F32), long, precision=lax.Precision.HIGHEST
    )
    upper, lower = spectrum[: FFT // 2], spectrum[FFT // 2 :]
    first_row = (jnp.arange(FFT // 2) == 0)[:, None]
    spectra = [upper, jnp.where(first_row, 0.0, lower), jnp.where(first_row, lower, upper)]
    matrices = [jnp.asarray(m) for pair in (split(forward_dft), split(inverse_dft)) for m in pair]

    def unit(step, plan, pieces, count):
        index = lax.rem(z - step + steps, steps)
        return filter_rows(plan, pieces, scales, index, jnp.where(index > 0, 1, 0), short, spectra, matrices, count)

    tail = rows - mid
    before = (tail - HALO, HALO, 1, rows - HALO, True)
    done = []
    for step in range(steps - 1):
        plan = (before, (0, mid, 0, 0, False), (0, tail, 0, mid, False))
        pieces = [table[step + 1, mid], table[step, 0], table[step, mid]]
        done.append(unit(step, plan, pieces, rows))
    step = steps - 1
    early = unit(
        step,
        ((late - HALO - small, mid - (late - HALO), 0, late - HALO, False), (0, tail, 0, mid, False)),
        [table[step, small], table[step, mid]],
        rows - late,
    )
    begin = unit(
        step,
        (before, (0, small, 0, 0, False), (0, late - small, 0, small, False)),
        [table[0, mid], table[step, 0], table[step, small]],
        late,
    )

    part = lax.rem(x - owner + across, across)

    def chosen(k, cut):
        options = [cut((k + group * w) % steps) for w in range(across)]
        result = options[0]
        for w in range(1, across):
            result = jnp.where(part == w, options[w], result)
        return result

    def returned(k, block):
        pairs = []
        for c in range(steps):
            for v in range(across):
                w = (v - c // group) % across
                target = (c - k - group * w) % steps
                pairs.append((c * across + v, target * across + c // group))
        return lax.ppermute(block, ("ctx", "width"), pairs)

    def place(output, k, block, first):
        source = group * x + lax.rem(z + k, group)
        w = lax.rem((source - z - k + 2 * steps) // group, across)
        column = lax.rem(source, group) * panel + lax.rem(x + w, across) * kept
        return lax.dynamic_update_slice(output, block, (first, column))

    output = jnp.zeros((rows, panel * group), BF16)
    rounds = [k for k in range(steps) if any((k + group * w) % steps == steps - 1 for w in range(across))]
    for k in range(steps):
        if k not in rounds:
            output = place(output, k, returned(k, chosen(k, lambda j: done[j])), 0)
    for k in rounds:
        block = chosen(k, lambda j: early if j == steps - 1 else done[j][late:])
        output = place(output, k, returned(k, block), late)
    for k in rounds:
        block = chosen(k, lambda j: begin if j == steps - 1 else done[j][:late])
        output = place(output, k, returned(k, block), 0)
    return output[:, None, :]


def solution(mesh):
    placed = (
        P(("parts", "ctx"), "width"),
        P("width"),
        P(None, "width", "sub", "ctx"),
        P(None, None, "sub", "width"),
        P(None, "sub", "width"),
    )
    return jax.shard_map(
        shards,
        mesh=mesh,
        in_specs=placed,
        out_specs=P(("parts", "ctx"), "sub", "width"),
        check_vma=False,
    )
```

time: 1000 us -> 270 us (0.27)
  waiting for transfers between devices: 908 us -> 45.6 us
  Pallas kernels: 0 us -> 84.2 us
  blocking collectives: 5.84 us -> 64 us
  matrix products: 56.3 us -> 0.36 us
  starting transfers between devices: 7.03 us -> 40.6 us
  local copies, waits for them, and re-layouts: 2.35 us -> 23.3 us
  between operations: 13.5 us -> 0.63 us
    all_gather x1 -> x0, waiting for transfers between devices: 831 us -> none  [shards(): lax.all_gather(in_weight, 'ctx', axis=3, tiled=True)[:, :, 0, :]]
    pallas_call x0 -> x23, Pallas kernels: none -> 84.2 us  [the longest x18 70.1 us: project(): pl.pallas_call(functools.partial(project_kernel, count), out_shape=jax.Sh...]
    reduce_scatter x1 -> x0, waiting for transfers between devices: 74 us -> none  [shards(): lax.psum_scatter(partial_sums.astype(jnp.bfloat16), 'width', scatter_dime...]
    all_gather x0 -> x1, blocking collectives: none -> 64 us  [shards(): lax.all_gather(power, ('ctx', 'width'), axis=0).reshape(steps, across, rows)]
    ppermute x2 -> x31, waiting for transfers between devices: 1.89 us -> 45.6 us  [the longest x7 32.9 us: shards(): forward = lambda block: lax.ppermute(block, 'ctx', ring)]
    ppermute x2 -> x31, starting transfers between devices: 6.99 us -> 40.6 us  [the longest x6 21.4 us: returned(): return lax.ppermute(block, ('ctx', 'width'), pairs)]
    dot_general x1, matrix products: 33.8 us -> 0.36 us  [shards(): jnp.dot(jnp.asarray(forward_dft[:, :long.shape[0]], F32), long, precision...]
    conv_general_dilated x1 -> x0, matrix products: 22.5 us -> none  [medium_filter(): lax.conv_general_dilated(inputs, kernel, (1,), 'VALID', dimension_numbers...]
  transfers between devices with their start and end apart: 4 -> 31, of which waited for: 3 -> 7; matrix products, arithmetic and copies ran while one was open for 1% -> 5% of each run, Pallas kernels for 0% -> 31%
where the time goes in v1:
time: 270 us; the launch traced here: 269 us
  Pallas kernels  84.2 us (31%)
  blocking collectives  64 us (24%)
  waiting for transfers between devices  45.6 us (17%)
  starting transfers between devices  40.6 us (15%)
  local copies, waits for them, and re-layouts  23.3 us (9%)
  other arithmetic  10 us (4%)
    pallas_call x18, Pallas kernels, project(): pl.pallas_call(functools.partial(project_kernel, count), out_shape=jax.Sh...  70.1 us
    all_gather x1, blocking collectives, shards(): lax.all_gather(power, ('ctx', 'width'), axis=0).reshape(steps, across, rows)  64 us
    ppermute x7, waiting for transfers between devices, shards(): forward = lambda block: lax.ppermute(block, 'ctx', ring)  32.9 us
    ppermute x6, starting transfers between devices, returned(): return lax.ppermute(block, ('ctx', 'width'), pairs)  21.4 us
    unnamed x40, local copies, waits for them, and re-layouts  16 us
    pallas_call x5, Pallas kernels, filter_rows(): pl.pallas_call(functools.partial(filter_kernel, plan, terms, rows), out_s...  14.1 us
    ppermute x9, starting transfers between devices, partials(): lax.ppermute(block, 'width', [(i, (i + w) % across) for i in range(across)])  10.8 us
    ppermute x9, waiting for transfers between devices, partials(): lax.ppermute(block, 'width', [(i, (i + w) % across) for i in range(across)])  10 us
  transfers between devices with their start and end apart: 31, of which 7 were waited for; matrix products, arithmetic and copies ran while one was open for 5% of the time, Pallas kernels for 31%

profile of v1, /device:TPU:0, one launch (start us, length us, event | category | flops | bytes accessed | tf_op | source)
XLA Modules:
  0.0 268.8 jit_solution(13272652535283839788)
XLA Ops:
  0.7 4.2 %multiply_convert_fusion = (bf16[256,2048]{1,0:T(8,128)(2,1)S(1)}, bf16[256,2048]{1,0:T(8,128)(2,1)S(1)}, bf16[256,2048]{1,0:T(8,128)(2,1)}, bf16[256,2048]{1,0:T(8,128)(2,1)S(1)}) fusion(bf16[512,4096]{1,0:T(8,128)(2,1)} %param.10, s32[]{:T(128)S(6)} %select_n.140, f32[2048]{0:T(1024)S(1)} %get-tuple-element.24, f32[2048]{0:T(1024)S(1)} %get-tuple-element.25, ...), kind=kLoop, calls=%fused_computation.1 | loop fusion | flops 6291456 | bytes 8405000 | tf_op jit(solution)/shard_map/convert_element_type | solution.py:196
  4.9 3.0 %collective-permute-start.5 = (bf16[256,2048]{1,0:T(8,128)(2,1)S(1)}, bf16[256,2048]{1,0:T(8,128)(2,1)}, u32[]{:S(2)}, u32[]{:S(2)}) collective-permute-start(bf16[256,2048]{1,0:T(8,128)(2,1)S(1)} %get-tuple-element.10.refs_1_), channel_id=1, source_target_pairs={{0,4},{4,8},{8,12},{12,0},{1,5},{5,9},{9,13},{13,1},{2,6},{6,10},{... | collective-permute-start | bytes 3145736 | tf_op jit(solution)/shard_map/ppermute | solution.py:199
  15.2 3.1 %multiply_reduce_fusion = f32[512]{0:T(512)S(1)} fusion(bf16[512,4096]{1,0:T(8,128)(2,1)} %param.10), kind=kLoop, calls=%fused_computation | loop fusion | flops 6290944 | bytes 4196352 | tf_op jit(solution)/shard_map/reduce_sum | solution.py:190
  18.3 15.7 %collective-permute-done.5.refs_1_ = bf16[256,2048]{1,0:T(8,128)(2,1)} collective-permute-done((bf16[256,2048]{1,0:T(8,128)(2,1)S(1)}, bf16[256,2048]{1,0:T(8,128)(2,1)}, u32[]{:S(2)}, u32[]{:S(2)}) %collective-permute-start.5) | collective-permute-done | bytes 1048608 | tf_op jit(solution)/shard_map/ppermute | solution.py:199
  34.1 64.0 %all-gather.1 = f32[8,1,512]{2,1,0:T(1,128)S(1)} all-gather(f32[1,1,512]{2,1,0:T(1,128)S(1)} %bitcast.81), channel_id=2, replica_groups=mesh['parts'=2,'ctx'=4,'width'=2,'sub'=2] {'ctx','width'}, dimensions={0}, use_global_device_ids=true | all-gather | bytes 18432 | tf_op jit(solution)/shard_map/all_gather | solution.py:218
  98.2 4.6 %copy-done = bf16[3,4096,1,512]{3,1,2,0:T(8,128)(2,1)S(1)} copy-done((bf16[3,4096,1,512]{3,1,2,0:T(8,128)(2,1)S(1)}, bf16[3,4096,1,512]{3,1,2,0:T(8,128)(2,1)}, u32[]{:S(2)}) %copy-start) | copy-done | bytes 12582936
  102.8 4.6 %project.28.refs_5_.refs_1_ = bf16[3,256,256]{2,1,0:T(8,128)(2,1)S(1)} custom-call(s32[2]{0:T(128)S(1)} %pad_add_fusion.1.refs_0_, bf16[256,2048]{1,0:T(8,128)(2,1)} %get-tuple-element.9.refs_1_, bf16[256,2048]{1,0:T(8,128)(2,1)S(1)} %get-tuple-element.5.refs_2_, bf16[3,4096,512]{2,1,0:T(8,128)(2,1)S(1)} %bitcast.43, bf16[3,4096,512]{2,1,0:T(8,128)(2,1)S(1)} %bitcast.44), custom_call_target="tpu_custom_call" | custom-call | flops 1610612736 | bytes 8781824 | tf_op jit(solution)/shard_map/project/pallas_call | solution.py:65
  108.3 4.9 %project.29 = bf16[3,256,256]{2,1,0:T(8,128)(2,1)} custom-call(s32[2]{0:T(128)S(1)} %pad_add_fusion.2.refs_0_, bf16[256,2048]{1,0:T(8,128)(2,1)} %get-tuple-element.9.refs_1_, bf16[256,2048]{1,0:T(8,128)(2,1)S(1)} %get-tuple-element.5.refs_2_, bf16[3,4096,512]{2,1,0:T(8,128)(2,1)S(1)} %bitcast.45, bf16[3,4096,512]{2,1,0:T(8,128)(2,1)S(1)} %bitcast.46), custom_call_target="tpu_custom_call" | custom-call | flops 1610612736 | bytes 8781824 | tf_op jit(solution)/shard_map/project/pallas_call | solution.py:65
  113.3 3.9 %project.27 = bf16[3,256,256]{2,1,0:T(8,128)(2,1)} custom-call(s32[2]{0:T(128)S(1)} %pad_add_fusion.2.refs_0_, bf16[256,2048]{1,0:T(8,128)(2,1)S(1)} %get-tuple-element.10.refs_1_, bf16[256,2048]{1,0:T(8,128)(2,1)S(1)} %get-tuple-element.6.refs_2_, bf16[3,4096,512]{2,1,0:T(8,128)(2,1)S(1)} %bitcast.47, bf16[3,4096,512]{2,1,0:T(8,128)(2,1)S(1)} %bitcast.48), custom_call_target="tpu_custom_call" | custom-call | flops 1610612736 | bytes 8781824 | tf_op jit(solution)/shard_map/project/pallas_call | solution.py:65
  122.3 4.6 %copy-done.2 = bf16[3,4096,1,512]{3,1,2,0:T(8,128)(2,1)S(1)} copy-done((bf16[3,4096,1,512]{3,1,2,0:T(8,128)(2,1)S(1)}, bf16[3,4096,1,512]{3,1,2,0:T(8,128)(2,1)}, u32[]{:S(2)}) %copy-start.2) | copy-done | bytes 12582936
  126.9 3.3 %project.26.refs_3_ = bf16[3,256,256]{2,1,0:T(8,128)(2,1)S(1)} custom-call(s32[2]{0:T(128)S(1)} %pad_add_fusion.1.refs_0_, bf16[256,2048]{1,0:T(8,128)(2,1)S(1)} %get-tuple-element.10.refs_1_, bf16[256,2048]{1,0:T(8,128)(2,1)S(1)} %get-tuple-element.6.refs_2_, bf16[3,4096,512]{2,1,0:T(8,128)(2,1)S(1)} %bitcast.49, bf16[3,4096,512]{2,1,0:T(8,128)(2,1)S(1)} %bitcast.50), custom_call_target="tpu_custom_call" | custom-call | flops 1610612736 | bytes 8781824 | tf_op jit(solution)/shard_map/project/pallas_call | solution.py:65
  132.8 5.8 %collective-permute-done.16.refs_6_.refs_2_ = bf16[3,256,256]{2,1,0:T(8,128)(2,1)} collective-permute-done((bf16[3,256,256]{2,1,0:T(8,128)(2,1)}, bf16[3,256,256]{2,1,0:T(8,128)(2,1)}, u32[]{:S(2)}, u32[]{:S(2)}) %collective-permute-start.16) | collective-permute-done | bytes 393248 | tf_op jit(solution)/shard_map/ppermute | solution.py:209
  139.5 4.6 %copy-done.3 = bf16[3,4096,1,512]{3,1,2,0:T(8,128)(2,1)S(1)} copy-done((bf16[3,4096,1,512]{3,1,2,0:T(8,128)(2,1)S(1)}, bf16[3,4096,1,512]{3,1,2,0:T(8,128)(2,1)}, u32[]{:S(2)}) %copy-start.3) | copy-done | bytes 12582936
  144.1 5.1 %project.25 = bf16[3,256,256]{2,1,0:T(8,128)(2,1)S(1)} custom-call(s32[2]{0:T(128)S(1)} %pad_add_fusion.2.refs_0_, bf16[256,2048]{1,0:T(8,128)(2,1)} %collective-permute-done.refs_1_, bf16[256,2048]{1,0:T(8,128)(2,1)} %collective-permute-done.13.refs_2_, bf16[3,4096,512]{2,1,0:T(8,128)(2,1)S(1)} %bitcast.51, bf16[3,4096,512]{2,1,0:T(8,128)(2,1)S(1)} %bitcast.52), custom_call_target="tpu_custom_call" | custom-call | flops 1610612736 | bytes 8781824 | tf_op jit(solution)/shard_map/project/pallas_call | solution.py:65
  151.6 4.6 %project.24.refs_1_.refs_5_ = bf16[3,256,256]{2,1,0:T(8,128)(2,1)S(1)} custom-call(s32[2]{0:T(128)S(1)} %pad_add_fusion.1.refs_0_, bf16[256,2048]{1,0:T(8,128)(2,1)} %collective-permute-done.refs_1_, bf16[256,2048]{1,0:T(8,128)(2,1)} %collective-permute-done.13.refs_2_, bf16[3,4096,512]{2,1,0:T(8,128)(2,1)S(1)} %bitcast.55, bf16[3,4096,512]{2,1,0:T(8,128)(2,1)S(1)} %bitcast.56), custom_call_target="tpu_custom_call" | custom-call | flops 1610612736 | bytes 8781824 | tf_op jit(solution)/shard_map/project/pallas_call | solution.py:65
  156.2 4.6 %project.33 = bf16[3,256,256]{2,1,0:T(8,128)(2,1)S(1)} custom-call(s32[2]{0:T(128)S(1)} %pad_add_fusion.2.refs_0_, bf16[256,2048]{1,0:T(8,128)(2,1)} %collective-permute-done.5.refs_1_, bf16[256,2048]{1,0:T(8,128)(2,1)} %collective-permute-done.22.refs_2_, bf16[3,4096,512]{2,1,0:T(8,128)(2,1)S(1)} %bitcast.57, bf16[3,4096,512]{2,1,0:T(8,128)(2,1)S(1)} %bitcast.58), custom_call_target="tpu_custom_call" | custom-call | flops 1610612736 | bytes 8781824 | tf_op jit(solution)/shard_map/project/pallas_call | solution.py:65
  162.3 4.6 %project.32.refs_3_ = bf16[3,256,256]{2,1,0:T(8,128)(2,1)S(1)} custom-call(s32[2]{0:T(128)S(1)} %pad_add_fusion.1.refs_0_, bf16[256,2048]{1,0:T(8,128)(2,1)} %collective-permute-done.5.refs_1_, bf16[256,2048]{1,0:T(8,128)(2,1)} %collective-permute-done.22.refs_2_, bf16[3,4096,512]{2,1,0:T(8,128)(2,1)S(1)} %bitcast.59, bf16[3,4096,512]{2,1,0:T(8,128)(2,1)S(1)} %bitcast.60), custom_call_target="tpu_custom_call" | custom-call | flops 1610612736 | bytes 8781824 | tf_op jit(solution)/shard_map/project/pallas_call | solution.py:65
  166.9 16.3 %collective-permute-done.2.refs_1_ = bf16[256,2048]{1,0:T(8,128)(2,1)S(1)} collective-permute-done((bf16[256,2048]{1,0:T(8,128)(2,1)}, bf16[256,2048]{1,0:T(8,128)(2,1)S(1)}, u32[]{:S(2)}, u32[]{:S(2)}) %collective-permute-start.2) | collective-permute-done | bytes 1048608 | tf_op jit(solution)/shard_map/ppermute | solution.py:199
  183.3 3.8 %filter.6 = bf16[512,256]{1,0:T(8,128)(2,1)S(1)} custom-call(s32[3]{0:T(128)S(1)} %copy-done.8, bf16[3,256,256]{2,1,0:T(8,128)(2,1)S(1)} %project.24.refs_1_.refs_5_, bf16[3,256,256]{2,1,0:T(8,128)(2,1)S(1)} %collective-permute-done.14.refs_2_.refs_6_, bf16[3,256,256]{2,1,0:T(8,128)(2,1)S(1)} %project.26.refs_3_, ...), custom_call_target="tpu_custom_call" | custom-call | flops 838860800 | bytes 2621440 | tf_op jit(solution)/shard_map/filter/pallas_call | solution.py:149
  194.2 4.3 %project.22.refs_5_.refs_1_ = bf16[3,256,256]{2,1,0:T(8,128)(2,1)S(1)} custom-call(s32[2]{0:T(128)S(1)} %pad_add_fusion.1.refs_0_, bf16[256,2048]{1,0:T(8,128)(2,1)} %collective-permute-done.1.refs_1_, bf16[256,2048]{1,0:T(8,128)(2,1)S(1)} %collective-permute-done.9.refs_2_, bf16[3,4096,512]{2,1,0:T(8,128)(2,1)S(1)} %bitcast.65, ...), custom_call_target="tpu_custom_call" | custom-call | flops 1610612736 | bytes 8781824 | tf_op jit(solution)/shard_map/project/pallas_call | solution.py:65
  198.4 4.3 %project.23 = bf16[3,256,256]{2,1,0:T(8,128)(2,1)S(1)} custom-call(s32[2]{0:T(128)S(1)} %pad_add_fusion.2.refs_0_, bf16[256,2048]{1,0:T(8,128)(2,1)} %collective-permute-done.1.refs_1_, bf16[256,2048]{1,0:T(8,128)(2,1)S(1)} %collective-permute-done.9.refs_2_, bf16[3,4096,512]{2,1,0:T(8,128)(2,1)S(1)} %bitcast.67, bf16[3,4096,512]{2,1,0:T(8,128)(2,1)S(1)} %bitcast.68), custom_call_target="tpu_custom_call" | custom-call | flops 1610612736 | bytes 8781824 | tf_op jit(solution)/shard_map/project/pallas_call | solution.py:65
  203.4 4.3 %project.21 = bf16[3,256,256]{2,1,0:T(8,128)(2,1)S(1)} custom-call(s32[2]{0:T(128)S(1)} %pad_add_fusion.2.refs_0_, bf16[256,2048]{1,0:T(8,128)(2,1)} %collective-permute-done.6.refs_1_, bf16[256,2048]{1,0:T(8,128)(2,1)S(1)} %collective-permute-done.7.refs_2_, bf16[3,4096,512]{2,1,0:T(8,128)(2,1)S(1)} %bitcast.69, bf16[3,4096,512]{2,1,0:T(8,128)(2,1)S(1)} %bitcast.70), custom_call_target="tpu_custom_call" | custom-call | flops 1610612736 | bytes 8781824 | tf_op jit(solution)/shard_map/project/pallas_call | solution.py:65
  207.7 4.3 %project.20.refs_3_ = bf16[3,256,256]{2,1,0:T(8,128)(2,1)S(1)} custom-call(s32[2]{0:T(128)S(1)} %pad_add_fusion.1.refs_0_, bf16[256,2048]{1,0:T(8,128)(2,1)} %collective-permute-done.6.refs_1_, bf16[256,2048]{1,0:T(8,128)(2,1)S(1)} %collective-permute-done.7.refs_2_, bf16[3,4096,512]{2,1,0:T(8,128)(2,1)S(1)} %bitcast.71, bf16[3,4096,512]{2,1,0:T(8,128)(2,1)S(1)} %bitcast.72), custom_call_target="tpu_custom_call" | custom-call | flops 1610612736 | bytes 8781824 | tf_op jit(solution)/shard_map/project/pallas_call | solution.py:65
  213.5 2.9 %project.31 = bf16[3,208,256]{2,1,0:T(8,128)(2,1)S(1)} custom-call(s32[2]{0:T(128)S(1)} %pad_add_fusion.2.refs_0_, bf16[208,2048]{1,0:T(8,128)(2,1)S(1)} %collective-permute-done.19.refs_1_, bf16[208,2048]{1,0:T(8,128)(2,1)S(1)} %collective-permute-done.20.refs_2_, bf16[3,4096,512]{2,1,0:T(8,128)(2,1)S(1)} %bitcast.73, bf16[3,4096,512]{2,1,0:T(8,128)(2,1)S(1)} %bitcast.74), custom_call_target="tpu_custom_call" | custom-call | flops 1308622848 | bytes 8314880 | tf_op jit(solution)/shard_map/project/pallas_call | solution.py:65
  217.1 2.6 filter.8
  219.8 2.9 %project.30.refs_1_.refs_5_ = bf16[3,208,256]{2,1,0:T(8,128)(2,1)S(1)} custom-call(s32[2]{0:T(128)S(1)} %pad_add_fusion.1.refs_0_, bf16[208,2048]{1,0:T(8,128)(2,1)S(1)} %collective-permute-done.19.refs_1_, bf16[208,2048]{1,0:T(8,128)(2,1)S(1)} %collective-permute-done.20.refs_2_, bf16[3,4096,512]{2,1,0:T(8,128)(2,1)S(1)} %bitcast.75, ...), custom_call_target="tpu_custom_call" | custom-call | flops 1308622848 | bytes 8314880 | tf_op jit(solution)/shard_map/project/pallas_call | solution.py:65
  222.7 3.4 %project.19 = bf16[3,256,256]{2,1,0:T(8,128)(2,1)S(1)} custom-call(s32[2]{0:T(128)S(1)} %pad_add_fusion.2.refs_0_, bf16[256,2048]{1,0:T(8,128)(2,1)S(1)} %collective-permute-done.2.refs_1_, bf16[256,2048]{1,0:T(8,128)(2,1)S(1)} %collective-permute-done.3.refs_2_, bf16[3,4096,512]{2,1,0:T(8,128)(2,1)S(1)} %bitcast.77, bf16[3,4096,512]{2,1,0:T(8,128)(2,1)S(1)} %bitcast.78), custom_call_target="tpu_custom_call" | custom-call | flops 1610612736 | bytes 8781824 | tf_op jit(solution)/shard_map/project/pallas_call | solution.py:65
  227.6 3.3 %collective-permute-done.21.refs_2_.refs_6_ = bf16[3,208,256]{2,1,0:T(8,128)(2,1)S(1)} collective-permute-done((bf16[3,208,256]{2,1,0:T(8,128)(2,1)S(1)}, bf16[3,208,256]{2,1,0:T(8,128)(2,1)S(1)}, u32[]{:S(2)}, u32[]{:S(2)}) %collective-permute-start.21) | collective-permute-done | bytes 319520 | tf_op jit(solution)/shard_map/ppermute | solution.py:209
  230.9 2.8 %filter.9 = bf16[192,256]{1,0:T(8,128)(2,1)S(1)} custom-call(s32[3]{0:T(128)S(1)} %get-tuple-element.28.refs_0_, bf16[3,256,256]{2,1,0:T(8,128)(2,1)S(1)} %project.28.refs_5_.refs_1_, bf16[3,256,256]{2,1,0:T(8,128)(2,1)} %collective-permute-done.16.refs_6_.refs_2_, bf16[3,48,256]{2,1,0:T(8,128)(2,1)S(1)} %project.34.refs_3_, ...), custom_call_target="tpu_custom_call" | custom-call | flops 335544320 | bytes 1671168 | tf_op jit(solution)/shard_map/filter/pallas_call | solution.py:149
  236.1 3.2 %project.18.refs_1_.refs_3_ = bf16[3,256,256]{2,1,0:T(8,128)(2,1)S(1)} custom-call(s32[2]{0:T(128)S(1)} %pad_add_fusion.1.refs_0_, bf16[256,2048]{1,0:T(8,128)(2,1)S(1)} %collective-permute-done.2.refs_1_, bf16[256,2048]{1,0:T(8,128)(2,1)S(1)} %collective-permute-done.3.refs_2_, bf16[3,4096,512]{2,1,0:T(8,128)(2,1)S(1)} %bitcast.79, ...), custom_call_target="tpu_custom_call" | custom-call | flops 1610612736 | bytes 8781824 | tf_op jit(solution)/shard_map/project/pallas_call | solution.py:65
  240.1 2.6 filter.5
  249.8 14.4 %collective-permute-start.24 = (bf16[320,256]{1,0:T(8,128)(2,1)S(1)}, bf16[320,256]{1,0:T(8,128)(2,1)S(1)}, u32[]{:S(2)}, u32[]{:S(2)}) collective-permute-start(bf16[320,256]{1,0:T(8,128)(2,1)S(1)} %get-tuple-element.16), channel_id=1, source_target_pairs={{0,12},{2,4},{4,0},{6,8},{8,14},{10,6},{12,2},{14,10},{1,13},{3,5}... | collective-permute-start | bytes 491528 | tf_op jit(solution)/shard_map/ppermute | solution.py:293
  (125 shorter events, 47.5 us)
Async XLA Ops:
  4.9 29.1 %collective-permute-start.5 = (bf16[256,2048]{1,0:T(8,128)(2,1)S(1)}, bf16[256,2048]{1,0:T(8,128)(2,1)}, u32[]{:S(2)}, u32[]{:S(2)}) collective-permute-start(bf16[256,2048]{1,0:T(8,128)(2,1)S(1)} %get-tuple-element.10.refs_1_), channel_id=1, source_target_pairs={{0,4},{4,8},{8,12},{12,0},{1,5},{5,9},{9,13},{13,1},{2,6},{6,10},{... | collective-permute-start | bytes 3145736 | tf_op jit(solution)/shard_map/ppermute | solution.py:199
  7.9 100.1 %collective-permute-start = (bf16[256,2048]{1,0:T(8,128)(2,1)}, bf16[256,2048]{1,0:T(8,128)(2,1)}, u32[]{:S(2)}, u32[]{:S(2)}) collective-permute-start(bf16[256,2048]{1,0:T(8,128)(2,1)} %get-tuple-element.9.refs_1_), channel_id=1, source_target_pairs={{0,4},{4,8},{8,12},{12,0},{1,5},{5,9},{9,13},{13,1},{2,6},{6,10},{... | collective-permute-start | bytes 3145736 | tf_op jit(solution)/shard_map/ppermute | solution.py:199
  10.7 106.5 %collective-permute-start.11 = (f32[3,3,256]{2,1,0:T(4,128)}, f32[3,3,256]{2,1,0:T(4,128)}, u32[]{:S(2)}, u32[]{:S(2)}) collective-permute-start(f32[3,3,256]{2,1,0:T(4,128)} %bitcast.42), channel_id=1, source_target_pairs={{0,2},{2,0},{1,3},{3,1},{4,6},{6,4},{5,7},{7,5},{8,10},{10,8},{9,1... | collective-permute-start | bytes 27656 | tf_op jit(solution)/shard_map/ppermute | solution.py:237
  14.7 104.0 %collective-permute-start.12 = (f32[128,256]{1,0:T(8,128)}, f32[128,256]{1,0:T(8,128)}, u32[]{:S(2)}, u32[]{:S(2)}) collective-permute-start(f32[128,256]{1,0:T(8,128)} %bitcast.41), channel_id=1, source_target_pairs={{0,2},{2,0},{1,3},{3,1},{4,6},{6,4},{5,7},{7,5},{8,10},{10,8},{9,1... | collective-permute-start | bytes 393224 | tf_op jit(solution)/shard_map/ppermute | solution.py:237
  34.0 84.6 %collective-permute-start.6 = (bf16[256,2048]{1,0:T(8,128)(2,1)}, bf16[256,2048]{1,0:T(8,128)(2,1)}, u32[]{:S(2)}, u32[]{:S(2)}) collective-permute-start(bf16[256,2048]{1,0:T(8,128)(2,1)} %collective-permute-done.5.refs_1_), channel_id=1, source_target_pairs={{0,4},{4,8},{8,12},{12,0},{1,5},{5,9},{9,13},{13,1},{2,6},{6,10},{... | collective-permute-start | bytes 3145736 | tf_op jit(solution)/shard_map/ppermute | solution.py:199
  108.0 30.9 %collective-permute-start.13 = (bf16[256,2048]{1,0:T(8,128)(2,1)}, bf16[256,2048]{1,0:T(8,128)(2,1)}, u32[]{:S(2)}, u32[]{:S(2)}) collective-permute-start(bf16[256,2048]{1,0:T(8,128)(2,1)} %collective-permute-done.refs_1_), channel_id=1, source_target_pairs={{1,0},{0,1},{3,2},{2,3},{5,4},{4,5},{7,6},{6,7},{9,8},{8,9},{11,10... | collective-permute-start | bytes 3145736 | tf_op jit(solution)/shard_map/ppermute | solution.py:203
  108.0 30.9 %collective-permute-start.1 = (bf16[256,2048]{1,0:T(8,128)(2,1)}, bf16[256,2048]{1,0:T(8,128)(2,1)}, u32[]{:S(2)}, u32[]{:S(2)}) collective-permute-start(bf16[256,2048]{1,0:T(8,128)(2,1)} %collective-permute-done.refs_1_), channel_id=1, source_target_pairs={{0,4},{4,8},{8,12},{12,0},{1,5},{5,9},{9,13},{13,1},{2,6},{6,10},{... | collective-permute-start | bytes 3145736 | tf_op jit(solution)/shard_map/ppermute | solution.py:199
  117.2 32.0 %collective-permute-start.22 = (bf16[256,2048]{1,0:T(8,128)(2,1)}, bf16[256,2048]{1,0:T(8,128)(2,1)}, u32[]{:S(2)}, u32[]{:S(2)}) collective-permute-start(bf16[256,2048]{1,0:T(8,128)(2,1)} %collective-permute-done.5.refs_1_), channel_id=1, source_target_pairs={{1,0},{0,1},{3,2},{2,3},{5,4},{4,5},{7,6},{6,7},{9,8},{8,9},{11,10... | collective-permute-start | bytes 3145736 | tf_op jit(solution)/shard_map/ppermute | solution.py:203
  118.6 13.9 %collective-permute-start.15 = (bf16[3,256,256]{2,1,0:T(8,128)(2,1)}, bf16[3,256,256]{2,1,0:T(8,128)(2,1)}, u32[]{:S(2)}, u32[]{:S(2)}) collective-permute-start(bf16[3,256,256]{2,1,0:T(8,128)(2,1)} %project.27), channel_id=1, source_target_pairs={{0,2},{2,0},{1,3},{3,1},{4,6},{6,4},{5,7},{7,5},{8,10},{10,8},{9,1... | collective-permute-start | bytes 1179656 | tf_op jit(solution)/shard_map/ppermute | solution.py:209
  118.6 20.0 %collective-permute-start.16 = (bf16[3,256,256]{2,1,0:T(8,128)(2,1)}, bf16[3,256,256]{2,1,0:T(8,128)(2,1)}, u32[]{:S(2)}, u32[]{:S(2)}) collective-permute-start(bf16[3,256,256]{2,1,0:T(8,128)(2,1)} %project.29), channel_id=1, source_target_pairs={{0,2},{2,0},{1,3},{3,1},{4,6},{6,4},{5,7},{7,5},{8,10},{10,8},{9,1... | collective-permute-start | bytes 1179656 | tf_op jit(solution)/shard_map/ppermute | solution.py:209
  126.9 24.7 %slice-start.1 = ((s8[12582912]{0:T(1024)(128)(4,1)}), s8[4194304]{0:T(1024)(128)(4,1)S(1)}, s32[]{:S(2)}) async-start(s8[12582912]{0:T(1024)(128)(4,1)} %bitcast.53), calls=%async_computation.1 | async-start | bytes 8388608
  132.5 19.0 %collective-permute-start.26 = (bf16[48,2048]{1,0:T(8,128)(2,1)S(1)}, bf16[48,2048]{1,0:T(8,128)(2,1)S(1)}, u32[]{:S(2)}, u32[]{:S(2)}) collective-permute-start(bf16[48,2048]{1,0:T(8,128)(2,1)S(1)} %slice.30), channel_id=1, source_target_pairs={{0,4},{4,8},{8,12},{12,0},{1,5},{5,9},{9,13},{13,1},{2,6},{6,10},{... | collective-permute-start | bytes 589832 | tf_op jit(solution)/shard_map/ppermute | solution.py:199
  138.6 23.7 %collective-permute-start.19 = (bf16[208,2048]{1,0:T(8,128)(2,1)S(1)}, bf16[208,2048]{1,0:T(8,128)(2,1)S(1)}, u32[]{:S(2)}, u32[]{:S(2)}) collective-permute-start(bf16[208,2048]{1,0:T(8,128)(2,1)S(1)} %slice.28), channel_id=1, source_target_pairs={{0,4},{4,8},{8,12},{12,0},{1,5},{5,9},{9,13},{13,1},{2,6},{6,10},{... | collective-permute-start | bytes 2555912 | tf_op jit(solution)/shard_map/ppermute | solution.py:199
  138.9 53.8 %collective-permute-start.9 = (bf16[256,2048]{1,0:T(8,128)(2,1)}, bf16[256,2048]{1,0:T(8,128)(2,1)S(1)}, u32[]{:S(2)}, u32[]{:S(2)}) collective-permute-start(bf16[256,2048]{1,0:T(8,128)(2,1)} %collective-permute-done.1.refs_1_), channel_id=1, source_target_pairs={{1,0},{0,1},{3,2},{2,3},{5,4},{4,5},{7,6},{6,7},{9,8},{8,9},{11,10... | collective-permute-start | bytes 3145736 | tf_op jit(solution)/shard_map/ppermute | solution.py:203
  138.9 44.4 %collective-permute-start.2 = (bf16[256,2048]{1,0:T(8,128)(2,1)}, bf16[256,2048]{1,0:T(8,128)(2,1)S(1)}, u32[]{:S(2)}, u32[]{:S(2)}) collective-permute-start(bf16[256,2048]{1,0:T(8,128)(2,1)} %collective-permute-done.1.refs_1_), channel_id=1, source_target_pairs={{0,4},{4,8},{8,12},{12,0},{1,5},{5,9},{9,13},{13,1},{2,6},{6,10},{... | collective-permute-start | bytes 3145736 | tf_op jit(solution)/shard_map/ppermute | solution.py:199
  149.2 11.7 %collective-permute-start.14 = (bf16[3,256,256]{2,1,0:T(8,128)(2,1)S(1)}, bf16[3,256,256]{2,1,0:T(8,128)(2,1)S(1)}, u32[]{:S(2)}, u32[]{:S(2)}) collective-permute-start(bf16[3,256,256]{2,1,0:T(8,128)(2,1)S(1)} %project.25), channel_id=1, source_target_pairs={{0,2},{2,0},{1,3},{3,1},{4,6},{6,4},{5,7},{7,5},{8,10},{10,8},{9,1... | collective-permute-start | bytes 1179656 | tf_op jit(solution)/shard_map/ppermute | solution.py:209
  151.5 51.2 %collective-permute-start.7 = (bf16[256,2048]{1,0:T(8,128)(2,1)}, bf16[256,2048]{1,0:T(8,128)(2,1)S(1)}, u32[]{:S(2)}, u32[]{:S(2)}) collective-permute-start(bf16[256,2048]{1,0:T(8,128)(2,1)} %collective-permute-done.6.refs_1_), channel_id=1, source_target_pairs={{1,0},{0,1},{3,2},{2,3},{5,4},{4,5},{7,6},{6,7},{9,8},{8,9},{11,10... | collective-permute-start | bytes 3145736 | tf_op jit(solution)/shard_map/ppermute | solution.py:203
  160.9 26.1 %collective-permute-start.27 = (bf16[48,2048]{1,0:T(8,128)(2,1)S(1)}, bf16[48,2048]{1,0:T(8,128)(2,1)S(1)}, u32[]{:S(2)}, u32[]{:S(2)}) collective-permute-start(bf16[48,2048]{1,0:T(8,128)(2,1)S(1)} %collective-permute-done.26.refs_1_), channel_id=1, source_target_pairs={{1,0},{0,1},{3,2},{2,3},{5,4},{4,5},{7,6},{6,7},{9,8},{8,9},{11,10... | collective-permute-start | bytes 589832 | tf_op jit(solution)/shard_map/ppermute | solution.py:203
  162.3 49.7 %collective-permute-start.20 = (bf16[208,2048]{1,0:T(8,128)(2,1)S(1)}, bf16[208,2048]{1,0:T(8,128)(2,1)S(1)}, u32[]{:S(2)}, u32[]{:S(2)}) collective-permute-start(bf16[208,2048]{1,0:T(8,128)(2,1)S(1)} %collective-permute-done.19.refs_1_), channel_id=1, source_target_pairs={{1,0},{0,1},{3,2},{2,3},{5,4},{4,5},{7,6},{6,7},{9,8},{8,9},{11,10... | collective-permute-start | bytes 2555912 | tf_op jit(solution)/shard_map/ppermute | solution.py:203
  183.3 39.4 %collective-permute-start.3 = (bf16[256,2048]{1,0:T(8,128)(2,1)S(1)}, bf16[256,2048]{1,0:T(8,128)(2,1)S(1)}, u32[]{:S(2)}, u32[]{:S(2)}) collective-permute-start(bf16[256,2048]{1,0:T(8,128)(2,1)S(1)} %collective-permute-done.2.refs_1_), channel_id=1, source_target_pairs={{1,0},{0,1},{3,2},{2,3},{5,4},{4,5},{7,6},{6,7},{9,8},{8,9},{11,10... | collective-permute-start | bytes 3145736 | tf_op jit(solution)/shard_map/ppermute | solution.py:203
  187.1 29.3 %collective-permute-start.23 = (bf16[3,256,256]{2,1,0:T(8,128)(2,1)S(1)}, bf16[3,256,256]{2,1,0:T(8,128)(2,1)S(1)}, u32[]{:S(2)}, u32[]{:S(2)}) collective-permute-start(bf16[3,256,256]{2,1,0:T(8,128)(2,1)S(1)} %project.33), channel_id=1, source_target_pairs={{0,2},{2,0},{1,3},{3,1},{4,6},{6,4},{5,7},{7,5},{8,10},{10,8},{9,1... | collective-permute-start | bytes 1179656 | tf_op jit(solution)/shard_map/ppermute | solution.py:209
  192.7 34.9 %collective-permute-start.28 = (bf16[3,48,256]{2,1,0:T(8,128)(2,1)S(1)}, bf16[3,48,256]{2,1,0:T(8,128)(2,1)S(1)}, u32[]{:S(2)}, u32[]{:S(2)}) collective-permute-start(bf16[3,48,256]{2,1,0:T(8,128)(2,1)S(1)} %project.35), channel_id=1, source_target_pairs={{0,2},{2,0},{1,3},{3,1},{4,6},{6,4},{5,7},{7,5},{8,10},{10,8},{9,1... | collective-permute-start | bytes 221192 | tf_op jit(solution)/shard_map/ppermute | solution.py:209
  202.7 14.4 %collective-permute-start.10 = (bf16[3,256,256]{2,1,0:T(8,128)(2,1)S(1)}, bf16[3,256,256]{2,1,0:T(8,128)(2,1)S(1)}, u32[]{:S(2)}, u32[]{:S(2)}) collective-permute-start(bf16[3,256,256]{2,1,0:T(8,128)(2,1)S(1)} %project.23), channel_id=1, source_target_pairs={{0,2},{2,0},{1,3},{3,1},{4,6},{6,4},{5,7},{7,5},{8,10},{10,8},{9,1... | collective-permute-start | bytes 1179656 | tf_op jit(solution)/shard_map/ppermute | solution.py:209
  212.0 27.3 %collective-permute-start.8 = (bf16[3,256,256]{2,1,0:T(8,128)(2,1)S(1)}, bf16[3,256,256]{2,1,0:T(8,128)(2,1)S(1)}, u32[]{:S(2)}, u32[]{:S(2)}) collective-permute-start(bf16[3,256,256]{2,1,0:T(8,128)(2,1)S(1)} %project.21), channel_id=1, source_target_pairs={{0,2},{2,0},{1,3},{3,1},{4,6},{6,4},{5,7},{7,5},{8,10},{10,8},{9,1... | collective-permute-start | bytes 1179656 | tf_op jit(solution)/shard_map/ppermute | solution.py:209
  216.4 14.5 %collective-permute-start.21 = (bf16[3,208,256]{2,1,0:T(8,128)(2,1)S(1)}, bf16[3,208,256]{2,1,0:T(8,128)(2,1)S(1)}, u32[]{:S(2)}, u32[]{:S(2)}) collective-permute-start(bf16[3,208,256]{2,1,0:T(8,128)(2,1)S(1)} %project.31), channel_id=1, source_target_pairs={{0,2},{2,0},{1,3},{3,1},{4,6},{6,4},{5,7},{7,5},{8,10},{10,8},{9,1... | collective-permute-start | bytes 958472 | tf_op jit(solution)/shard_map/ppermute | solution.py:209
  226.1 14.0 %collective-permute-start.4 = (bf16[3,256,256]{2,1,0:T(8,128)(2,1)S(1)}, bf16[3,256,256]{2,1,0:T(8,128)(2,1)S(1)}, u32[]{:S(2)}, u32[]{:S(2)}) collective-permute-start(bf16[3,256,256]{2,1,0:T(8,128)(2,1)S(1)} %project.19), channel_id=1, source_target_pairs={{0,2},{2,0},{1,3},{3,1},{4,6},{6,4},{5,7},{7,5},{8,10},{10,8},{9,1... | collective-permute-start | bytes 1179656 | tf_op jit(solution)/shard_map/ppermute | solution.py:209
  233.8 33.4 %collective-permute-start.30 = (bf16[192,256]{1,0:T(8,128)(2,1)S(1)}, bf16[192,256]{1,0:T(8,128)(2,1)S(1)}, u32[]{:S(2)}, u32[]{:S(2)}) collective-permute-start(bf16[192,256]{1,0:T(8,128)(2,1)S(1)} %get-tuple-element.17), channel_id=1, source_target_pairs={{0,4},{2,12},{4,8},{6,0},{8,6},{10,14},{12,10},{14,2},{1,5},{3,13}... | collective-permute-start | bytes 294920 | tf_op jit(solution)/shard_map/ppermute | solution.py:293
  233.8 33.3 %collective-permute-start.29 = (bf16[192,256]{1,0:T(8,128)(2,1)S(1)}, bf16[192,256]{1,0:T(8,128)(2,1)S(1)}, u32[]{:S(2)}, u32[]{:S(2)}) collective-permute-start(bf16[192,256]{1,0:T(8,128)(2,1)S(1)} %get-tuple-element.18), channel_id=1, source_target_pairs={{0,12},{2,4},{4,0},{6,8},{8,14},{10,6},{12,2},{14,10},{1,13},{3,5}... | collective-permute-start | bytes 294920 | tf_op jit(solution)/shard_map/ppermute | solution.py:293
  242.8 21.6 %collective-permute-start.18 = (bf16[512,256]{1,0:T(8,128)(2,1)S(1)}, bf16[512,256]{1,0:T(8,128)(2,1)S(1)}, u32[]{:S(2)}, u32[]{:S(2)}) collective-permute-start(bf16[512,256]{1,0:T(8,128)(2,1)S(1)} %get-tuple-element.11), channel_id=1, source_target_pairs={{0,8},{2,0},{4,12},{6,4},{8,10},{10,2},{12,14},{14,6},{1,9},{3,1},... | collective-permute-start | bytes 786440 | tf_op jit(solution)/shard_map/ppermute | solution.py:293
  245.1 4.8 %collective-permute-start.17 = (bf16[512,256]{1,0:T(8,128)(2,1)S(1)}, bf16[512,256]{1,0:T(8,128)(2,1)S(1)}, u32[]{:S(2)}, u32[]{:S(2)}) collective-permute-start(bf16[512,256]{1,0:T(8,128)(2,1)S(1)} %get-tuple-element.12), channel_id=1, source_target_pairs={{0,0},{2,8},{4,4},{6,12},{8,2},{10,10},{12,6},{14,14},{1,1},{3,9},... | collective-permute-start | bytes 786440 | tf_op jit(solution)/shard_map/ppermute | solution.py:293
  248.0 19.1 %collective-permute-start.25 = (bf16[320,256]{1,0:T(8,128)(2,1)S(1)}, bf16[320,256]{1,0:T(8,128)(2,1)S(1)}, u32[]{:S(2)}, u32[]{:S(2)}) collective-permute-start(bf16[320,256]{1,0:T(8,128)(2,1)S(1)} %get-tuple-element.15), channel_id=1, source_target_pairs={{0,4},{2,12},{4,8},{6,0},{8,6},{10,14},{12,10},{14,2},{1,5},{3,13}... | collective-permute-start | bytes 491528 | tf_op jit(solution)/shard_map/ppermute | solution.py:293
  249.8 17.2 %collective-permute-start.24 = (bf16[320,256]{1,0:T(8,128)(2,1)S(1)}, bf16[320,256]{1,0:T(8,128)(2,1)S(1)}, u32[]{:S(2)}, u32[]{:S(2)}) collective-permute-start(bf16[320,256]{1,0:T(8,128)(2,1)S(1)} %get-tuple-element.16), channel_id=1, source_target_pairs={{0,12},{2,4},{4,0},{6,8},{8,14},{10,6},{12,2},{14,10},{1,13},{3,5}... | collective-permute-start | bytes 491528 | tf_op jit(solution)/shard_map/ppermute | solution.py:293
  (18 other events, 206.9 us)

commit v2 on v1

v2 whole, which is shorter than its diff:
```python
import functools

import jax
import jax.numpy as jnp
import numpy as np
from jax import lax
from jax.experimental import pallas as pl
from jax.experimental.pallas import tpu as pltpu
from jax.sharding import PartitionSpec as P

EPSILON = 1e-05
HALO = 144
FFT = 256
STEP = 128
EXTRA = 8
BF16 = jnp.bfloat16
F32 = jnp.float32


def repeat(count, unrolled, body):
    if unrolled:
        for i in range(count):
            body(i)
    else:
        pl.loop(0, count)(body)


def at_multiple(value, multiple):
    return value if isinstance(value, int) else pl.multiple_of(value, multiple)


def split(matrix):
    high = np.asarray(matrix, np.float32).astype(jnp.bfloat16)
    low = (np.asarray(matrix, np.float32) - high.astype(np.float32)).astype(jnp.bfloat16)
    return high, low


def transforms():
    half = FFT // 2
    n = np.arange(FFT)
    k = np.arange(half)
    angle = 2.0 * np.pi * np.outer(k, n) / FFT
    real, imag = np.cos(angle), -np.sin(angle)
    imag[0] = np.cos(np.pi * n)
    forward = np.concatenate([real, imag], axis=0)
    weight = np.full((half,), 2.0)
    weight[0] = 1.0
    back_real = (weight[:, None] * np.cos(angle)).T / FFT
    back_imag = (-2.0 * np.sin(angle)).T / FFT
    back_imag[:, 0] = np.cos(np.pi * n) / FFT
    inverse = np.concatenate([back_real, back_imag], axis=1)[FFT - STEP :]
    return forward, inverse


def project(parts, rows, weight, places, column, kept):
    depth = parts[0].shape[1]
    streams = weight.shape[0]
    count = len(parts)

    narrow = weight.shape[2] == kept

    def body(places, *refs):
        blocks, weight, out = refs[:count], refs[count], refs[count + 1]
        columns = slice(None) if narrow else pl.ds(pl.multiple_of(places[column] * kept, kept), kept)

        def one(stream):
            total = None
            for offset, block in enumerate(blocks):
                row = pl.multiple_of(lax.rem(places[0] + offset, count) * depth, depth)
                term = jnp.dot(
                    block[:rows, :], weight[stream, pl.ds(row, depth), columns], preferred_element_type=F32
                )
                total = term if total is None else total + term
            out[stream] = total.astype(BF16)

        repeat(streams, rows < 256, one)

    whole = pl.BlockSpec(memory_space=pltpu.VMEM)
    return pl.pallas_call(
        body,
        out_shape=jax.ShapeDtypeStruct((streams, rows, kept), BF16),
        in_specs=[pl.BlockSpec(memory_space=pltpu.SMEM)] + [whole] * (count + 1),
        out_specs=whole,
        compiler_params=pltpu.CompilerParams(vmem_limit_bytes=12 << 20),
        cost_estimate=pl.CostEstimate(flops=1 << 20, bytes_accessed=1 << 16, transcendentals=0),
        name="project",
    )(places, *parts, pltpu.with_memory_space_constraint(weight, pltpu.VMEM))


def filter_kernel(plan, terms, rows, flag, places, *refs):
    pieces = []
    for _ in plan:
        pieces.append(refs[:terms])
        refs = refs[terms:]
    near, far, short, spec_a, spec_b, spec_c, fh, fl, gh, gl, out, held, query, gated, spread = refs
    tile = 64
    kept = out.shape[1]
    extent = spread.shape[1]
    for which, scale in enumerate((near, far)):
        row = scale[0:1, :extent].astype(F32) + scale[1:2, :extent].astype(F32) + scale[2:3, :extent].astype(F32)
        for low in range(0, extent, 128):
            spread[which, low : low + 128, :] = jnp.broadcast_to(row[:, low : low + 128], (128, 128)).T
    at = 0
    for (first, count, scale, scale_first, masked), sources in zip(plan, pieces):
        for low in range(0, count, tile):
            size = min(tile, count - low)
            factor = spread[scale, scale_first + low : scale_first + low + size, :]
            if masked:
                factor = factor * places[flag].astype(F32)
            factor = jnp.concatenate([factor] * (kept // 128), axis=1) if kept % 128 == 0 else factor[:, :kept]
            for stream in range(3):
                total = sources[0][stream, first + low : first + low + size, :].astype(F32)
                for source in sources[1:]:
                    total = total + source[stream, first + low : first + low + size, :].astype(F32)
                value = (total * factor).astype(BF16).astype(F32)
                held[stream, at + low : at + low + size, :] = value
        at += count

    def short_filter(stream, row):
        window = held[stream, pl.ds(at_multiple(row - 8, 8), tile + 8), :]
        return sum(short[j, stream][None, :] * window[8 - j : 8 - j + tile] for j in range(3))

    lead = HALO - STEP

    def gate(i):
        low = at_multiple(i * tile, tile)
        value = short_filter(1, lead + low) * short_filter(2, lead + low)
        gated[pl.ds(low, tile), :] = value.astype(BF16)

    def ask(i):
        low = at_multiple(i * tile, tile)
        query[pl.ds(low, tile), :] = short_filter(0, HALO + low)

    half = FFT // 2

    def convolve(i):
        start = min(i * STEP, rows - STEP) if isinstance(i, int) else jnp.minimum(i * STEP, rows - STEP)
        start = at_multiple(start, tile)
        window = gated[pl.ds(start, FFT), :]
        spectrum = jnp.dot(fh[...], window, preferred_element_type=F32)
        spectrum = spectrum + jnp.dot(fl[...], window, preferred_element_type=F32)
        upper, lower = spectrum[:half], spectrum[half:]
        product = jnp.concatenate(
            [upper * spec_a[...] - lower * spec_b[...], upper * spec_b[...] + lower * spec_c[...]], axis=0
        )
        high = product.astype(BF16)
        rest = (product - high.astype(F32)).astype(BF16)
        result = jnp.dot(gh[...], high, preferred_element_type=F32)
        result = result + jnp.dot(gh[...], rest, preferred_element_type=F32)
        result = result + jnp.dot(gl[...], high, preferred_element_type=F32)
        out[pl.ds(start, STEP), :] = (result * query[pl.ds(start, STEP), :]).astype(BF16)

    unrolled = rows < 512
    repeat((STEP + rows) // tile, unrolled, gate)
    repeat(rows // tile, unrolled, ask)
    repeat(-(-rows // STEP), unrolled, convolve)


def filter_rows(plan, pieces, scales, flag, places, short, spectra, matrices, rows):
    terms = len(pieces[0])
    streams, _, kept = pieces[0][0].shape
    extent = scales[0].shape[1]
    arrays = [array for piece in pieces for array in piece]
    constants = [*scales, short, *spectra, *matrices]
    whole = pl.BlockSpec(memory_space=pltpu.VMEM)
    return pl.pallas_call(
        functools.partial(filter_kernel, plan, terms, rows, flag),
        out_shape=jax.ShapeDtypeStruct((rows, kept), BF16),
        in_specs=[pl.BlockSpec(memory_space=pltpu.SMEM)] + [whole] * (len(arrays) + len(constants)),
        out_specs=whole,
        scratch_shapes=[
            pltpu.VMEM((streams, HALO + rows, kept), F32),
            pltpu.VMEM((rows, kept), F32),
            pltpu.VMEM((STEP + rows, kept), BF16),
            pltpu.VMEM((2, extent, 128), F32),
        ],
        compiler_params=pltpu.CompilerParams(vmem_limit_bytes=12 << 20),
        cost_estimate=pl.CostEstimate(flops=1 << 20, bytes_accessed=1 << 16, transcendentals=0),
        name="filter",
    )(places, *arrays, *constants)


def shards(tokens, norm_gain, in_weight, short_taps, long_taps):
    steps, across, cores = (lax.axis_size(a) for a in ("ctx", "width", "sub"))
    z, x, sub = (lax.axis_index(a) for a in ("ctx", "width", "sub"))
    rows, features = tokens.shape
    panel = in_weight.shape[3]
    kept = panel // across
    group = steps // across
    owner = z // group
    depth = features // cores
    mid, small, late = rows // 2, 48, 192

    kinds = range(across)
    places = [sub] + [lax.rem(x + w, across) for w in kinds]
    flag_at = len(places)
    places += [jnp.where(z == k % steps, 0, 1) for k in range(steps)]
    starts = [lax.rem(sub + o, cores) * depth for o in range(cores)]
    part = lax.rem(x - owner + across, across)
    mine = [part == w for w in kinds]
    tap_first = [lax.rem(z, group) * panel + lax.rem(x + w, across) * kept for w in kinds]
    targets = []
    for k in range(steps):
        source = group * x + lax.rem(z + k, group)
        w = lax.rem((source - z - k + 2 * steps) // group, across)
        targets.append(lax.rem(source, group) * panel + lax.rem(x + w, across) * kept)
    places = jnp.stack(places).astype(jnp.int32)
    if kept % 128 == 0:
        targets = jnp.stack(targets).astype(jnp.int32)
    tokens, places, starts, mine, tap_first, targets = lax.optimization_barrier(
        (tokens, places, starts, mine, tap_first, targets)
    )

    def scaled_part(source, first, count, offset):
        block = lax.dynamic_slice(source, (first, starts[offset]), (count, depth)).astype(F32)
        gain = lax.dynamic_slice(norm_gain, (starts[offset],), (depth,))
        return (block * gain[None, :]).astype(BF16)

    ring = [(i, (i + 1) % steps) for i in range(steps)]
    forward = lambda block: lax.ppermute(block, "ctx", ring)

    def sideways(block, w):
        return lax.ppermute(block, "width", [(i, (i + w) % across) for i in range(across)])

    def all_parts(block):
        swaps = [[((c + o) % cores, c) for c in range(cores)] for o in range(1, cores)]
        return [block] + [lax.ppermute(block, "sub", swap) for swap in swaps]

    weight = in_weight[:, :, 0, :]

    def partial(parts, count, w):
        if kept % 128:
            first = lax.rem(x + w, across) * kept
            narrow = lax.dynamic_slice_in_dim(weight, first, kept, 2)
            return project(parts, count, narrow, places, 1, kept)
        return project(parts, count, weight, places, 1 + w, kept)

    def partials(parts, count):
        sent = [partial(parts, count, w) for w in range(1, across)]
        received = [sideways(block, w + 1) for w, block in enumerate(sent)]
        kept_block = partial(parts, count, 0)
        return [kept_block] + sent, [kept_block] + received

    halves = [(mid, rows - mid), (0, mid)]
    last = [(mid, rows - mid), (small, mid - small), (0, small)]
    first, count = halves[0]
    upper = scaled_part(tokens, first, count, 0)
    source, upper = lax.optimization_barrier((tokens, upper))
    power = jnp.sum(source.astype(F32) ** 2, axis=1)
    whole_power = power
    for w in range(1, across):
        whole_power = whole_power + sideways(power, w)
    scale = lax.rsqrt(whole_power / (features * across) + EPSILON)
    terms = [lax.reduce_precision(scale, 8, 7)]
    terms.append(lax.reduce_precision(scale - terms[0], 8, 7))
    terms.append(scale - terms[0] - terms[1])
    extra = jnp.pad(jnp.stack(terms), ((0, EXTRA - 3), (0, depth - rows))).astype(BF16)
    first, count = halves[1]
    lower = jnp.concatenate([scaled_part(source, first, count, 0), extra], axis=0)
    scales = [extra[:, :rows]]

    def taps_of(taps):
        cut = lambda w: lax.dynamic_slice_in_dim(taps, tap_first[w], kept, taps.ndim - 1)
        result = cut(0)
        for w in range(1, across):
            other = sideways(cut(w), w)
            result = jnp.where(mine[w], other, result)
        return result

    short = taps_of(short_taps[:, :, 0, :])
    long = taps_of(long_taps[:, 0, :])
    forward_dft, inverse_dft = transforms()
    spectrum = jnp.dot(
        jnp.asarray(forward_dft[:, : long.shape[0]], F32), long, precision=lax.Precision.HIGHEST
    )
    real, imag = spectrum[: FFT // 2], spectrum[FFT // 2 :]
    first_row = (jnp.arange(FFT // 2) == 0)[:, None]
    spectra = [real, jnp.where(first_row, 0.0, imag), jnp.where(first_row, imag, real)]
    matrices = [jnp.asarray(m) for pair in (split(forward_dft), split(inverse_dft)) for m in pair]

    def unit(step, plan, pieces, count):
        near_far = (scales[step], scales[(step + 1) % steps])
        return filter_rows(plan, pieces, near_far, flag_at + step, places, short, spectra, matrices, count)

    tail = rows - mid
    before = (tail - HALO, HALO, 1, rows - HALO, True)

    def whole_unit(step):
        plan = (before, (0, mid, 0, 0, False), (0, tail, 0, mid, False))
        return unit(step, plan, [table[step + 1, mid], table[step, 0], table[step, mid]], rows)

    table, done = {}, {}
    received, ready = [], set()
    held = {"filters": (short, spectra)}
    waiting = []

    def multiply(key, parts, count):
        local, table[key] = partials(parts, count)
        held["local", key] = local
        received.append(key)

    def arrived(block):
        coming = [key for key in received[:-1] if key not in ready]
        names = list(held)
        pack = (block, [held[n] for n in names], [table[key] for key in coming])
        block, kept_back, blocks = lax.optimization_barrier(pack)
        for key, value in zip(coming, blocks):
            table[key] = value
            ready.add(key)
        for name, value in zip(names, kept_back):
            if name[0] == "unit":
                done[name[1]] = value
        held.clear()
        return block

    def filter_ready():
        for step in range(steps - 1):
            if step not in done and {(step + 1, mid), (step, 0), (step, mid)} <= ready:
                done[step] = whole_unit(step)
                held["unit", step] = done[step]

    for (first, count), block in zip(halves, [upper, lower]):
        own = [block] + [scaled_part(source, first, count, o) for o in range(1, cores)]
        multiply((0, first), own, count)

    moving = [upper, lower]
    for step in range(1, steps):
        if step < steps - 1:
            spans = halves
            moving = [forward(block) for block in moving]
        else:
            spans = last
            upper, lower = moving
            moving = [forward(upper), forward(lower[small:]), forward(lower[:small])]
        for i, (first, count) in enumerate(spans):
            moving[i] = arrived(moving[i])
            if i == 1:
                scales.append(moving[1][-EXTRA:, :rows])
            waiting.append(((step, first), all_parts(moving[i]), count))
            if len(waiting) > 1:
                multiply(*waiting.pop(0))
            filter_ready()
    while waiting:
        multiply(*waiting.pop(0))
    for step in range(steps - 1):
        if step not in done:
            done[step] = whole_unit(step)
    step = steps - 1
    early = unit(
        step,
        ((late - HALO - small, mid - (late - HALO), 0, late - HALO, False), (0, tail, 0, mid, False)),
        [table[step, small], table[step, mid]],
        rows - late,
    )
    begin = unit(
        step,
        (before, (0, small, 0, 0, False), (0, late - small, 0, small, False)),
        [table[0, mid], table[step, 0], table[step, small]],
        late,
    )

    def chosen(k, cut):
        options = [cut((k + group * w) % steps) for w in kinds]
        result = options[0]
        for w in range(1, across):
            result = jnp.where(mine[w], options[w], result)
        return result

    def returned(k, block):
        pairs = []
        for c in range(steps):
            for v in kinds:
                w = (v - c // group) % across
                target = (c - k - group * w) % steps
                pairs.append((c * across + v, target * across + c // group))
        return lax.ppermute(block, ("ctx", "width"), pairs)

    landed = []
    rounds = [k for k in range(steps) if any((k + group * w) % steps == steps - 1 for w in kinds)]
    for k in range(steps):
        if k not in rounds:
            landed.append((k, 0, returned(k, chosen(k, lambda j: done[j]))))
    for k in rounds:
        block = chosen(k, lambda j: early if j == steps - 1 else done[j][late:])
        landed.append((k, late, returned(k, block)))
    for k in rounds:
        block = chosen(k, lambda j: begin if j == steps - 1 else done[j][:late])
        landed.append((k, 0, returned(k, block)))
    return assemble(landed, targets, rows, panel * group, kept)[:, None, :]


def assemble(landed, targets, rows, columns, kept):
    if kept % 128:
        output = jnp.zeros((rows, columns), BF16)
        for k, first, block in landed:
            output = lax.dynamic_update_slice(output, block, (first, targets[k]))
        return output
    count = len(landed)

    def body(targets, *refs):
        blocks, out, sems = refs[:count], refs[count], refs[count + 1]
        copies = []
        for i, (k, first, block) in enumerate(landed):
            column = pl.multiple_of(targets[k], 128)
            spot = out.at[pl.ds(first, block.shape[0]), pl.ds(column, kept)]
            copies.append(pltpu.make_async_copy(blocks[i], spot, sems.at[i]))
            copies[-1].start()
        for copy in copies:
            copy.wait()

    return pl.pallas_call(
        body,
        out_shape=jax.ShapeDtypeStruct((rows, columns), BF16),
        in_specs=[pl.BlockSpec(memory_space=pltpu.SMEM)] + [pl.BlockSpec(memory_space=pl.ANY)] * count,
        out_specs=pl.BlockSpec(memory_space=pl.ANY),
        scratch_shapes=[pltpu.SemaphoreType.DMA((count,))],
        compiler_params=pltpu.CompilerParams(vmem_limit_bytes=12 << 20),
        name="assemble",
    )(targets, *[block for _, _, block in landed])


def solution(mesh):
    placed = (
        P(("parts", "ctx"), "width"),
        P("width"),
        P(None, "width", "sub", "ctx"),
        P(None, None, "sub", "width"),
        P(None, "sub", "width"),
    )
    return jax.shard_map(
        shards,
        mesh=mesh,
        in_specs=placed,
        out_specs=P(("parts", "ctx"), "sub", "width"),
        check_vma=False,
    )
```

time: 270 us -> 198 us (0.73)
  blocking collectives: 64 us -> 0 us
  waiting for transfers between devices: 45.6 us -> 84.9 us
  Pallas kernels: 84.2 us -> 63.3 us
  local copies, waits for them, and re-layouts: 23.3 us -> 6.42 us
  starting transfers between devices: 40.6 us -> 32 us
    all_gather x1 -> x0, blocking collectives: 64 us -> none  [shards(): lax.all_gather(power, ('ctx', 'width'), axis=0).reshape(steps, across, rows)]
    ppermute x7, waiting for transfers between devices: 32.9 us -> 67.5 us  [shards(): forward = lambda block: lax.ppermute(block, 'ctx', ring)]
    pallas_call x23 -> x24, Pallas kernels: 84.2 us -> 63.3 us  [the longest x18 46.4 us: project(): pl.pallas_call(body, out_shape=jax.ShapeDtypeStruct((streams, rows, kept)...]
    unnamed x40 -> x26, local copies, waits for them, and re-layouts: 16 us -> 4.65 us
    ppermute x6, starting transfers between devices: 21.4 us -> 10.5 us  [returned(): return lax.ppermute(block, ('ctx', 'width'), pairs)]
    ppermute x6, waiting for transfers between devices: 2.64 us -> 11.8 us  [returned(): return lax.ppermute(block, ('ctx', 'width'), pairs)]
    ppermute x11 -> x12, waiting for transfers between devices: 10 us -> 5.49 us  [sideways(): lax.ppermute(block, 'width', [(i, (i + w) % across) for i in range(across)])]
    ppermute x11 -> x12, starting transfers between devices: 12.8 us -> 14.8 us  [sideways(): lax.ppermute(block, 'width', [(i, (i + w) % across) for i in range(across)])]
  transfers between devices with their start and end apart: 31 -> 32, of which waited for: 7 -> 9; matrix products, arithmetic and copies ran while one was open for 5% -> 3% of each run, Pallas kernels for 31% -> 32%
where the time goes in v2:
time: 198 us; the launch traced here: 195 us
  waiting for transfers between devices  84.9 us (43%)
  Pallas kernels  63.3 us (32%)
  starting transfers between devices  32 us (16%)
  other arithmetic  7.46 us (4%)
  local copies, waits for them, and re-layouts  6.42 us (3%)
    ppermute x7, waiting for transfers between devices, shards(): forward = lambda block: lax.ppermute(block, 'ctx', ring)  67.5 us
    pallas_call x18, Pallas kernels, project(): pl.pallas_call(body, out_shape=jax.ShapeDtypeStruct((streams, rows, kept)...  46.4 us
    pallas_call x5, Pallas kernels, filter_rows(): pl.pallas_call(functools.partial(filter_kernel, plan, terms, rows, flag),...  15.4 us
    ppermute x12, starting transfers between devices, sideways(): lax.ppermute(block, 'width', [(i, (i + w) % across) for i in range(across)])  14.8 us
    ppermute x6, waiting for transfers between devices, returned(): return lax.ppermute(block, ('ctx', 'width'), pairs)  11.8 us
    ppermute x6, starting transfers between devices, returned(): return lax.ppermute(block, ('ctx', 'width'), pairs)  10.5 us
    ppermute x7, starting transfers between devices, shards(): forward = lambda block: lax.ppermute(block, 'ctx', ring)  6.63 us
    ppermute x12, waiting for transfers between devices, sideways(): lax.ppermute(block, 'width', [(i, (i + w) % across) for i in range(across)])  5.49 us
  transfers between devices with their start and end apart: 32, of which 9 were waited for; matrix products, arithmetic and copies ran while one was open for 3% of the time, Pallas kernels for 32%

profile of v2, /device:TPU:0, one launch (start us, length us, event | category | flops | bytes accessed | tf_op | source)
XLA Modules:
  0.0 195.1 jit_solution(13100781403702997051)
XLA Ops:
  2.8 3.1 %collective-permute-start = (bf16[256,2048]{1,0:T(8,128)(2,1)S(1)}, bf16[256,2048]{1,0:T(8,128)(2,1)S(1)}, u32[]{:S(2)}, u32[]{:S(2)}) collective-permute-start(bf16[256,2048]{1,0:T(8,128)(2,1)S(1)} %multiply_convert_fusion.3.refs_0_), channel_id=1, source_target_pairs={{0,4},{4,8},{8,12},{12,0},{1,5},{5,9},{9,13},{13,1},{2,6},{6,10},{... | collective-permute-start | bytes 3145736 | tf_op jit(solution)/shard_map/ppermute | solution.py:220
  8.8 3.4 %multiply_reduce_fusion = f32[512]{0:T(512)S(1)} fusion(bf16[512,4096]{1,0:T(8,128)(2,1)} %param.10), kind=kLoop, calls=%fused_computation | loop fusion | flops 6290944 | bytes 4196352 | tf_op jit(solution)/shard_map/reduce_sum | solution.py:249
  15.4 4.6 %copy-done = bf16[3,4096,1,512]{3,1,2,0:T(8,128)(2,1)S(1)} copy-done((bf16[3,4096,1,512]{3,1,2,0:T(8,128)(2,1)S(1)}, bf16[3,4096,1,512]{3,1,2,0:T(8,128)(2,1)}, u32[]{:S(2)}) %copy-start) | copy-done | bytes 12582936
  19.9 2.8 %project.18 = bf16[3,256,256]{2,1,0:T(8,128)(2,1)S(1)} custom-call(s32[7]{0:T(128)S(1)} %stack.62.places, bf16[256,2048]{1,0:T(8,128)(2,1)S(1)} %multiply_convert_fusion.3.refs_0_, bf16[256,2048]{1,0:T(8,128)(2,1)S(1)} %get-tuple-element.66.refs_1_, bf16[3,4096,512]{2,1,0:T(8,128)(2,1)S(1)} %bitcast.25), custom_call_target="tpu_custom_call" | custom-call | flops 1048576 | bytes 65536 | tf_op jit(solution)/shard_map/project/pallas_call | solution.py:79
  23.6 2.8 %project.21.refs_4_.refs_0_ = bf16[3,256,256]{2,1,0:T(8,128)(2,1)S(1)} custom-call(s32[7]{0:T(128)S(1)} %stack.62.places, bf16[256,2048]{1,0:T(8,128)(2,1)S(1)} %multiply_convert_fusion.3.refs_0_, bf16[256,2048]{1,0:T(8,128)(2,1)S(1)} %get-tuple-element.66.refs_1_, bf16[3,4096,512]{2,1,0:T(8,128)(2,1)S(1)} %bitcast.26), custom_call_target="tpu_custom_call" | custom-call | flops 1048576 | bytes 65536 | tf_op jit(solution)/shard_map/project/pallas_call | solution.py:79
  28.3 2.7 %project.19.refs_2_ = bf16[3,256,256]{2,1,0:T(8,128)(2,1)S(1)} custom-call(s32[7]{0:T(128)S(1)} %stack.62.places, bf16[264,2048]{1,0:T(8,128)(2,1)S(1)} %pad_maximum_fusion.refs_0_, bf16[256,2048]{1,0:T(8,128)(2,1)S(1)} %get-tuple-element.65.refs_1_, bf16[3,4096,512]{2,1,0:T(8,128)(2,1)S(1)} %bitcast.29), custom_call_target="tpu_custom_call" | custom-call | flops 1048576 | bytes 65536 | tf_op jit(solution)/shard_map/project/pallas_call | solution.py:79
  31.0 2.8 %project.20 = bf16[3,256,256]{2,1,0:T(8,128)(2,1)S(1)} custom-call(s32[7]{0:T(128)S(1)} %stack.62.places, bf16[264,2048]{1,0:T(8,128)(2,1)S(1)} %pad_maximum_fusion.refs_0_, bf16[256,2048]{1,0:T(8,128)(2,1)S(1)} %get-tuple-element.65.refs_1_, bf16[3,4096,512]{2,1,0:T(8,128)(2,1)S(1)} %bitcast.30), custom_call_target="tpu_custom_call" | custom-call | flops 1048576 | bytes 65536 | tf_op jit(solution)/shard_map/project/pallas_call | solution.py:79
  36.0 19.2 %collective-permute-done.10.refs_0_ = bf16[264,2048]{1,0:T(8,128)(2,1)S(1)} collective-permute-done((bf16[264,2048]{1,0:T(8,128)(2,1)S(1)}, bf16[264,2048]{1,0:T(8,128)(2,1)S(1)}, u32[]{:S(2)}, u32[]{:S(2)}) %collective-permute-start.10) | collective-permute-done | bytes 1081376 | tf_op jit(solution)/shard_map/ppermute | solution.py:220
  56.8 2.8 %project.22.refs_0_.refs_4_ = bf16[3,256,256]{2,1,0:T(8,128)(2,1)S(1)} custom-call(s32[7]{0:T(128)S(1)} %stack.62.places, bf16[256,2048]{1,0:T(8,128)(2,1)S(1)} %collective-permute-done.refs_0_, bf16[256,2048]{1,0:T(8,128)(2,1)S(1)} %collective-permute-done.6.refs_1_, bf16[3,4096,512]{2,1,0:T(8,128)(2,1)S(1)} %bitcast.31), custom_call_target="tpu_custom_call" | custom-call | flops 1048576 | bytes 65536 | tf_op jit(solution)/shard_map/project/pallas_call | solution.py:79
  59.6 2.8 %project.23 = bf16[3,256,256]{2,1,0:T(8,128)(2,1)S(1)} custom-call(s32[7]{0:T(128)S(1)} %stack.62.places, bf16[256,2048]{1,0:T(8,128)(2,1)S(1)} %collective-permute-done.refs_0_, bf16[256,2048]{1,0:T(8,128)(2,1)S(1)} %collective-permute-done.6.refs_1_, bf16[3,4096,512]{2,1,0:T(8,128)(2,1)S(1)} %bitcast.32), custom_call_target="tpu_custom_call" | custom-call | flops 1048576 | bytes 65536 | tf_op jit(solution)/shard_map/project/pallas_call | solution.py:79
  62.4 4.4 %collective-permute-done.7.refs_3_ = bf16[3,256,256]{2,1,0:T(8,128)(2,1)S(1)} collective-permute-done((bf16[3,256,256]{2,1,0:T(8,128)(2,1)S(1)}, bf16[3,256,256]{2,1,0:T(8,128)(2,1)S(1)}, u32[]{:S(2)}, u32[]{:S(2)}) %collective-permute-start.7) | collective-permute-done | bytes 393248 | tf_op jit(solution)/shard_map/ppermute | solution.py:223
  66.8 10.9 %collective-permute-done.5.refs_0_ = bf16[256,2048]{1,0:T(8,128)(2,1)S(1)} collective-permute-done((bf16[256,2048]{1,0:T(8,128)(2,1)S(1)}, bf16[256,2048]{1,0:T(8,128)(2,1)S(1)}, u32[]{:S(2)}, u32[]{:S(2)}) %collective-permute-start.5) | collective-permute-done | bytes 1048608 | tf_op jit(solution)/shard_map/ppermute | solution.py:220
  79.3 2.8 %project.26.refs_2_ = bf16[3,256,256]{2,1,0:T(8,128)(2,1)S(1)} custom-call(s32[7]{0:T(128)S(1)} %stack.62.places, bf16[264,2048]{1,0:T(8,128)(2,1)S(1)} %collective-permute-done.10.refs_0_, bf16[264,2048]{1,0:T(8,128)(2,1)S(1)} %collective-permute-done.12.refs_1_, bf16[3,4096,512]{2,1,0:T(8,128)(2,1)S(1)} %bitcast.33), custom_call_target="tpu_custom_call" | custom-call | flops 1048576 | bytes 65536 | tf_op jit(solution)/shard_map/project/pallas_call | solution.py:79
  82.2 2.8 %project.27 = bf16[3,256,256]{2,1,0:T(8,128)(2,1)S(1)} custom-call(s32[7]{0:T(128)S(1)} %stack.62.places, bf16[264,2048]{1,0:T(8,128)(2,1)S(1)} %collective-permute-done.10.refs_0_, bf16[264,2048]{1,0:T(8,128)(2,1)S(1)} %collective-permute-done.12.refs_1_, bf16[3,4096,512]{2,1,0:T(8,128)(2,1)S(1)} %bitcast.34), custom_call_target="tpu_custom_call" | custom-call | flops 1048576 | bytes 65536 | tf_op jit(solution)/shard_map/project/pallas_call | solution.py:79
  84.9 16.0 %collective-permute-done.11.refs_0_ = bf16[264,2048]{1,0:T(8,128)(2,1)S(1)} collective-permute-done((bf16[264,2048]{1,0:T(8,128)(2,1)S(1)}, bf16[264,2048]{1,0:T(8,128)(2,1)S(1)}, u32[]{:S(2)}, u32[]{:S(2)}) %collective-permute-start.11) | collective-permute-done | bytes 1081376 | tf_op jit(solution)/shard_map/ppermute | solution.py:220
  102.9 3.8 %filter.5 = bf16[512,256]{1,0:T(8,128)(2,1)S(1)} custom-call(s32[7]{0:T(128)S(1)} %stack.62.places, bf16[3,256,256]{2,1,0:T(8,128)(2,1)S(1)} %project.22.refs_0_.refs_4_, bf16[3,256,256]{2,1,0:T(8,128)(2,1)S(1)} %collective-permute-done.13.refs_1_.refs_5_, bf16[3,256,256]{2,1,0:T(8,128)(2,1)S(1)} %project.19.refs_2_, ...), custom_call_target="tpu_custom_call" | custom-call | flops 1048576 | bytes 65536 | tf_op jit(solution)/shard_map/filter/pallas_call | solution.py:166
  106.7 2.7 %project.24.refs_0_.refs_4_ = bf16[3,256,256]{2,1,0:T(8,128)(2,1)S(1)} custom-call(s32[7]{0:T(128)S(1)} %stack.62.places, bf16[256,2048]{1,0:T(8,128)(2,1)S(1)} %collective-permute-done.5.refs_0_, bf16[256,2048]{1,0:T(8,128)(2,1)S(1)} %collective-permute-done.9.refs_1_, bf16[3,4096,512]{2,1,0:T(8,128)(2,1)S(1)} %bitcast.35), custom_call_target="tpu_custom_call" | custom-call | flops 1048576 | bytes 65536 | tf_op jit(solution)/shard_map/project/pallas_call | solution.py:79
  109.4 2.8 %project.25 = bf16[3,256,256]{2,1,0:T(8,128)(2,1)S(1)} custom-call(s32[7]{0:T(128)S(1)} %stack.62.places, bf16[256,2048]{1,0:T(8,128)(2,1)S(1)} %collective-permute-done.5.refs_0_, bf16[256,2048]{1,0:T(8,128)(2,1)S(1)} %collective-permute-done.9.refs_1_, bf16[3,4096,512]{2,1,0:T(8,128)(2,1)S(1)} %bitcast.36), custom_call_target="tpu_custom_call" | custom-call | flops 1048576 | bytes 65536 | tf_op jit(solution)/shard_map/project/pallas_call | solution.py:79
  112.8 10.5 %collective-permute-done.8.refs_0_ = bf16[256,2048]{1,0:T(8,128)(2,1)S(1)} collective-permute-done((bf16[256,2048]{1,0:T(8,128)(2,1)S(1)}, bf16[256,2048]{1,0:T(8,128)(2,1)S(1)}, u32[]{:S(2)}, u32[]{:S(2)}) %collective-permute-start.8) | collective-permute-done | bytes 1048608 | tf_op jit(solution)/shard_map/ppermute | solution.py:220
  124.9 2.7 %project.30.refs_2_ = bf16[3,256,256]{2,1,0:T(8,128)(2,1)S(1)} custom-call(s32[7]{0:T(128)S(1)} %stack.62.places, bf16[264,2048]{1,0:T(8,128)(2,1)S(1)} %collective-permute-done.11.refs_0_, bf16[264,2048]{1,0:T(8,128)(2,1)S(1)} %collective-permute-done.19.refs_1_, bf16[3,4096,512]{2,1,0:T(8,128)(2,1)S(1)} %bitcast.37), custom_call_target="tpu_custom_call" | custom-call | flops 1048576 | bytes 65536 | tf_op jit(solution)/shard_map/project/pallas_call | solution.py:79
  127.7 2.8 %project.31 = bf16[3,256,256]{2,1,0:T(8,128)(2,1)S(1)} custom-call(s32[7]{0:T(128)S(1)} %stack.62.places, bf16[264,2048]{1,0:T(8,128)(2,1)S(1)} %collective-permute-done.11.refs_0_, bf16[264,2048]{1,0:T(8,128)(2,1)S(1)} %collective-permute-done.19.refs_1_, bf16[3,4096,512]{2,1,0:T(8,128)(2,1)S(1)} %bitcast.38), custom_call_target="tpu_custom_call" | custom-call | flops 1048576 | bytes 65536 | tf_op jit(solution)/shard_map/project/pallas_call | solution.py:79
  130.5 10.8 %collective-permute-done.18.refs_0_ = bf16[216,2048]{1,0:T(8,128)(2,1)S(1)} collective-permute-done((bf16[216,2048]{1,0:T(8,128)(2,1)S(1)}, bf16[216,2048]{1,0:T(8,128)(2,1)S(1)}, u32[]{:S(2)}, u32[]{:S(2)}) %collective-permute-start.18) | collective-permute-done | bytes 884768 | tf_op jit(solution)/shard_map/ppermute | solution.py:220
  142.9 2.8 %project.29 = bf16[3,256,256]{2,1,0:T(8,128)(2,1)S(1)} custom-call(s32[7]{0:T(128)S(1)} %stack.62.places, bf16[256,2048]{1,0:T(8,128)(2,1)S(1)} %collective-permute-done.8.refs_0_, bf16[256,2048]{1,0:T(8,128)(2,1)S(1)} %collective-permute-done.15.refs_1_, bf16[3,4096,512]{2,1,0:T(8,128)(2,1)S(1)} %bitcast.39), custom_call_target="tpu_custom_call" | custom-call | flops 1048576 | bytes 65536 | tf_op jit(solution)/shard_map/project/pallas_call | solution.py:79
  146.2 3.8 %filter.6 = bf16[512,256]{1,0:T(8,128)(2,1)S(1)} custom-call(s32[7]{0:T(128)S(1)} %stack.62.places, bf16[3,256,256]{2,1,0:T(8,128)(2,1)S(1)} %project.24.refs_0_.refs_4_, bf16[3,256,256]{2,1,0:T(8,128)(2,1)S(1)} %collective-permute-done.20.refs_1_.refs_5_, bf16[3,256,256]{2,1,0:T(8,128)(2,1)S(1)} %project.26.refs_2_, ...), custom_call_target="tpu_custom_call" | custom-call | flops 1048576 | bytes 65536 | tf_op jit(solution)/shard_map/filter/pallas_call | solution.py:166
  150.0 2.7 %project.28.refs_0_.refs_2_ = bf16[3,256,256]{2,1,0:T(8,128)(2,1)S(1)} custom-call(s32[7]{0:T(128)S(1)} %stack.62.places, bf16[256,2048]{1,0:T(8,128)(2,1)S(1)} %collective-permute-done.8.refs_0_, bf16[256,2048]{1,0:T(8,128)(2,1)S(1)} %collective-permute-done.15.refs_1_, bf16[3,4096,512]{2,1,0:T(8,128)(2,1)S(1)} %bitcast.40), custom_call_target="tpu_custom_call" | custom-call | flops 1048576 | bytes 65536 | tf_op jit(solution)/shard_map/project/pallas_call | solution.py:79
  153.2 2.0 %project.33 = bf16[3,208,256]{2,1,0:T(8,128)(2,1)S(1)} custom-call(s32[7]{0:T(128)S(1)} %stack.62.places, bf16[216,2048]{1,0:T(8,128)(2,1)S(1)} %collective-permute-done.18.refs_0_, bf16[216,2048]{1,0:T(8,128)(2,1)S(1)} %collective-permute-done.24.refs_1_, bf16[3,4096,512]{2,1,0:T(8,128)(2,1)S(1)} %bitcast.41), custom_call_target="tpu_custom_call" | custom-call | flops 1048576 | bytes 65536 | tf_op jit(solution)/shard_map/project/pallas_call | solution.py:79
  160.9 2.1 %project.32.refs_0_.refs_4_ = bf16[3,208,256]{2,1,0:T(8,128)(2,1)S(1)} custom-call(s32[7]{0:T(128)S(1)} %stack.62.places, bf16[216,2048]{1,0:T(8,128)(2,1)S(1)} %collective-permute-done.18.refs_0_, bf16[216,2048]{1,0:T(8,128)(2,1)S(1)} %collective-permute-done.24.refs_1_, bf16[3,4096,512]{2,1,0:T(8,128)(2,1)S(1)} %bitcast.44), custom_call_target="tpu_custom_call" | custom-call | flops 1048576 | bytes 65536 | tf_op jit(solution)/shard_map/project/pallas_call | solution.py:79
  163.1 3.8 %filter.7 = bf16[512,256]{1,0:T(8,128)(2,1)S(1)} custom-call(s32[7]{0:T(128)S(1)} %stack.62.places, bf16[3,256,256]{2,1,0:T(8,128)(2,1)S(1)} %project.28.refs_0_.refs_2_, bf16[3,256,256]{2,1,0:T(8,128)(2,1)S(1)} %collective-permute-done.16.refs_1_.refs_3_, bf16[3,256,256]{2,1,0:T(8,128)(2,1)S(1)} %project.30.refs_2_, ...), custom_call_target="tpu_custom_call" | custom-call | flops 1048576 | bytes 65536 | tf_op jit(solution)/shard_map/filter/pallas_call | solution.py:166
  167.6 5.1 %collective-permute-start.23 = (bf16[512,256]{1,0:T(8,128)(2,1)S(1)}, bf16[512,256]{1,0:T(8,128)(2,1)S(1)}, u32[]{:S(2)}, u32[]{:S(2)}) collective-permute-start(bf16[512,256]{1,0:T(8,128)(2,1)S(1)} %get-tuple-element.68), channel_id=1, source_target_pairs={{0,8},{2,0},{4,12},{6,4},{8,10},{10,2},{12,14},{14,6},{1,9},{3,1},... | collective-permute-start | bytes 786440 | tf_op jit(solution)/shard_map/ppermute | solution.py:376
  172.8 2.2 %filter.8 = bf16[320,256]{1,0:T(8,128)(2,1)S(1)} custom-call(s32[7]{0:T(128)S(1)} %stack.62.places, bf16[3,208,256]{2,1,0:T(8,128)(2,1)S(1)} %project.32.refs_0_.refs_4_, bf16[3,208,256]{2,1,0:T(8,128)(2,1)S(1)} %collective-permute-done.25.refs_1_.refs_5_, bf16[3,256,256]{2,1,0:T(8,128)(2,1)S(1)} %project.28.refs_0_.refs_2_, ...), custom_call_target="tpu_custom_call" | custom-call | flops 1048576 | bytes 65536 | tf_op jit(solution)/shard_map/filter/pallas_call | solution.py:166
  179.0 2.0 %collective-permute-start.30 = (bf16[192,256]{1,0:T(8,128)(2,1)S(1)}, bf16[192,256]{1,0:T(8,128)(2,1)S(1)}, u32[]{:S(2)}, u32[]{:S(2)}) collective-permute-start(bf16[192,256]{1,0:T(8,128)(2,1)S(1)} %get-tuple-element.75), channel_id=1, source_target_pairs={{0,12},{2,4},{4,0},{6,8},{8,14},{10,6},{12,2},{14,10},{1,13},{3,5}... | collective-permute-start | bytes 294920 | tf_op jit(solution)/shard_map/ppermute | solution.py:376
  181.5 11.8 %collective-permute-done.30.refs_4_ = bf16[192,256]{1,0:T(8,128)(2,1)S(1)} collective-permute-done((bf16[192,256]{1,0:T(8,128)(2,1)S(1)}, bf16[192,256]{1,0:T(8,128)(2,1)S(1)}, u32[]{:S(2)}, u32[]{:S(2)}) %collective-permute-start.30) | collective-permute-done | bytes 98336 | tf_op jit(solution)/shard_map/ppermute | solution.py:376
  (110 shorter events, 36.1 us)
Async XLA Ops:
  2.8 31.5 %collective-permute-start = (bf16[256,2048]{1,0:T(8,128)(2,1)S(1)}, bf16[256,2048]{1,0:T(8,128)(2,1)S(1)}, u32[]{:S(2)}, u32[]{:S(2)}) collective-permute-start(bf16[256,2048]{1,0:T(8,128)(2,1)S(1)} %multiply_convert_fusion.3.refs_0_), channel_id=1, source_target_pairs={{0,4},{4,8},{8,12},{12,0},{1,5},{5,9},{9,13},{13,1},{2,6},{6,10},{... | collective-permute-start | bytes 3145736 | tf_op jit(solution)/shard_map/ppermute | solution.py:220
  6.0 27.8 %collective-permute-start.1 = (f32[3,3,256]{2,1,0:T(4,128)S(1)}, f32[3,3,256]{2,1,0:T(4,128)S(1)}, u32[]{:S(2)}, u32[]{:S(2)}) collective-permute-start(f32[3,3,256]{2,1,0:T(4,128)S(1)} %bitcast.46), channel_id=1, source_target_pairs={{0,2},{2,0},{1,3},{3,1},{4,6},{6,4},{5,7},{7,5},{8,10},{10,8},{9,1... | collective-permute-start | bytes 27656 | tf_op jit(solution)/shard_map/ppermute | solution.py:223
  8.2 25.6 %collective-permute-start.2 = (f32[128,256]{1,0:T(8,128)S(1)}, f32[128,256]{1,0:T(8,128)S(1)}, u32[]{:S(2)}, u32[]{:S(2)}) collective-permute-start(f32[128,256]{1,0:T(8,128)S(1)} %bitcast.45), channel_id=1, source_target_pairs={{0,2},{2,0},{1,3},{3,1},{4,6},{6,4},{5,7},{7,5},{8,10},{10,8},{9,1... | collective-permute-start | bytes 393224 | tf_op jit(solution)/shard_map/ppermute | solution.py:223
  12.2 14.2 %collective-permute-start.3 = (f32[512]{0:T(512)S(1)}, f32[512]{0:T(512)S(1)}, u32[]{:S(2)}, u32[]{:S(2)}) collective-permute-start(f32[512]{0:T(512)S(1)} %multiply_reduce_fusion), channel_id=1, source_target_pairs={{0,2},{2,0},{1,3},{3,1},{4,6},{6,4},{5,7},{7,5},{8,10},{10,8},{9,1... | collective-permute-start | bytes 6152 | tf_op jit(solution)/shard_map/ppermute | solution.py:223
  22.7 11.6 %collective-permute-start.4 = (bf16[3,256,256]{2,1,0:T(8,128)(2,1)S(1)}, bf16[3,256,256]{2,1,0:T(8,128)(2,1)S(1)}, u32[]{:S(2)}, u32[]{:S(2)}) collective-permute-start(bf16[3,256,256]{2,1,0:T(8,128)(2,1)S(1)} %project.18), channel_id=1, source_target_pairs={{0,2},{2,0},{1,3},{3,1},{4,6},{6,4},{5,7},{7,5},{8,10},{10,8},{9,1... | collective-permute-start | bytes 1179656 | tf_op jit(solution)/shard_map/ppermute | solution.py:223
  26.6 28.6 %collective-permute-start.10 = (bf16[264,2048]{1,0:T(8,128)(2,1)S(1)}, bf16[264,2048]{1,0:T(8,128)(2,1)S(1)}, u32[]{:S(2)}, u32[]{:S(2)}) collective-permute-start(bf16[264,2048]{1,0:T(8,128)(2,1)S(1)} %pad_maximum_fusion.refs_0_), channel_id=1, source_target_pairs={{0,4},{4,8},{8,12},{12,0},{1,5},{5,9},{9,13},{13,1},{2,6},{6,10},{... | collective-permute-start | bytes 3244040 | tf_op jit(solution)/shard_map/ppermute | solution.py:220
  34.3 22.5 %collective-permute-start.6 = (bf16[256,2048]{1,0:T(8,128)(2,1)S(1)}, bf16[256,2048]{1,0:T(8,128)(2,1)S(1)}, u32[]{:S(2)}, u32[]{:S(2)}) collective-permute-start(bf16[256,2048]{1,0:T(8,128)(2,1)S(1)} %collective-permute-done.refs_0_), channel_id=1, source_target_pairs={{1,0},{0,1},{3,2},{2,3},{5,4},{4,5},{7,6},{6,7},{9,8},{8,9},{11,10... | collective-permute-start | bytes 3145736 | tf_op jit(solution)/shard_map/ppermute | solution.py:227
  34.4 43.3 %collective-permute-start.5 = (bf16[256,2048]{1,0:T(8,128)(2,1)S(1)}, bf16[256,2048]{1,0:T(8,128)(2,1)S(1)}, u32[]{:S(2)}, u32[]{:S(2)}) collective-permute-start(bf16[256,2048]{1,0:T(8,128)(2,1)S(1)} %collective-permute-done.refs_0_), channel_id=1, source_target_pairs={{0,4},{4,8},{8,12},{12,0},{1,5},{5,9},{9,13},{13,1},{2,6},{6,10},{... | collective-permute-start | bytes 3145736 | tf_op jit(solution)/shard_map/ppermute | solution.py:220
  55.3 24.0 %collective-permute-start.12 = (bf16[264,2048]{1,0:T(8,128)(2,1)S(1)}, bf16[264,2048]{1,0:T(8,128)(2,1)S(1)}, u32[]{:S(2)}, u32[]{:S(2)}) collective-permute-start(bf16[264,2048]{1,0:T(8,128)(2,1)S(1)} %collective-permute-done.10.refs_0_), channel_id=1, source_target_pairs={{1,0},{0,1},{3,2},{2,3},{5,4},{4,5},{7,6},{6,7},{9,8},{8,9},{11,10... | collective-permute-start | bytes 3244040 | tf_op jit(solution)/shard_map/ppermute | solution.py:227
  55.3 45.6 %collective-permute-start.11 = (bf16[264,2048]{1,0:T(8,128)(2,1)S(1)}, bf16[264,2048]{1,0:T(8,128)(2,1)S(1)}, u32[]{:S(2)}, u32[]{:S(2)}) collective-permute-start(bf16[264,2048]{1,0:T(8,128)(2,1)S(1)} %collective-permute-done.10.refs_0_), channel_id=1, source_target_pairs={{0,4},{4,8},{8,12},{12,0},{1,5},{5,9},{9,13},{13,1},{2,6},{6,10},{... | collective-permute-start | bytes 3244040 | tf_op jit(solution)/shard_map/ppermute | solution.py:220
  55.3 11.5 %collective-permute-start.7 = (bf16[3,256,256]{2,1,0:T(8,128)(2,1)S(1)}, bf16[3,256,256]{2,1,0:T(8,128)(2,1)S(1)}, u32[]{:S(2)}, u32[]{:S(2)}) collective-permute-start(bf16[3,256,256]{2,1,0:T(8,128)(2,1)S(1)} %project.20), channel_id=1, source_target_pairs={{0,2},{2,0},{1,3},{3,1},{4,6},{6,4},{5,7},{7,5},{8,10},{10,8},{9,1... | collective-permute-start | bytes 1179656 | tf_op jit(solution)/shard_map/ppermute | solution.py:223
  77.7 29.0 %collective-permute-start.9 = (bf16[256,2048]{1,0:T(8,128)(2,1)S(1)}, bf16[256,2048]{1,0:T(8,128)(2,1)S(1)}, u32[]{:S(2)}, u32[]{:S(2)}) collective-permute-start(bf16[256,2048]{1,0:T(8,128)(2,1)S(1)} %collective-permute-done.5.refs_0_), channel_id=1, source_target_pairs={{1,0},{0,1},{3,2},{2,3},{5,4},{4,5},{7,6},{6,7},{9,8},{8,9},{11,10... | collective-permute-start | bytes 3145736 | tf_op jit(solution)/shard_map/ppermute | solution.py:227
  77.7 45.6 %collective-permute-start.8 = (bf16[256,2048]{1,0:T(8,128)(2,1)S(1)}, bf16[256,2048]{1,0:T(8,128)(2,1)S(1)}, u32[]{:S(2)}, u32[]{:S(2)}) collective-permute-start(bf16[256,2048]{1,0:T(8,128)(2,1)S(1)} %collective-permute-done.5.refs_0_), channel_id=1, source_target_pairs={{0,4},{4,8},{8,12},{12,0},{1,5},{5,9},{9,13},{13,1},{2,6},{6,10},{... | collective-permute-start | bytes 3145736 | tf_op jit(solution)/shard_map/ppermute | solution.py:220
  77.7 23.2 %collective-permute-start.13 = (bf16[3,256,256]{2,1,0:T(8,128)(2,1)S(1)}, bf16[3,256,256]{2,1,0:T(8,128)(2,1)S(1)}, u32[]{:S(2)}, u32[]{:S(2)}) collective-permute-start(bf16[3,256,256]{2,1,0:T(8,128)(2,1)S(1)} %project.23), channel_id=1, source_target_pairs={{0,2},{2,0},{1,3},{3,1},{4,6},{6,4},{5,7},{7,5},{8,10},{10,8},{9,1... | collective-permute-start | bytes 1179656 | tf_op jit(solution)/shard_map/ppermute | solution.py:223
  100.9 24.0 %collective-permute-start.19 = (bf16[264,2048]{1,0:T(8,128)(2,1)S(1)}, bf16[264,2048]{1,0:T(8,128)(2,1)S(1)}, u32[]{:S(2)}, u32[]{:S(2)}) collective-permute-start(bf16[264,2048]{1,0:T(8,128)(2,1)S(1)} %collective-permute-done.11.refs_0_), channel_id=1, source_target_pairs={{1,0},{0,1},{3,2},{2,3},{5,4},{4,5},{7,6},{6,7},{9,8},{8,9},{11,10... | collective-permute-start | bytes 3244040 | tf_op jit(solution)/shard_map/ppermute | solution.py:227
  101.0 40.3 %collective-permute-start.18 = (bf16[216,2048]{1,0:T(8,128)(2,1)S(1)}, bf16[216,2048]{1,0:T(8,128)(2,1)S(1)}, u32[]{:S(2)}, u32[]{:S(2)}) collective-permute-start(bf16[216,2048]{1,0:T(8,128)(2,1)S(1)} %slice.37), channel_id=1, source_target_pairs={{0,4},{4,8},{8,12},{12,0},{1,5},{5,9},{9,13},{13,1},{2,6},{6,10},{... | collective-permute-start | bytes 2654216 | tf_op jit(solution)/shard_map/ppermute | solution.py:220
  101.2 11.6 %collective-permute-start.14 = (bf16[3,256,256]{2,1,0:T(8,128)(2,1)S(1)}, bf16[3,256,256]{2,1,0:T(8,128)(2,1)S(1)}, u32[]{:S(2)}, u32[]{:S(2)}) collective-permute-start(bf16[3,256,256]{2,1,0:T(8,128)(2,1)S(1)} %project.27), channel_id=1, source_target_pairs={{0,2},{2,0},{1,3},{3,1},{4,6},{6,4},{5,7},{7,5},{8,10},{10,8},{9,1... | collective-permute-start | bytes 1179656 | tf_op jit(solution)/shard_map/ppermute | solution.py:223
  123.4 19.5 %collective-permute-start.15 = (bf16[256,2048]{1,0:T(8,128)(2,1)S(1)}, bf16[256,2048]{1,0:T(8,128)(2,1)S(1)}, u32[]{:S(2)}, u32[]{:S(2)}) collective-permute-start(bf16[256,2048]{1,0:T(8,128)(2,1)S(1)} %collective-permute-done.8.refs_0_), channel_id=1, source_target_pairs={{1,0},{0,1},{3,2},{2,3},{5,4},{4,5},{7,6},{6,7},{9,8},{8,9},{11,10... | collective-permute-start | bytes 3145736 | tf_op jit(solution)/shard_map/ppermute | solution.py:227
  123.4 17.9 %collective-permute-start.20 = (bf16[3,256,256]{2,1,0:T(8,128)(2,1)S(1)}, bf16[3,256,256]{2,1,0:T(8,128)(2,1)S(1)}, u32[]{:S(2)}, u32[]{:S(2)}) collective-permute-start(bf16[3,256,256]{2,1,0:T(8,128)(2,1)S(1)} %project.25), channel_id=1, source_target_pairs={{0,2},{2,0},{1,3},{3,1},{4,6},{6,4},{5,7},{7,5},{8,10},{10,8},{9,1... | collective-permute-start | bytes 1179656 | tf_op jit(solution)/shard_map/ppermute | solution.py:223
  141.3 11.9 %collective-permute-start.24 = (bf16[216,2048]{1,0:T(8,128)(2,1)S(1)}, bf16[216,2048]{1,0:T(8,128)(2,1)S(1)}, u32[]{:S(2)}, u32[]{:S(2)}) collective-permute-start(bf16[216,2048]{1,0:T(8,128)(2,1)S(1)} %collective-permute-done.18.refs_0_), channel_id=1, source_target_pairs={{1,0},{0,1},{3,2},{2,3},{5,4},{4,5},{7,6},{6,7},{9,8},{8,9},{11,10... | collective-permute-start | bytes 2654216 | tf_op jit(solution)/shard_map/ppermute | solution.py:227
  141.3 11.9 %collective-permute-start.21 = (bf16[3,256,256]{2,1,0:T(8,128)(2,1)S(1)}, bf16[3,256,256]{2,1,0:T(8,128)(2,1)S(1)}, u32[]{:S(2)}, u32[]{:S(2)}) collective-permute-start(bf16[3,256,256]{2,1,0:T(8,128)(2,1)S(1)} %project.31), channel_id=1, source_target_pairs={{0,2},{2,0},{1,3},{3,1},{4,6},{6,4},{5,7},{7,5},{8,10},{10,8},{9,1... | collective-permute-start | bytes 1179656 | tf_op jit(solution)/shard_map/ppermute | solution.py:223
  142.8 9.9 %collective-permute-start.17 = (bf16[48,2048]{1,0:T(8,128)(2,1)S(1)}, bf16[48,2048]{1,0:T(8,128)(2,1)S(1)}, u32[]{:S(2)}, u32[]{:S(2)}) collective-permute-start(bf16[48,2048]{1,0:T(8,128)(2,1)S(1)} %slice.36), channel_id=1, source_target_pairs={{0,4},{4,8},{8,12},{12,0},{1,5},{5,9},{9,13},{13,1},{2,6},{6,10},{... | collective-permute-start | bytes 589832 | tf_op jit(solution)/shard_map/ppermute | solution.py:220
  145.7 17.4 %collective-permute-start.16 = (bf16[3,256,256]{2,1,0:T(8,128)(2,1)S(1)}, bf16[3,256,256]{2,1,0:T(8,128)(2,1)S(1)}, u32[]{:S(2)}, u32[]{:S(2)}) collective-permute-start(bf16[3,256,256]{2,1,0:T(8,128)(2,1)S(1)} %project.29), channel_id=1, source_target_pairs={{0,2},{2,0},{1,3},{3,1},{4,6},{6,4},{5,7},{7,5},{8,10},{10,8},{9,1... | collective-permute-start | bytes 1179656 | tf_op jit(solution)/shard_map/ppermute | solution.py:223
  153.2 3.7 %collective-permute-start.28 = (bf16[48,2048]{1,0:T(8,128)(2,1)S(1)}, bf16[48,2048]{1,0:T(8,128)(2,1)S(1)}, u32[]{:S(2)}, u32[]{:S(2)}) collective-permute-start(bf16[48,2048]{1,0:T(8,128)(2,1)S(1)} %collective-permute-done.17.refs_0_), channel_id=1, source_target_pairs={{1,0},{0,1},{3,2},{2,3},{5,4},{4,5},{7,6},{6,7},{9,8},{8,9},{11,10... | collective-permute-start | bytes 589832 | tf_op jit(solution)/shard_map/ppermute | solution.py:227
  155.3 17.5 %collective-permute-start.25 = (bf16[3,208,256]{2,1,0:T(8,128)(2,1)S(1)}, bf16[3,208,256]{2,1,0:T(8,128)(2,1)S(1)}, u32[]{:S(2)}, u32[]{:S(2)}) collective-permute-start(bf16[3,208,256]{2,1,0:T(8,128)(2,1)S(1)} %project.33), channel_id=1, source_target_pairs={{0,2},{2,0},{1,3},{3,1},{4,6},{6,4},{5,7},{7,5},{8,10},{10,8},{9,1... | collective-permute-start | bytes 958472 | tf_op jit(solution)/shard_map/ppermute | solution.py:223
  158.7 18.5 %collective-permute-start.29 = (bf16[3,48,256]{2,1,0:T(8,128)(2,1)S(1)}, bf16[3,48,256]{2,1,0:T(8,128)(2,1)S(1)}, u32[]{:S(2)}, u32[]{:S(2)}) collective-permute-start(bf16[3,48,256]{2,1,0:T(8,128)(2,1)S(1)} %project.35), channel_id=1, source_target_pairs={{0,2},{2,0},{1,3},{3,1},{4,6},{6,4},{5,7},{7,5},{8,10},{10,8},{9,1... | collective-permute-start | bytes 221192 | tf_op jit(solution)/shard_map/ppermute | solution.py:223
  166.9 14.0 %collective-permute-start.22 = (bf16[512,256]{1,0:T(8,128)(2,1)S(1)}, bf16[512,256]{1,0:T(8,128)(2,1)S(1)}, u32[]{:S(2)}, u32[]{:S(2)}) collective-permute-start(bf16[512,256]{1,0:T(8,128)(2,1)S(1)} %get-tuple-element.69), channel_id=1, source_target_pairs={{0,0},{2,8},{4,4},{6,12},{8,2},{10,10},{12,6},{14,14},{1,1},{3,9},... | collective-permute-start | bytes 786440 | tf_op jit(solution)/shard_map/ppermute | solution.py:376
  167.6 13.9 %collective-permute-start.23 = (bf16[512,256]{1,0:T(8,128)(2,1)S(1)}, bf16[512,256]{1,0:T(8,128)(2,1)S(1)}, u32[]{:S(2)}, u32[]{:S(2)}) collective-permute-start(bf16[512,256]{1,0:T(8,128)(2,1)S(1)} %get-tuple-element.68), channel_id=1, source_target_pairs={{0,8},{2,0},{4,12},{6,4},{8,10},{10,2},{12,14},{14,6},{1,9},{3,1},... | collective-permute-start | bytes 786440 | tf_op jit(solution)/shard_map/ppermute | solution.py:376
  175.1 18.3 %collective-permute-start.26 = (bf16[320,256]{1,0:T(8,128)(2,1)S(1)}, bf16[320,256]{1,0:T(8,128)(2,1)S(1)}, u32[]{:S(2)}, u32[]{:S(2)}) collective-permute-start(bf16[320,256]{1,0:T(8,128)(2,1)S(1)} %get-tuple-element.73), channel_id=1, source_target_pairs={{0,12},{2,4},{4,0},{6,8},{8,14},{10,6},{12,2},{14,10},{1,13},{3,5}... | collective-permute-start | bytes 491528 | tf_op jit(solution)/shard_map/ppermute | solution.py:376
  175.6 17.8 %collective-permute-start.27 = (bf16[320,256]{1,0:T(8,128)(2,1)S(1)}, bf16[320,256]{1,0:T(8,128)(2,1)S(1)}, u32[]{:S(2)}, u32[]{:S(2)}) collective-permute-start(bf16[320,256]{1,0:T(8,128)(2,1)S(1)} %get-tuple-element.72), channel_id=1, source_target_pairs={{0,4},{2,12},{4,8},{6,0},{8,6},{10,14},{12,10},{14,2},{1,5},{3,13}... | collective-permute-start | bytes 491528 | tf_op jit(solution)/shard_map/ppermute | solution.py:376
  179.0 14.4 %collective-permute-start.30 = (bf16[192,256]{1,0:T(8,128)(2,1)S(1)}, bf16[192,256]{1,0:T(8,128)(2,1)S(1)}, u32[]{:S(2)}, u32[]{:S(2)}) collective-permute-start(bf16[192,256]{1,0:T(8,128)(2,1)S(1)} %get-tuple-element.75), channel_id=1, source_target_pairs={{0,12},{2,4},{4,0},{6,8},{8,14},{10,6},{12,2},{14,10},{1,13},{3,5}... | collective-permute-start | bytes 294920 | tf_op jit(solution)/shard_map/ppermute | solution.py:376
  180.9 12.4 %collective-permute-start.31 = (bf16[192,256]{1,0:T(8,128)(2,1)S(1)}, bf16[192,256]{1,0:T(8,128)(2,1)S(1)}, u32[]{:S(2)}, u32[]{:S(2)}) collective-permute-start(bf16[192,256]{1,0:T(8,128)(2,1)S(1)} %get-tuple-element.74), channel_id=1, source_target_pairs={{0,4},{2,12},{4,8},{6,0},{8,6},{10,14},{12,10},{14,2},{1,5},{3,13}... | collective-permute-start | bytes 294920 | tf_op jit(solution)/shard_map/ppermute | solution.py:376
  (12 other events, 130.5 us)

commit v3 on v2

--- a/solution.py
+++ b/solution.py
@@ -85,6 +85,27 @@
         cost_estimate=pl.CostEstimate(flops=1 << 20, bytes_accessed=1 << 16, transcendentals=0),
         name="project",
     )(places, *parts, pltpu.with_memory_space_constraint(weight, pltpu.VMEM))
+
+
+def row_power(tokens):
+    rows, features = tokens.shape
+    tile = 128
+
+    def body(block, out):
+        values = block[...].astype(F32)
+        total = jnp.sum(values * values, axis=1, keepdims=True)
+        out[...] = jnp.broadcast_to(total, (tile, tile)).T[:EXTRA]
+
+    return pl.pallas_call(
+        body,
+        out_shape=jax.ShapeDtypeStruct((EXTRA, rows), F32),
+        grid=(rows // tile,),
+        in_specs=[pl.BlockSpec((tile, features), lambda i: (i, 0))],
+        out_specs=pl.BlockSpec((EXTRA, tile), lambda i: (0, i)),
+        compiler_params=pltpu.CompilerParams(vmem_limit_bytes=12 << 20),
+        cost_estimate=pl.CostEstimate(flops=1 << 20, bytes_accessed=1 << 16, transcendentals=0),
+        name="power",
+    )(tokens)
 
 
 def filter_kernel(plan, terms, rows, flag, places, *refs):
@@ -212,8 +233,10 @@
     )
 
     def scaled_part(source, first, count, offset):
-        block = lax.dynamic_slice(source, (first, starts[offset]), (count, depth)).astype(F32)
-        gain = lax.dynamic_slice(norm_gain, (starts[offset],), (depth,))
+        block = lax.dynamic_slice(
+            source, (jnp.int32(first), starts[offset]), (count, depth), allow_negative_indices=False
+        ).astype(F32)
+        gain = lax.dynamic_slice(norm_gain, (starts[offset],), (depth,), allow_negative_indices=False)
         return (block * gain[None, :]).astype(BF16)
 
     ring = [(i, (i + 1) % steps) for i in range(steps)]
@@ -243,10 +266,28 @@
 
     halves = [(mid, rows - mid), (0, mid)]
     last = [(mid, rows - mid), (small, mid - small), (0, small)]
+    table, done, held = {}, {}, {}
+    received, ready = [], set()
+    waiting = []
+
+    def multiply(key, parts, count):
+        local, table[key] = partials(parts, count)
+        held["local", key] = local
+        received.append(key)
+        return local
+
     first, count = halves[0]
     upper = scaled_part(tokens, first, count, 0)
     source, upper = lax.optimization_barrier((tokens, upper))
-    power = jnp.sum(source.astype(F32) ** 2, axis=1)
+    own = [scaled_part(source, first, count, o) for o in range(1, cores)]
+    first, count = halves[1]
+    lowers = [scaled_part(source, first, count, o) for o in range(cores)]
+    own, lowers = lax.optimization_barrier((own, lowers))
+    first, count = halves[0]
+    local = multiply((0, first), [upper] + own, count)
+    source, short_taps, long_taps, _ = lax.optimization_barrier((source, short_taps, long_taps, local[1:]))
+
+    power = row_power(source)
     whole_power = power
     for w in range(1, across):
         whole_power = whole_power + sideways(power, w)
@@ -254,13 +295,16 @@
     terms = [lax.reduce_precision(scale, 8, 7)]
     terms.append(lax.reduce_precision(scale - terms[0], 8, 7))
     terms.append(scale - terms[0] - terms[1])
-    extra = jnp.pad(jnp.stack(terms), ((0, EXTRA - 3), (0, depth - rows))).astype(BF16)
+    line = lax.broadcasted_iota(jnp.int32, scale.shape, 0)
+    extra = jnp.where(line == 0, terms[0], jnp.where(line == 1, terms[1], jnp.where(line == 2, terms[2], 0.0)))
+    extra = jnp.pad(extra.astype(BF16), ((0, 0), (0, depth - rows)))
     first, count = halves[1]
-    lower = jnp.concatenate([scaled_part(source, first, count, 0), extra], axis=0)
+    lower = jnp.concatenate([lowers[0], extra], axis=0)
     scales = [extra[:, :rows]]
+    waiting.append(((0, first), [lower] + lowers[1:], count))
 
     def taps_of(taps):
-        cut = lambda w: lax.dynamic_slice_in_dim(taps, tap_first[w], kept, taps.ndim - 1)
+        cut = lambda w: lax.dynamic_slice_in_dim(taps, tap_first[w], kept, taps.ndim - 1, allow_negative_indices=False)
         result = cut(0)
         for w in range(1, across):
             other = sideways(cut(w), w)
@@ -289,18 +333,10 @@
         plan = (before, (0, mid, 0, 0, False), (0, tail, 0, mid, False))
         return unit(step, plan, [table[step + 1, mid], table[step, 0], table[step, mid]], rows)
 
-    table, done = {}, {}
-    received, ready = [], set()
-    held = {"filters": (short, spectra)}
-    waiting = []
-
-    def multiply(key, parts, count):
-        local, table[key] = partials(parts, count)
-        held["local", key] = local
-        received.append(key)
-
-    def arrived(block):
-        coming = [key for key in received[:-1] if key not in ready]
+    held["filters", 0] = (short, spectra)
+
+    def arrived(block, final=False):
+        coming = [key for key in (received if final else received[:-1]) if key not in ready]
         names = list(held)
         pack = (block, [held[n] for n in names], [table[key] for key in coming])
         block, kept_back, blocks = lax.optimization_barrier(pack)
@@ -319,10 +355,6 @@
                 done[step] = whole_unit(step)
                 held["unit", step] = done[step]
 
-    for (first, count), block in zip(halves, [upper, lower]):
-        own = [block] + [scaled_part(source, first, count, o) for o in range(1, cores)]
-        multiply((0, first), own, count)
-
     moving = [upper, lower]
     for step in range(1, steps):
         if step < steps - 1:
@@ -333,18 +365,24 @@
             upper, lower = moving
             moving = [forward(upper), forward(lower[small:]), forward(lower[:small])]
         for i, (first, count) in enumerate(spans):
-            moving[i] = arrived(moving[i])
+            moving[i] = arrived(moving[i], step == steps - 1 and i <= 1)
             if i == 1:
                 scales.append(moving[1][-EXTRA:, :rows])
+            if step == 1 and i == 0:
+                (key, parts, number), = waiting
+                moving[i], parts = lax.optimization_barrier((moving[i], parts))
+                waiting = [(key, parts, number)]
             waiting.append(((step, first), all_parts(moving[i]), count))
             if len(waiting) > 1:
                 multiply(*waiting.pop(0))
             filter_ready()
-    while waiting:
-        multiply(*waiting.pop(0))
+    crossing = [[sideways(partial(parts, count, w), w) for w in range(1, across)] for _, parts, count in waiting]
     for step in range(steps - 1):
         if step not in done:
             done[step] = whole_unit(step)
+    blocks, done = lax.optimization_barrier(([parts for _, parts, _ in waiting], done))
+    for (key, _, count), parts, terms in zip(waiting, blocks, crossing):
+        table[key] = [partial(parts, count, 0)] + terms
     step = steps - 1
     early = unit(
         step,

time: 198 us -> 192 us (0.970); the launches traced: 195 us -> 191 us
  waiting for transfers between devices: 84.9 us -> 82.1 us
    ppermute x7, waiting for transfers between devices: 67.5 us -> 61.9 us  [shards(): forward = lambda block: lax.ppermute(block, 'ctx', ring)]
    ppermute x12, waiting for transfers between devices: 5.49 us -> 9.09 us  [sideways(): lax.ppermute(block, 'width', [(i, (i + w) % across) for i in range(across)])]
    reduce_sum x1 -> x0, other arithmetic: 3.38 us -> none  [shards(): power = jnp.sum(source.astype(F32) ** 2, axis=1)]
  transfers between devices with their start and end apart: 32 -> 32, of which waited for: 9 -> 11; matrix products, arithmetic and copies ran while one was open for 3% -> 3% of each run, Pallas kernels for 32% -> 33%
where the time goes in v3:
time: 192 us; the launch traced here: 191 us
  waiting for transfers between devices  82.1 us (43%)
  Pallas kernels  64.4 us (34%)
  starting transfers between devices  31.3 us (16%)
  local copies, waits for them, and re-layouts  6.4 us (3%)
  other arithmetic  6.06 us (3%)
    ppermute x7, waiting for transfers between devices, shards(): forward = lambda block: lax.ppermute(block, 'ctx', ring)  61.9 us
    pallas_call x18, Pallas kernels, project(): pl.pallas_call(body, out_shape=jax.ShapeDtypeStruct((streams, rows, kept)...  46.3 us
    ppermute x12, starting transfers between devices, sideways(): lax.ppermute(block, 'width', [(i, (i + w) % across) for i in range(across)])  16.2 us
    pallas_call x5, Pallas kernels, filter_rows(): pl.pallas_call(functools.partial(filter_kernel, plan, terms, rows, flag),...  15.4 us
    ppermute x6, waiting for transfers between devices, returned(): return lax.ppermute(block, ('ctx', 'width'), pairs)  11.1 us
    ppermute x6, starting transfers between devices, returned(): return lax.ppermute(block, ('ctx', 'width'), pairs)  9.96 us
    ppermute x12, waiting for transfers between devices, sideways(): lax.ppermute(block, 'width', [(i, (i + w) % across) for i in range(across)])  9.09 us
    convert_element_type x2, other arithmetic, scaled_part(): return (block * gain[None, :]).astype(BF16)  5.57 us
  transfers between devices with their start and end apart: 32, of which 11 were waited for; matrix products, arithmetic and copies ran while one was open for 3% of the time, Pallas kernels for 33%

profile of v3, /device:TPU:0, one launch (start us, length us, event | category | flops | bytes accessed | tf_op | source)
XLA Modules:
  0.0 191.3 jit_solution(12595721428575570616)
XLA Ops:
  3.0 3.1 %collective-permute-start.2 = (bf16[256,2048]{1,0:T(8,128)(2,1)S(1)}, bf16[256,2048]{1,0:T(8,128)(2,1)S(1)}, u32[]{:S(2)}, u32[]{:S(2)}) collective-permute-start(bf16[256,2048]{1,0:T(8,128)(2,1)S(1)} %multiply_convert_fusion.3.refs_0_), channel_id=1, source_target_pairs={{0,4},{4,8},{8,12},{12,0},{1,5},{5,9},{9,13},{13,1},{2,6},{6,10},{... | collective-permute-start | bytes 3145736 | tf_op jit(solution)/shard_map/ppermute | solution.py:243
  6.0 3.6 %multiply_convert_fusion = (bf16[256,2048]{1,0:T(8,128)(2,1)S(1)}, bf16[256,2048]{1,0:T(8,128)(2,1)S(1)}, bf16[256,2048]{1,0:T(8,128)(2,1)S(1)}) fusion(bf16[512,4096]{1,0:T(8,128)(2,1)} %block, s32[]{:T(128)S(6)} %mul.75, f32[2048]{0:T(1024)S(1)} %get-tuple-element.111, f32[2048]{0:T(1024)S(1)} %get-tuple-element.112, s32[]{:T(128)S(6)} %mul.74), kind=kLoop, calls=%fused_computation.2 | loop fusion | flops 4718592 | bytes 6307848 | tf_op jit(solution)/shard_map/convert_element_type | solution.py:240
  9.7 4.6 %copy-done = bf16[3,4096,1,512]{3,1,2,0:T(8,128)(2,1)S(1)} copy-done((bf16[3,4096,1,512]{3,1,2,0:T(8,128)(2,1)S(1)}, bf16[3,4096,1,512]{3,1,2,0:T(8,128)(2,1)}, u32[]{:S(2)}) %copy-start) | copy-done | bytes 12582936
  14.3 2.8 %project.18 = bf16[3,256,256]{2,1,0:T(8,128)(2,1)S(1)} custom-call(s32[7]{0:T(128)S(1)} %stack.46.places, bf16[256,2048]{1,0:T(8,128)(2,1)S(1)} %multiply_convert_fusion.3.refs_0_, bf16[256,2048]{1,0:T(8,128)(2,1)S(1)} %get-tuple-element.59.refs_1_, bf16[3,4096,512]{2,1,0:T(8,128)(2,1)S(1)} %bitcast.25), custom_call_target="tpu_custom_call" | custom-call | flops 1048576 | bytes 65536 | tf_op jit(solution)/shard_map/project/pallas_call | solution.py:79
  22.8 2.7 %project.19.refs_4_.refs_0_ = bf16[3,256,256]{2,1,0:T(8,128)(2,1)S(1)} custom-call(s32[7]{0:T(128)S(1)} %stack.46.places, bf16[256,2048]{1,0:T(8,128)(2,1)S(1)} %multiply_convert_fusion.3.refs_0_, bf16[256,2048]{1,0:T(8,128)(2,1)S(1)} %get-tuple-element.59.refs_1_, bf16[3,4096,512]{2,1,0:T(8,128)(2,1)S(1)} %bitcast.28), custom_call_target="tpu_custom_call" | custom-call | flops 1048576 | bytes 65536 | tf_op jit(solution)/shard_map/project/pallas_call | solution.py:79
  27.9 4.2 %collective-permute-done.2.refs_0_ = bf16[256,2048]{1,0:T(8,128)(2,1)S(1)} collective-permute-done((bf16[256,2048]{1,0:T(8,128)(2,1)S(1)}, bf16[256,2048]{1,0:T(8,128)(2,1)S(1)}, u32[]{:S(2)}, u32[]{:S(2)}) %collective-permute-start.2) | collective-permute-done | bytes 1048608 | tf_op jit(solution)/shard_map/ppermute | solution.py:243
  33.8 2.8 %project.21 = bf16[3,256,256]{2,1,0:T(8,128)(2,1)S(1)} custom-call(s32[7]{0:T(128)S(1)} %stack.46.places, bf16[264,2048]{1,0:T(8,128)(2,1)S(1)} %fusion.1.refs_0_, bf16[256,2048]{1,0:T(8,128)(2,1)S(1)} %get-tuple-element.68.refs_1_, bf16[3,4096,512]{2,1,0:T(8,128)(2,1)S(1)} %bitcast.29), custom_call_target="tpu_custom_call" | custom-call | flops 1048576 | bytes 65536 | tf_op jit(solution)/shard_map/project/pallas_call | solution.py:79
  36.6 2.7 %project.20.refs_2_ = bf16[3,256,256]{2,1,0:T(8,128)(2,1)S(1)} custom-call(s32[7]{0:T(128)S(1)} %stack.46.places, bf16[264,2048]{1,0:T(8,128)(2,1)S(1)} %fusion.1.refs_0_, bf16[256,2048]{1,0:T(8,128)(2,1)S(1)} %get-tuple-element.68.refs_1_, bf16[3,4096,512]{2,1,0:T(8,128)(2,1)S(1)} %bitcast.30), custom_call_target="tpu_custom_call" | custom-call | flops 1048576 | bytes 65536 | tf_op jit(solution)/shard_map/project/pallas_call | solution.py:79
  39.3 4.3 %collective-permute-done.5.refs_5_.refs_1_ = bf16[3,256,256]{2,1,0:T(8,128)(2,1)S(1)} collective-permute-done((bf16[3,256,256]{2,1,0:T(8,128)(2,1)S(1)}, bf16[3,256,256]{2,1,0:T(8,128)(2,1)S(1)}, u32[]{:S(2)}, u32[]{:S(2)}) %collective-permute-start.5) | collective-permute-done | bytes 393248 | tf_op jit(solution)/shard_map/ppermute | solution.py:246
  43.6 11.6 %collective-permute-done.1.refs_0_ = bf16[264,2048]{1,0:T(8,128)(2,1)S(1)} collective-permute-done((bf16[264,2048]{1,0:T(8,128)(2,1)S(1)}, bf16[264,2048]{1,0:T(8,128)(2,1)S(1)}, u32[]{:S(2)}, u32[]{:S(2)}) %collective-permute-start.1) | collective-permute-done | bytes 1081376 | tf_op jit(solution)/shard_map/ppermute | solution.py:243
  57.0 2.8 %project.25 = bf16[3,256,256]{2,1,0:T(8,128)(2,1)S(1)} custom-call(s32[7]{0:T(128)S(1)} %stack.46.places, bf16[256,2048]{1,0:T(8,128)(2,1)S(1)} %collective-permute-done.2.refs_0_, bf16[256,2048]{1,0:T(8,128)(2,1)S(1)} %collective-permute-done.8.refs_1_, bf16[3,4096,512]{2,1,0:T(8,128)(2,1)S(1)} %bitcast.31), custom_call_target="tpu_custom_call" | custom-call | flops 1048576 | bytes 65536 | tf_op jit(solution)/shard_map/project/pallas_call | solution.py:79
  59.8 2.8 %project.24.refs_0_.refs_4_ = bf16[3,256,256]{2,1,0:T(8,128)(2,1)S(1)} custom-call(s32[7]{0:T(128)S(1)} %stack.46.places, bf16[256,2048]{1,0:T(8,128)(2,1)S(1)} %collective-permute-done.2.refs_0_, bf16[256,2048]{1,0:T(8,128)(2,1)S(1)} %collective-permute-done.8.refs_1_, bf16[3,4096,512]{2,1,0:T(8,128)(2,1)S(1)} %bitcast.32), custom_call_target="tpu_custom_call" | custom-call | flops 1048576 | bytes 65536 | tf_op jit(solution)/shard_map/project/pallas_call | solution.py:79
  62.6 4.2 %collective-permute-done.12.refs_3_ = bf16[3,256,256]{2,1,0:T(8,128)(2,1)S(1)} collective-permute-done((bf16[3,256,256]{2,1,0:T(8,128)(2,1)S(1)}, bf16[3,256,256]{2,1,0:T(8,128)(2,1)S(1)}, u32[]{:S(2)}, u32[]{:S(2)}) %collective-permute-start.12) | collective-permute-done | bytes 393248 | tf_op jit(solution)/shard_map/ppermute | solution.py:246
  66.8 10.9 %collective-permute-done.11.refs_0_ = bf16[256,2048]{1,0:T(8,128)(2,1)S(1)} collective-permute-done((bf16[256,2048]{1,0:T(8,128)(2,1)S(1)}, bf16[256,2048]{1,0:T(8,128)(2,1)S(1)}, u32[]{:S(2)}, u32[]{:S(2)}) %collective-permute-start.11) | collective-permute-done | bytes 1048608 | tf_op jit(solution)/shard_map/ppermute | solution.py:243
  79.5 2.8 %project.23 = bf16[3,256,256]{2,1,0:T(8,128)(2,1)S(1)} custom-call(s32[7]{0:T(128)S(1)} %stack.46.places, bf16[264,2048]{1,0:T(8,128)(2,1)S(1)} %collective-permute-done.1.refs_0_, bf16[264,2048]{1,0:T(8,128)(2,1)S(1)} %collective-permute-done.7.refs_1_, bf16[3,4096,512]{2,1,0:T(8,128)(2,1)S(1)} %bitcast.33), custom_call_target="tpu_custom_call" | custom-call | flops 1048576 | bytes 65536 | tf_op jit(solution)/shard_map/project/pallas_call | solution.py:79
  82.3 2.7 %project.22.refs_2_ = bf16[3,256,256]{2,1,0:T(8,128)(2,1)S(1)} custom-call(s32[7]{0:T(128)S(1)} %stack.46.places, bf16[264,2048]{1,0:T(8,128)(2,1)S(1)} %collective-permute-done.1.refs_0_, bf16[264,2048]{1,0:T(8,128)(2,1)S(1)} %collective-permute-done.7.refs_1_, bf16[3,4096,512]{2,1,0:T(8,128)(2,1)S(1)} %bitcast.34), custom_call_target="tpu_custom_call" | custom-call | flops 1048576 | bytes 65536 | tf_op jit(solution)/shard_map/project/pallas_call | solution.py:79
  85.0 15.9 %collective-permute-done.6.refs_0_ = bf16[264,2048]{1,0:T(8,128)(2,1)S(1)} collective-permute-done((bf16[264,2048]{1,0:T(8,128)(2,1)S(1)}, bf16[264,2048]{1,0:T(8,128)(2,1)S(1)}, u32[]{:S(2)}, u32[]{:S(2)}) %collective-permute-start.6) | collective-permute-done | bytes 1081376 | tf_op jit(solution)/shard_map/ppermute | solution.py:243
  103.1 2.8 %project.26 = bf16[3,256,256]{2,1,0:T(8,128)(2,1)S(1)} custom-call(s32[7]{0:T(128)S(1)} %stack.46.places, bf16[256,2048]{1,0:T(8,128)(2,1)S(1)} %collective-permute-done.11.refs_0_, bf16[256,2048]{1,0:T(8,128)(2,1)S(1)} %collective-permute-done.14.refs_1_, bf16[3,4096,512]{2,1,0:T(8,128)(2,1)S(1)} %bitcast.35), custom_call_target="tpu_custom_call" | custom-call | flops 1048576 | bytes 65536 | tf_op jit(solution)/shard_map/project/pallas_call | solution.py:79
  106.2 3.8 %filter.5 = bf16[512,256]{1,0:T(8,128)(2,1)S(1)} custom-call(s32[7]{0:T(128)S(1)} %stack.46.places, bf16[3,256,256]{2,1,0:T(8,128)(2,1)S(1)} %project.24.refs_0_.refs_4_, bf16[3,256,256]{2,1,0:T(8,128)(2,1)S(1)} %collective-permute-done.9.refs_1_.refs_5_, bf16[3,256,256]{2,1,0:T(8,128)(2,1)S(1)} %project.20.refs_2_, ...), custom_call_target="tpu_custom_call" | custom-call | flops 1048576 | bytes 65536 | tf_op jit(solution)/shard_map/filter/pallas_call | solution.py:187
  109.9 2.7 %project.27.refs_0_.refs_4_ = bf16[3,256,256]{2,1,0:T(8,128)(2,1)S(1)} custom-call(s32[7]{0:T(128)S(1)} %stack.46.places, bf16[256,2048]{1,0:T(8,128)(2,1)S(1)} %collective-permute-done.11.refs_0_, bf16[256,2048]{1,0:T(8,128)(2,1)S(1)} %collective-permute-done.14.refs_1_, bf16[3,4096,512]{2,1,0:T(8,128)(2,1)S(1)} %bitcast.36), custom_call_target="tpu_custom_call" | custom-call | flops 1048576 | bytes 65536 | tf_op jit(solution)/shard_map/project/pallas_call | solution.py:79
  113.2 10.1 %collective-permute-done.13.refs_0_ = bf16[256,2048]{1,0:T(8,128)(2,1)S(1)} collective-permute-done((bf16[256,2048]{1,0:T(8,128)(2,1)S(1)}, bf16[256,2048]{1,0:T(8,128)(2,1)S(1)}, u32[]{:S(2)}, u32[]{:S(2)}) %collective-permute-start.13) | collective-permute-done | bytes 1048608 | tf_op jit(solution)/shard_map/ppermute | solution.py:243
  123.4 2.8 %project.30 = bf16[3,256,256]{2,1,0:T(8,128)(2,1)S(1)} custom-call(s32[7]{0:T(128)S(1)} %stack.46.places, bf16[264,2048]{1,0:T(8,128)(2,1)S(1)} %collective-permute-done.6.refs_0_, bf16[264,2048]{1,0:T(8,128)(2,1)S(1)} %collective-permute-done.20.refs_1_, bf16[3,4096,512]{2,1,0:T(8,128)(2,1)S(1)} %bitcast.37), custom_call_target="tpu_custom_call" | custom-call | flops 1048576 | bytes 65536 | tf_op jit(solution)/shard_map/project/pallas_call | solution.py:79
  127.9 3.8 %filter.6 = bf16[512,256]{1,0:T(8,128)(2,1)S(1)} custom-call(s32[7]{0:T(128)S(1)} %stack.46.places, bf16[3,256,256]{2,1,0:T(8,128)(2,1)S(1)} %project.27.refs_0_.refs_4_, bf16[3,256,256]{2,1,0:T(8,128)(2,1)S(1)} %collective-permute-done.16.refs_1_.refs_5_, bf16[3,256,256]{2,1,0:T(8,128)(2,1)S(1)} %project.22.refs_2_, ...), custom_call_target="tpu_custom_call" | custom-call | flops 1048576 | bytes 65536 | tf_op jit(solution)/shard_map/filter/pallas_call | solution.py:187
  131.7 2.8 %project.31.refs_2_ = bf16[3,256,256]{2,1,0:T(8,128)(2,1)S(1)} custom-call(s32[7]{0:T(128)S(1)} %stack.46.places, bf16[264,2048]{1,0:T(8,128)(2,1)S(1)} %collective-permute-done.6.refs_0_, bf16[264,2048]{1,0:T(8,128)(2,1)S(1)} %collective-permute-done.20.refs_1_, bf16[3,4096,512]{2,1,0:T(8,128)(2,1)S(1)} %bitcast.38), custom_call_target="tpu_custom_call" | custom-call | flops 1048576 | bytes 65536 | tf_op jit(solution)/shard_map/project/pallas_call | solution.py:79
  134.5 7.0 %collective-permute-done.19.refs_0_ = bf16[216,2048]{1,0:T(8,128)(2,1)S(1)} collective-permute-done((bf16[216,2048]{1,0:T(8,128)(2,1)S(1)}, bf16[216,2048]{1,0:T(8,128)(2,1)S(1)}, u32[]{:S(2)}, u32[]{:S(2)}) %collective-permute-start.19) | collective-permute-done | bytes 884768 | tf_op jit(solution)/shard_map/ppermute | solution.py:243
  141.5 2.8 %project.29 = bf16[3,256,256]{2,1,0:T(8,128)(2,1)S(1)} custom-call(s32[7]{0:T(128)S(1)} %stack.46.places, bf16[256,2048]{1,0:T(8,128)(2,1)S(1)} %collective-permute-done.13.refs_0_, bf16[256,2048]{1,0:T(8,128)(2,1)S(1)} %collective-permute-done.17.refs_1_, bf16[3,4096,512]{2,1,0:T(8,128)(2,1)S(1)} %bitcast.39), custom_call_target="tpu_custom_call" | custom-call | flops 1048576 | bytes 65536 | tf_op jit(solution)/shard_map/project/pallas_call | solution.py:79
  145.8 2.7 %project.28.refs_0_.refs_2_ = bf16[3,256,256]{2,1,0:T(8,128)(2,1)S(1)} custom-call(s32[7]{0:T(128)S(1)} %stack.46.places, bf16[256,2048]{1,0:T(8,128)(2,1)S(1)} %collective-permute-done.13.refs_0_, bf16[256,2048]{1,0:T(8,128)(2,1)S(1)} %collective-permute-done.17.refs_1_, bf16[3,4096,512]{2,1,0:T(8,128)(2,1)S(1)} %bitcast.40), custom_call_target="tpu_custom_call" | custom-call | flops 1048576 | bytes 65536 | tf_op jit(solution)/shard_map/project/pallas_call | solution.py:79
  150.6 2.1 %project.33 = bf16[3,208,256]{2,1,0:T(8,128)(2,1)S(1)} custom-call(s32[7]{0:T(128)S(1)} %stack.46.places, bf16[216,2048]{1,0:T(8,128)(2,1)S(1)} %collective-permute-done.19.refs_0_, bf16[216,2048]{1,0:T(8,128)(2,1)S(1)} %collective-permute-done.25.refs_1_, bf16[3,4096,512]{2,1,0:T(8,128)(2,1)S(1)} %bitcast.41), custom_call_target="tpu_custom_call" | custom-call | flops 1048576 | bytes 65536 | tf_op jit(solution)/shard_map/project/pallas_call | solution.py:79
  158.8 3.8 %filter.7 = bf16[512,256]{1,0:T(8,128)(2,1)S(1)} custom-call(s32[7]{0:T(128)S(1)} %stack.46.places, bf16[3,256,256]{2,1,0:T(8,128)(2,1)S(1)} %project.28.refs_0_.refs_2_, bf16[3,256,256]{2,1,0:T(8,128)(2,1)S(1)} %collective-permute-done.22.refs_1_.refs_3_, bf16[3,256,256]{2,1,0:T(8,128)(2,1)S(1)} %project.31.refs_2_, ...), custom_call_target="tpu_custom_call" | custom-call | flops 1048576 | bytes 65536 | tf_op jit(solution)/shard_map/filter/pallas_call | solution.py:187
  163.3 5.1 %collective-permute-start.24 = (bf16[512,256]{1,0:T(8,128)(2,1)S(1)}, bf16[512,256]{1,0:T(8,128)(2,1)S(1)}, u32[]{:S(2)}, u32[]{:S(2)}) collective-permute-start(bf16[512,256]{1,0:T(8,128)(2,1)S(1)} %get-tuple-element.98), channel_id=1, source_target_pairs={{0,8},{2,0},{4,12},{6,4},{8,10},{10,2},{12,14},{14,6},{1,9},{3,1},... | collective-permute-start | bytes 786440 | tf_op jit(solution)/shard_map/ppermute | solution.py:414
  170.2 2.2 %filter.8 = bf16[320,256]{1,0:T(8,128)(2,1)S(1)} custom-call(s32[7]{0:T(128)S(1)} %stack.46.places, bf16[3,208,256]{2,1,0:T(8,128)(2,1)S(1)} %project.32.refs_0_.refs_4_, bf16[3,208,256]{2,1,0:T(8,128)(2,1)S(1)} %collective-permute-done.26.refs_1_.refs_5_, bf16[3,256,256]{2,1,0:T(8,128)(2,1)S(1)} %project.28.refs_0_.refs_2_, ...), custom_call_target="tpu_custom_call" | custom-call | flops 1048576 | bytes 65536 | tf_op jit(solution)/shard_map/filter/pallas_call | solution.py:187
  178.5 11.1 %collective-permute-done.30.refs_4_ = bf16[192,256]{1,0:T(8,128)(2,1)S(1)} collective-permute-done((bf16[192,256]{1,0:T(8,128)(2,1)S(1)}, bf16[192,256]{1,0:T(8,128)(2,1)S(1)}, u32[]{:S(2)}, u32[]{:S(2)}) %collective-permute-start.30) | collective-permute-done | bytes 98336 | tf_op jit(solution)/shard_map/ppermute | solution.py:414
  (107 shorter events, 40.6 us)
Async XLA Ops:
  3.0 29.1 %collective-permute-start.2 = (bf16[256,2048]{1,0:T(8,128)(2,1)S(1)}, bf16[256,2048]{1,0:T(8,128)(2,1)S(1)}, u32[]{:S(2)}, u32[]{:S(2)}) collective-permute-start(bf16[256,2048]{1,0:T(8,128)(2,1)S(1)} %multiply_convert_fusion.3.refs_0_), channel_id=1, source_target_pairs={{0,4},{4,8},{8,12},{12,0},{1,5},{5,9},{9,13},{13,1},{2,6},{6,10},{... | collective-permute-start | bytes 3145736 | tf_op jit(solution)/shard_map/ppermute | solution.py:243
  17.7 9.6 %collective-permute-start.4 = (f32[128,256]{1,0:T(8,128)S(1)}, f32[128,256]{1,0:T(8,128)S(1)}, u32[]{:S(2)}, u32[]{:S(2)}) collective-permute-start(f32[128,256]{1,0:T(8,128)S(1)} %bitcast.45), channel_id=1, source_target_pairs={{0,2},{2,0},{1,3},{3,1},{4,6},{6,4},{5,7},{7,5},{8,10},{10,8},{9,1... | collective-permute-start | bytes 393224 | tf_op jit(solution)/shard_map/ppermute | solution.py:246
  19.3 8.0 %collective-permute-start.3 = (f32[3,3,256]{2,1,0:T(4,128)S(1)}, f32[3,3,256]{2,1,0:T(4,128)S(1)}, u32[]{:S(2)}, u32[]{:S(2)}) collective-permute-start(f32[3,3,256]{2,1,0:T(4,128)S(1)} %bitcast.46), channel_id=1, source_target_pairs={{0,2},{2,0},{1,3},{3,1},{4,6},{6,4},{5,7},{7,5},{8,10},{10,8},{9,1... | collective-permute-start | bytes 27656 | tf_op jit(solution)/shard_map/ppermute | solution.py:246
  21.3 4.2 %collective-permute-start = (f32[8,512]{1,0:T(8,128)S(1)}, f32[8,512]{1,0:T(8,128)S(1)}, u32[]{:S(2)}, u32[]{:S(2)}) collective-permute-start(f32[8,512]{1,0:T(8,128)S(1)} %power.1), channel_id=1, source_target_pairs={{0,2},{2,0},{1,3},{3,1},{4,6},{6,4},{5,7},{7,5},{8,10},{10,8},{9,1... | collective-permute-start | bytes 49160 | tf_op jit(solution)/shard_map/ppermute | solution.py:246
  25.7 29.5 %collective-permute-start.1 = (bf16[264,2048]{1,0:T(8,128)(2,1)S(1)}, bf16[264,2048]{1,0:T(8,128)(2,1)S(1)}, u32[]{:S(2)}, u32[]{:S(2)}) collective-permute-start(bf16[264,2048]{1,0:T(8,128)(2,1)S(1)} %fusion.1.refs_0_), channel_id=1, source_target_pairs={{0,4},{4,8},{8,12},{12,0},{1,5},{5,9},{9,13},{13,1},{2,6},{6,10},{... | collective-permute-start | bytes 3244040 | tf_op jit(solution)/shard_map/ppermute | solution.py:243
  32.1 24.9 %collective-permute-start.8 = (bf16[256,2048]{1,0:T(8,128)(2,1)S(1)}, bf16[256,2048]{1,0:T(8,128)(2,1)S(1)}, u32[]{:S(2)}, u32[]{:S(2)}) collective-permute-start(bf16[256,2048]{1,0:T(8,128)(2,1)S(1)} %collective-permute-done.2.refs_0_), channel_id=1, source_target_pairs={{1,0},{0,1},{3,2},{2,3},{5,4},{4,5},{7,6},{6,7},{9,8},{8,9},{11,10... | collective-permute-start | bytes 3145736 | tf_op jit(solution)/shard_map/ppermute | solution.py:250
  32.1 45.6 %collective-permute-start.11 = (bf16[256,2048]{1,0:T(8,128)(2,1)S(1)}, bf16[256,2048]{1,0:T(8,128)(2,1)S(1)}, u32[]{:S(2)}, u32[]{:S(2)}) collective-permute-start(bf16[256,2048]{1,0:T(8,128)(2,1)S(1)} %collective-permute-done.2.refs_0_), channel_id=1, source_target_pairs={{0,4},{4,8},{8,12},{12,0},{1,5},{5,9},{9,13},{13,1},{2,6},{6,10},{... | collective-permute-start | bytes 3145736 | tf_op jit(solution)/shard_map/ppermute | solution.py:243
  32.1 11.5 %collective-permute-start.5 = (bf16[3,256,256]{2,1,0:T(8,128)(2,1)S(1)}, bf16[3,256,256]{2,1,0:T(8,128)(2,1)S(1)}, u32[]{:S(2)}, u32[]{:S(2)}) collective-permute-start(bf16[3,256,256]{2,1,0:T(8,128)(2,1)S(1)} %project.18), channel_id=1, source_target_pairs={{0,2},{2,0},{1,3},{3,1},{4,6},{6,4},{5,7},{7,5},{8,10},{10,8},{9,1... | collective-permute-start | bytes 1179656 | tf_op jit(solution)/shard_map/ppermute | solution.py:246
  55.2 24.2 %collective-permute-start.7 = (bf16[264,2048]{1,0:T(8,128)(2,1)S(1)}, bf16[264,2048]{1,0:T(8,128)(2,1)S(1)}, u32[]{:S(2)}, u32[]{:S(2)}) collective-permute-start(bf16[264,2048]{1,0:T(8,128)(2,1)S(1)} %collective-permute-done.1.refs_0_), channel_id=1, source_target_pairs={{1,0},{0,1},{3,2},{2,3},{5,4},{4,5},{7,6},{6,7},{9,8},{8,9},{11,10... | collective-permute-start | bytes 3244040 | tf_op jit(solution)/shard_map/ppermute | solution.py:250
  55.2 45.6 %collective-permute-start.6 = (bf16[264,2048]{1,0:T(8,128)(2,1)S(1)}, bf16[264,2048]{1,0:T(8,128)(2,1)S(1)}, u32[]{:S(2)}, u32[]{:S(2)}) collective-permute-start(bf16[264,2048]{1,0:T(8,128)(2,1)S(1)} %collective-permute-done.1.refs_0_), channel_id=1, source_target_pairs={{0,4},{4,8},{8,12},{12,0},{1,5},{5,9},{9,13},{13,1},{2,6},{6,10},{... | collective-permute-start | bytes 3244040 | tf_op jit(solution)/shard_map/ppermute | solution.py:243
  55.3 11.5 %collective-permute-start.12 = (bf16[3,256,256]{2,1,0:T(8,128)(2,1)S(1)}, bf16[3,256,256]{2,1,0:T(8,128)(2,1)S(1)}, u32[]{:S(2)}, u32[]{:S(2)}) collective-permute-start(bf16[3,256,256]{2,1,0:T(8,128)(2,1)S(1)} %project.21), channel_id=1, source_target_pairs={{0,2},{2,0},{1,3},{3,1},{4,6},{6,4},{5,7},{7,5},{8,10},{10,8},{9,1... | collective-permute-start | bytes 1179656 | tf_op jit(solution)/shard_map/ppermute | solution.py:246
  77.7 25.4 %collective-permute-start.14 = (bf16[256,2048]{1,0:T(8,128)(2,1)S(1)}, bf16[256,2048]{1,0:T(8,128)(2,1)S(1)}, u32[]{:S(2)}, u32[]{:S(2)}) collective-permute-start(bf16[256,2048]{1,0:T(8,128)(2,1)S(1)} %collective-permute-done.11.refs_0_), channel_id=1, source_target_pairs={{1,0},{0,1},{3,2},{2,3},{5,4},{4,5},{7,6},{6,7},{9,8},{8,9},{11,10... | collective-permute-start | bytes 3145736 | tf_op jit(solution)/shard_map/ppermute | solution.py:250
  77.7 23.2 %collective-permute-start.9 = (bf16[3,256,256]{2,1,0:T(8,128)(2,1)S(1)}, bf16[3,256,256]{2,1,0:T(8,128)(2,1)S(1)}, u32[]{:S(2)}, u32[]{:S(2)}) collective-permute-start(bf16[3,256,256]{2,1,0:T(8,128)(2,1)S(1)} %project.25), channel_id=1, source_target_pairs={{0,2},{2,0},{1,3},{3,1},{4,6},{6,4},{5,7},{7,5},{8,10},{10,8},{9,1... | collective-permute-start | bytes 1179656 | tf_op jit(solution)/shard_map/ppermute | solution.py:246
  79.4 43.9 %collective-permute-start.13 = (bf16[256,2048]{1,0:T(8,128)(2,1)S(1)}, bf16[256,2048]{1,0:T(8,128)(2,1)S(1)}, u32[]{:S(2)}, u32[]{:S(2)}) collective-permute-start(bf16[256,2048]{1,0:T(8,128)(2,1)S(1)} %collective-permute-done.11.refs_0_), channel_id=1, source_target_pairs={{0,4},{4,8},{8,12},{12,0},{1,5},{5,9},{9,13},{13,1},{2,6},{6,10},{... | collective-permute-start | bytes 3145736 | tf_op jit(solution)/shard_map/ppermute | solution.py:243
  100.9 22.5 %collective-permute-start.20 = (bf16[264,2048]{1,0:T(8,128)(2,1)S(1)}, bf16[264,2048]{1,0:T(8,128)(2,1)S(1)}, u32[]{:S(2)}, u32[]{:S(2)}) collective-permute-start(bf16[264,2048]{1,0:T(8,128)(2,1)S(1)} %collective-permute-done.6.refs_0_), channel_id=1, source_target_pairs={{1,0},{0,1},{3,2},{2,3},{5,4},{4,5},{7,6},{6,7},{9,8},{8,9},{11,10... | collective-permute-start | bytes 3244040 | tf_op jit(solution)/shard_map/ppermute | solution.py:250
  101.0 40.4 %collective-permute-start.19 = (bf16[216,2048]{1,0:T(8,128)(2,1)S(1)}, bf16[216,2048]{1,0:T(8,128)(2,1)S(1)}, u32[]{:S(2)}, u32[]{:S(2)}) collective-permute-start(bf16[216,2048]{1,0:T(8,128)(2,1)S(1)} %slice.34), channel_id=1, source_target_pairs={{0,4},{4,8},{8,12},{12,0},{1,5},{5,9},{9,13},{13,1},{2,6},{6,10},{... | collective-permute-start | bytes 2654216 | tf_op jit(solution)/shard_map/ppermute | solution.py:243
  101.3 12.0 %collective-permute-start.15 = (bf16[3,256,256]{2,1,0:T(8,128)(2,1)S(1)}, bf16[3,256,256]{2,1,0:T(8,128)(2,1)S(1)}, u32[]{:S(2)}, u32[]{:S(2)}) collective-permute-start(bf16[3,256,256]{2,1,0:T(8,128)(2,1)S(1)} %project.23), channel_id=1, source_target_pairs={{0,2},{2,0},{1,3},{3,1},{4,6},{6,4},{5,7},{7,5},{8,10},{10,8},{9,1... | collective-permute-start | bytes 1179656 | tf_op jit(solution)/shard_map/ppermute | solution.py:246
  105.9 17.5 %collective-permute-start.16 = (bf16[3,256,256]{2,1,0:T(8,128)(2,1)S(1)}, bf16[3,256,256]{2,1,0:T(8,128)(2,1)S(1)}, u32[]{:S(2)}, u32[]{:S(2)}) collective-permute-start(bf16[3,256,256]{2,1,0:T(8,128)(2,1)S(1)} %project.26), channel_id=1, source_target_pairs={{0,2},{2,0},{1,3},{3,1},{4,6},{6,4},{5,7},{7,5},{8,10},{10,8},{9,1... | collective-permute-start | bytes 1179656 | tf_op jit(solution)/shard_map/ppermute | solution.py:246
  123.4 18.2 %collective-permute-start.17 = (bf16[256,2048]{1,0:T(8,128)(2,1)S(1)}, bf16[256,2048]{1,0:T(8,128)(2,1)S(1)}, u32[]{:S(2)}, u32[]{:S(2)}) collective-permute-start(bf16[256,2048]{1,0:T(8,128)(2,1)S(1)} %collective-permute-done.13.refs_0_), channel_id=1, source_target_pairs={{1,0},{0,1},{3,2},{2,3},{5,4},{4,5},{7,6},{6,7},{9,8},{8,9},{11,10... | collective-permute-start | bytes 3145736 | tf_op jit(solution)/shard_map/ppermute | solution.py:250
  126.1 15.3 %collective-permute-start.21 = (bf16[3,256,256]{2,1,0:T(8,128)(2,1)S(1)}, bf16[3,256,256]{2,1,0:T(8,128)(2,1)S(1)}, u32[]{:S(2)}, u32[]{:S(2)}) collective-permute-start(bf16[3,256,256]{2,1,0:T(8,128)(2,1)S(1)} %project.30), channel_id=1, source_target_pairs={{0,2},{2,0},{1,3},{3,1},{4,6},{6,4},{5,7},{7,5},{8,10},{10,8},{9,1... | collective-permute-start | bytes 1179656 | tf_op jit(solution)/shard_map/ppermute | solution.py:246
  141.4 9.2 %collective-permute-start.25 = (bf16[216,2048]{1,0:T(8,128)(2,1)S(1)}, bf16[216,2048]{1,0:T(8,128)(2,1)S(1)}, u32[]{:S(2)}, u32[]{:S(2)}) collective-permute-start(bf16[216,2048]{1,0:T(8,128)(2,1)S(1)} %collective-permute-done.19.refs_0_), channel_id=1, source_target_pairs={{1,0},{0,1},{3,2},{2,3},{5,4},{4,5},{7,6},{6,7},{9,8},{8,9},{11,10... | collective-permute-start | bytes 2654216 | tf_op jit(solution)/shard_map/ppermute | solution.py:250
  141.5 9.2 %collective-permute-start.10 = (bf16[48,2048]{1,0:T(8,128)(2,1)S(1)}, bf16[48,2048]{1,0:T(8,128)(2,1)S(1)}, u32[]{:S(2)}, u32[]{:S(2)}) collective-permute-start(bf16[48,2048]{1,0:T(8,128)(2,1)S(1)} %slice.32), channel_id=1, source_target_pairs={{0,4},{4,8},{8,12},{12,0},{1,5},{5,9},{9,13},{13,1},{2,6},{6,10},{... | collective-permute-start | bytes 589832 | tf_op jit(solution)/shard_map/ppermute | solution.py:243
  144.3 14.4 %collective-permute-start.22 = (bf16[3,256,256]{2,1,0:T(8,128)(2,1)S(1)}, bf16[3,256,256]{2,1,0:T(8,128)(2,1)S(1)}, u32[]{:S(2)}, u32[]{:S(2)}) collective-permute-start(bf16[3,256,256]{2,1,0:T(8,128)(2,1)S(1)} %project.29), channel_id=1, source_target_pairs={{0,2},{2,0},{1,3},{3,1},{4,6},{6,4},{5,7},{7,5},{8,10},{10,8},{9,1... | collective-permute-start | bytes 1179656 | tf_op jit(solution)/shard_map/ppermute | solution.py:246
  150.6 3.6 %collective-permute-start.18 = (bf16[48,2048]{1,0:T(8,128)(2,1)S(1)}, bf16[48,2048]{1,0:T(8,128)(2,1)S(1)}, u32[]{:S(2)}, u32[]{:S(2)}) collective-permute-start(bf16[48,2048]{1,0:T(8,128)(2,1)S(1)} %collective-permute-done.10.refs_0_), channel_id=1, source_target_pairs={{1,0},{0,1},{3,2},{2,3},{5,4},{4,5},{7,6},{6,7},{9,8},{8,9},{11,10... | collective-permute-start | bytes 589832 | tf_op jit(solution)/shard_map/ppermute | solution.py:250
  152.8 17.4 %collective-permute-start.26 = (bf16[3,208,256]{2,1,0:T(8,128)(2,1)S(1)}, bf16[3,208,256]{2,1,0:T(8,128)(2,1)S(1)}, u32[]{:S(2)}, u32[]{:S(2)}) collective-permute-start(bf16[3,208,256]{2,1,0:T(8,128)(2,1)S(1)} %project.33), channel_id=1, source_target_pairs={{0,2},{2,0},{1,3},{3,1},{4,6},{6,4},{5,7},{7,5},{8,10},{10,8},{9,1... | collective-permute-start | bytes 958472 | tf_op jit(solution)/shard_map/ppermute | solution.py:246
  156.0 18.6 %collective-permute-start.29 = (bf16[3,48,256]{2,1,0:T(8,128)(2,1)S(1)}, bf16[3,48,256]{2,1,0:T(8,128)(2,1)S(1)}, u32[]{:S(2)}, u32[]{:S(2)}) collective-permute-start(bf16[3,48,256]{2,1,0:T(8,128)(2,1)S(1)} %project.35), channel_id=1, source_target_pairs={{0,2},{2,0},{1,3},{3,1},{4,6},{6,4},{5,7},{7,5},{8,10},{10,8},{9,1... | collective-permute-start | bytes 221192 | tf_op jit(solution)/shard_map/ppermute | solution.py:246
  162.6 14.1 %collective-permute-start.23 = (bf16[512,256]{1,0:T(8,128)(2,1)S(1)}, bf16[512,256]{1,0:T(8,128)(2,1)S(1)}, u32[]{:S(2)}, u32[]{:S(2)}) collective-permute-start(bf16[512,256]{1,0:T(8,128)(2,1)S(1)} %get-tuple-element.99), channel_id=1, source_target_pairs={{0,0},{2,8},{4,4},{6,12},{8,2},{10,10},{12,6},{14,14},{1,1},{3,9},... | collective-permute-start | bytes 786440 | tf_op jit(solution)/shard_map/ppermute | solution.py:414
  163.3 15.2 %collective-permute-start.24 = (bf16[512,256]{1,0:T(8,128)(2,1)S(1)}, bf16[512,256]{1,0:T(8,128)(2,1)S(1)}, u32[]{:S(2)}, u32[]{:S(2)}) collective-permute-start(bf16[512,256]{1,0:T(8,128)(2,1)S(1)} %get-tuple-element.98), channel_id=1, source_target_pairs={{0,8},{2,0},{4,12},{6,4},{8,10},{10,2},{12,14},{14,6},{1,9},{3,1},... | collective-permute-start | bytes 786440 | tf_op jit(solution)/shard_map/ppermute | solution.py:414
  172.5 17.1 %collective-permute-start.27 = (bf16[320,256]{1,0:T(8,128)(2,1)S(1)}, bf16[320,256]{1,0:T(8,128)(2,1)S(1)}, u32[]{:S(2)}, u32[]{:S(2)}) collective-permute-start(bf16[320,256]{1,0:T(8,128)(2,1)S(1)} %get-tuple-element.103), channel_id=1, source_target_pairs={{0,12},{2,4},{4,0},{6,8},{8,14},{10,6},{12,2},{14,10},{1,13},{3,5}... | collective-permute-start | bytes 491528 | tf_op jit(solution)/shard_map/ppermute | solution.py:414
  172.6 17.0 %collective-permute-start.28 = (bf16[320,256]{1,0:T(8,128)(2,1)S(1)}, bf16[320,256]{1,0:T(8,128)(2,1)S(1)}, u32[]{:S(2)}, u32[]{:S(2)}) collective-permute-start(bf16[320,256]{1,0:T(8,128)(2,1)S(1)} %get-tuple-element.102), channel_id=1, source_target_pairs={{0,4},{2,12},{4,8},{6,0},{8,6},{10,14},{12,10},{14,2},{1,5},{3,13}... | collective-permute-start | bytes 491528 | tf_op jit(solution)/shard_map/ppermute | solution.py:414
  176.4 13.1 %collective-permute-start.30 = (bf16[192,256]{1,0:T(8,128)(2,1)S(1)}, bf16[192,256]{1,0:T(8,128)(2,1)S(1)}, u32[]{:S(2)}, u32[]{:S(2)}) collective-permute-start(bf16[192,256]{1,0:T(8,128)(2,1)S(1)} %get-tuple-element.105), channel_id=1, source_target_pairs={{0,12},{2,4},{4,0},{6,8},{8,14},{10,6},{12,2},{14,10},{1,13},{3,5}... | collective-permute-start | bytes 294920 | tf_op jit(solution)/shard_map/ppermute | solution.py:414
  176.8 12.8 %collective-permute-start.31 = (bf16[192,256]{1,0:T(8,128)(2,1)S(1)}, bf16[192,256]{1,0:T(8,128)(2,1)S(1)}, u32[]{:S(2)}, u32[]{:S(2)}) collective-permute-start(bf16[192,256]{1,0:T(8,128)(2,1)S(1)} %get-tuple-element.104), channel_id=1, source_target_pairs={{0,4},{2,12},{4,8},{6,0},{8,6},{10,14},{12,10},{14,2},{1,5},{3,13}... | collective-permute-start | bytes 294920 | tf_op jit(solution)/shard_map/ppermute | solution.py:414
  (12 other events, 79.3 us)

commit v4 on v3

--- a/solution.py
+++ b/solution.py
@@ -171,7 +171,7 @@
         result = result + jnp.dot(gl[...], high, preferred_element_type=F32)
         out[pl.ds(start, STEP), :] = (result * query[pl.ds(start, STEP), :]).astype(BF16)
 
-    unrolled = rows < 512
+    unrolled = True
     repeat((STEP + rows) // tile, unrolled, gate)
     repeat(rows // tile, unrolled, ask)
     repeat(-(-rows // STEP), unrolled, convolve)

time: 192 us -> 191 us (level)
  Pallas kernels: 64.4 us -> 61.2 us
  waiting for transfers between devices: 82.1 us -> 84.3 us
    pallas_call x5, Pallas kernels: 15.4 us -> 12.1 us  [filter_rows(): pl.pallas_call(functools.partial(filter_kernel, plan, terms, rows, flag),...]
  transfers between devices with their start and end apart: 32 -> 32, of which waited for: 11 -> 11; matrix products, arithmetic and copies ran while one was open for 3% -> 3% of each run, Pallas kernels for 33% -> 31%
where the time goes in v4:
time: 191 us; the launch traced here: 190 us
  waiting for transfers between devices  84.3 us (44%)
  Pallas kernels  61.2 us (32%)
  starting transfers between devices  31.5 us (16%)
  local copies, waits for them, and re-layouts  6.4 us (3%)
  other arithmetic  6.06 us (3%)
    ppermute x7, waiting for transfers between devices, shards(): forward = lambda block: lax.ppermute(block, 'ctx', ring)  63 us
    pallas_call x18, Pallas kernels, project(): pl.pallas_call(body, out_shape=jax.ShapeDtypeStruct((streams, rows, kept)...  46.3 us
    ppermute x12, starting transfers between devices, sideways(): lax.ppermute(block, 'width', [(i, (i + w) % across) for i in range(across)])  16.2 us
    pallas_call x5, Pallas kernels, filter_rows(): pl.pallas_call(functools.partial(filter_kernel, plan, terms, rows, flag),...  12.1 us
    ppermute x6, waiting for transfers between devices, returned(): return lax.ppermute(block, ('ctx', 'width'), pairs)  11.1 us
    ppermute x12, waiting for transfers between devices, sideways(): lax.ppermute(block, 'width', [(i, (i + w) % across) for i in range(across)])  10.2 us
    ppermute x6, starting transfers between devices, returned(): return lax.ppermute(block, ('ctx', 'width'), pairs)  9.96 us
    convert_element_type x2, other arithmetic, scaled_part(): return (block * gain[None, :]).astype(BF16)  5.57 us
  transfers between devices with their start and end apart: 32, of which 11 were waited for; matrix products, arithmetic and copies ran while one was open for 3% of the time, Pallas kernels for 31%

profile of v4, /device:TPU:0, one launch (start us, length us, event | category | flops | bytes accessed | tf_op | source)
XLA Modules:
  0.0 190.4 jit_solution(9632883340873094786)
XLA Ops:
  3.0 3.1 %collective-permute-start.2 = (bf16[256,2048]{1,0:T(8,128)(2,1)S(1)}, bf16[256,2048]{1,0:T(8,128)(2,1)S(1)}, u32[]{:S(2)}, u32[]{:S(2)}) collective-permute-start(bf16[256,2048]{1,0:T(8,128)(2,1)S(1)} %multiply_convert_fusion.3.refs_0_), channel_id=1, source_target_pairs={{0,4},{4,8},{8,12},{12,0},{1,5},{5,9},{9,13},{13,1},{2,6},{6,10},{... | collective-permute-start | bytes 3145736 | tf_op jit(solution)/shard_map/ppermute | solution.py:243
  6.0 3.6 %multiply_convert_fusion = (bf16[256,2048]{1,0:T(8,128)(2,1)S(1)}, bf16[256,2048]{1,0:T(8,128)(2,1)S(1)}, bf16[256,2048]{1,0:T(8,128)(2,1)S(1)}) fusion(bf16[512,4096]{1,0:T(8,128)(2,1)} %block, s32[]{:T(128)S(6)} %mul.75, f32[2048]{0:T(1024)S(1)} %get-tuple-element.111, f32[2048]{0:T(1024)S(1)} %get-tuple-element.112, s32[]{:T(128)S(6)} %mul.74), kind=kLoop, calls=%fused_computation.2 | loop fusion | flops 4718592 | bytes 6307848 | tf_op jit(solution)/shard_map/convert_element_type | solution.py:240
  9.7 4.6 %copy-done = bf16[3,4096,1,512]{3,1,2,0:T(8,128)(2,1)S(1)} copy-done((bf16[3,4096,1,512]{3,1,2,0:T(8,128)(2,1)S(1)}, bf16[3,4096,1,512]{3,1,2,0:T(8,128)(2,1)}, u32[]{:S(2)}) %copy-start) | copy-done | bytes 12582936
  14.3 2.8 %project.18 = bf16[3,256,256]{2,1,0:T(8,128)(2,1)S(1)} custom-call(s32[7]{0:T(128)S(1)} %stack.46.places, bf16[256,2048]{1,0:T(8,128)(2,1)S(1)} %multiply_convert_fusion.3.refs_0_, bf16[256,2048]{1,0:T(8,128)(2,1)S(1)} %get-tuple-element.59.refs_1_, bf16[3,4096,512]{2,1,0:T(8,128)(2,1)S(1)} %bitcast.25), custom_call_target="tpu_custom_call" | custom-call | flops 1048576 | bytes 65536 | tf_op jit(solution)/shard_map/project/pallas_call | solution.py:79
  22.8 2.7 %project.19.refs_4_.refs_0_ = bf16[3,256,256]{2,1,0:T(8,128)(2,1)S(1)} custom-call(s32[7]{0:T(128)S(1)} %stack.46.places, bf16[256,2048]{1,0:T(8,128)(2,1)S(1)} %multiply_convert_fusion.3.refs_0_, bf16[256,2048]{1,0:T(8,128)(2,1)S(1)} %get-tuple-element.59.refs_1_, bf16[3,4096,512]{2,1,0:T(8,128)(2,1)S(1)} %bitcast.28), custom_call_target="tpu_custom_call" | custom-call | flops 1048576 | bytes 65536 | tf_op jit(solution)/shard_map/project/pallas_call | solution.py:79
  27.9 4.2 %collective-permute-done.2.refs_0_ = bf16[256,2048]{1,0:T(8,128)(2,1)S(1)} collective-permute-done((bf16[256,2048]{1,0:T(8,128)(2,1)S(1)}, bf16[256,2048]{1,0:T(8,128)(2,1)S(1)}, u32[]{:S(2)}, u32[]{:S(2)}) %collective-permute-start.2) | collective-permute-done | bytes 1048608 | tf_op jit(solution)/shard_map/ppermute | solution.py:243
  33.8 2.8 %project.21 = bf16[3,256,256]{2,1,0:T(8,128)(2,1)S(1)} custom-call(s32[7]{0:T(128)S(1)} %stack.46.places, bf16[264,2048]{1,0:T(8,128)(2,1)S(1)} %fusion.1.refs_0_, bf16[256,2048]{1,0:T(8,128)(2,1)S(1)} %get-tuple-element.68.refs_1_, bf16[3,4096,512]{2,1,0:T(8,128)(2,1)S(1)} %bitcast.29), custom_call_target="tpu_custom_call" | custom-call | flops 1048576 | bytes 65536 | tf_op jit(solution)/shard_map/project/pallas_call | solution.py:79
  36.6 2.7 %project.20.refs_2_ = bf16[3,256,256]{2,1,0:T(8,128)(2,1)S(1)} custom-call(s32[7]{0:T(128)S(1)} %stack.46.places, bf16[264,2048]{1,0:T(8,128)(2,1)S(1)} %fusion.1.refs_0_, bf16[256,2048]{1,0:T(8,128)(2,1)S(1)} %get-tuple-element.68.refs_1_, bf16[3,4096,512]{2,1,0:T(8,128)(2,1)S(1)} %bitcast.30), custom_call_target="tpu_custom_call" | custom-call | flops 1048576 | bytes 65536 | tf_op jit(solution)/shard_map/project/pallas_call | solution.py:79
  39.3 4.3 %collective-permute-done.5.refs_5_.refs_1_ = bf16[3,256,256]{2,1,0:T(8,128)(2,1)S(1)} collective-permute-done((bf16[3,256,256]{2,1,0:T(8,128)(2,1)S(1)}, bf16[3,256,256]{2,1,0:T(8,128)(2,1)S(1)}, u32[]{:S(2)}, u32[]{:S(2)}) %collective-permute-start.5) | collective-permute-done | bytes 393248 | tf_op jit(solution)/shard_map/ppermute | solution.py:246
  43.6 11.6 %collective-permute-done.1.refs_0_ = bf16[264,2048]{1,0:T(8,128)(2,1)S(1)} collective-permute-done((bf16[264,2048]{1,0:T(8,128)(2,1)S(1)}, bf16[264,2048]{1,0:T(8,128)(2,1)S(1)}, u32[]{:S(2)}, u32[]{:S(2)}) %collective-permute-start.1) | collective-permute-done | bytes 1081376 | tf_op jit(solution)/shard_map/ppermute | solution.py:243
  57.0 2.8 %project.25 = bf16[3,256,256]{2,1,0:T(8,128)(2,1)S(1)} custom-call(s32[7]{0:T(128)S(1)} %stack.46.places, bf16[256,2048]{1,0:T(8,128)(2,1)S(1)} %collective-permute-done.2.refs_0_, bf16[256,2048]{1,0:T(8,128)(2,1)S(1)} %collective-permute-done.8.refs_1_, bf16[3,4096,512]{2,1,0:T(8,128)(2,1)S(1)} %bitcast.31), custom_call_target="tpu_custom_call" | custom-call | flops 1048576 | bytes 65536 | tf_op jit(solution)/shard_map/project/pallas_call | solution.py:79
  59.8 2.8 %project.24.refs_0_.refs_4_ = bf16[3,256,256]{2,1,0:T(8,128)(2,1)S(1)} custom-call(s32[7]{0:T(128)S(1)} %stack.46.places, bf16[256,2048]{1,0:T(8,128)(2,1)S(1)} %collective-permute-done.2.refs_0_, bf16[256,2048]{1,0:T(8,128)(2,1)S(1)} %collective-permute-done.8.refs_1_, bf16[3,4096,512]{2,1,0:T(8,128)(2,1)S(1)} %bitcast.32), custom_call_target="tpu_custom_call" | custom-call | flops 1048576 | bytes 65536 | tf_op jit(solution)/shard_map/project/pallas_call | solution.py:79
  62.6 4.2 %collective-permute-done.12.refs_3_ = bf16[3,256,256]{2,1,0:T(8,128)(2,1)S(1)} collective-permute-done((bf16[3,256,256]{2,1,0:T(8,128)(2,1)S(1)}, bf16[3,256,256]{2,1,0:T(8,128)(2,1)S(1)}, u32[]{:S(2)}, u32[]{:S(2)}) %collective-permute-start.12) | collective-permute-done | bytes 393248 | tf_op jit(solution)/shard_map/ppermute | solution.py:246
  66.8 10.9 %collective-permute-done.11.refs_0_ = bf16[256,2048]{1,0:T(8,128)(2,1)S(1)} collective-permute-done((bf16[256,2048]{1,0:T(8,128)(2,1)S(1)}, bf16[256,2048]{1,0:T(8,128)(2,1)S(1)}, u32[]{:S(2)}, u32[]{:S(2)}) %collective-permute-start.11) | collective-permute-done | bytes 1048608 | tf_op jit(solution)/shard_map/ppermute | solution.py:243
  79.5 2.8 %project.23 = bf16[3,256,256]{2,1,0:T(8,128)(2,1)S(1)} custom-call(s32[7]{0:T(128)S(1)} %stack.46.places, bf16[264,2048]{1,0:T(8,128)(2,1)S(1)} %collective-permute-done.1.refs_0_, bf16[264,2048]{1,0:T(8,128)(2,1)S(1)} %collective-permute-done.7.refs_1_, bf16[3,4096,512]{2,1,0:T(8,128)(2,1)S(1)} %bitcast.33), custom_call_target="tpu_custom_call" | custom-call | flops 1048576 | bytes 65536 | tf_op jit(solution)/shard_map/project/pallas_call | solution.py:79
  82.3 2.7 %project.22.refs_2_ = bf16[3,256,256]{2,1,0:T(8,128)(2,1)S(1)} custom-call(s32[7]{0:T(128)S(1)} %stack.46.places, bf16[264,2048]{1,0:T(8,128)(2,1)S(1)} %collective-permute-done.1.refs_0_, bf16[264,2048]{1,0:T(8,128)(2,1)S(1)} %collective-permute-done.7.refs_1_, bf16[3,4096,512]{2,1,0:T(8,128)(2,1)S(1)} %bitcast.34), custom_call_target="tpu_custom_call" | custom-call | flops 1048576 | bytes 65536 | tf_op jit(solution)/shard_map/project/pallas_call | solution.py:79
  85.0 15.9 %collective-permute-done.6.refs_0_ = bf16[264,2048]{1,0:T(8,128)(2,1)S(1)} collective-permute-done((bf16[264,2048]{1,0:T(8,128)(2,1)S(1)}, bf16[264,2048]{1,0:T(8,128)(2,1)S(1)}, u32[]{:S(2)}, u32[]{:S(2)}) %collective-permute-start.6) | collective-permute-done | bytes 1081376 | tf_op jit(solution)/shard_map/ppermute | solution.py:243
  103.1 2.8 %project.26 = bf16[3,256,256]{2,1,0:T(8,128)(2,1)S(1)} custom-call(s32[7]{0:T(128)S(1)} %stack.46.places, bf16[256,2048]{1,0:T(8,128)(2,1)S(1)} %collective-permute-done.11.refs_0_, bf16[256,2048]{1,0:T(8,128)(2,1)S(1)} %collective-permute-done.14.refs_1_, bf16[3,4096,512]{2,1,0:T(8,128)(2,1)S(1)} %bitcast.35), custom_call_target="tpu_custom_call" | custom-call | flops 1048576 | bytes 65536 | tf_op jit(solution)/shard_map/project/pallas_call | solution.py:79
  106.2 2.7 %filter.5 = bf16[512,256]{1,0:T(8,128)(2,1)S(1)} custom-call(s32[7]{0:T(128)S(1)} %stack.46.places, bf16[3,256,256]{2,1,0:T(8,128)(2,1)S(1)} %project.24.refs_0_.refs_4_, bf16[3,256,256]{2,1,0:T(8,128)(2,1)S(1)} %collective-permute-done.9.refs_1_.refs_5_, bf16[3,256,256]{2,1,0:T(8,128)(2,1)S(1)} %project.20.refs_2_, ...), custom_call_target="tpu_custom_call" | custom-call | flops 1048576 | bytes 65536 | tf_op jit(solution)/shard_map/filter/pallas_call | solution.py:187
  108.9 2.7 %project.27.refs_0_.refs_4_ = bf16[3,256,256]{2,1,0:T(8,128)(2,1)S(1)} custom-call(s32[7]{0:T(128)S(1)} %stack.46.places, bf16[256,2048]{1,0:T(8,128)(2,1)S(1)} %collective-permute-done.11.refs_0_, bf16[256,2048]{1,0:T(8,128)(2,1)S(1)} %collective-permute-done.14.refs_1_, bf16[3,4096,512]{2,1,0:T(8,128)(2,1)S(1)} %bitcast.36), custom_call_target="tpu_custom_call" | custom-call | flops 1048576 | bytes 65536 | tf_op jit(solution)/shard_map/project/pallas_call | solution.py:79
  113.2 10.1 %collective-permute-done.13.refs_0_ = bf16[256,2048]{1,0:T(8,128)(2,1)S(1)} collective-permute-done((bf16[256,2048]{1,0:T(8,128)(2,1)S(1)}, bf16[256,2048]{1,0:T(8,128)(2,1)S(1)}, u32[]{:S(2)}, u32[]{:S(2)}) %collective-permute-start.13) | collective-permute-done | bytes 1048608 | tf_op jit(solution)/shard_map/ppermute | solution.py:243
  123.4 2.8 %project.30 = bf16[3,256,256]{2,1,0:T(8,128)(2,1)S(1)} custom-call(s32[7]{0:T(128)S(1)} %stack.46.places, bf16[264,2048]{1,0:T(8,128)(2,1)S(1)} %collective-permute-done.6.refs_0_, bf16[264,2048]{1,0:T(8,128)(2,1)S(1)} %collective-permute-done.20.refs_1_, bf16[3,4096,512]{2,1,0:T(8,128)(2,1)S(1)} %bitcast.37), custom_call_target="tpu_custom_call" | custom-call | flops 1048576 | bytes 65536 | tf_op jit(solution)/shard_map/project/pallas_call | solution.py:79
  127.9 2.7 %filter.6 = bf16[512,256]{1,0:T(8,128)(2,1)S(1)} custom-call(s32[7]{0:T(128)S(1)} %stack.46.places, bf16[3,256,256]{2,1,0:T(8,128)(2,1)S(1)} %project.27.refs_0_.refs_4_, bf16[3,256,256]{2,1,0:T(8,128)(2,1)S(1)} %collective-permute-done.16.refs_1_.refs_5_, bf16[3,256,256]{2,1,0:T(8,128)(2,1)S(1)} %project.22.refs_2_, ...), custom_call_target="tpu_custom_call" | custom-call | flops 1048576 | bytes 65536 | tf_op jit(solution)/shard_map/filter/pallas_call | solution.py:187
  130.6 2.8 %project.31.refs_2_ = bf16[3,256,256]{2,1,0:T(8,128)(2,1)S(1)} custom-call(s32[7]{0:T(128)S(1)} %stack.46.places, bf16[264,2048]{1,0:T(8,128)(2,1)S(1)} %collective-permute-done.6.refs_0_, bf16[264,2048]{1,0:T(8,128)(2,1)S(1)} %collective-permute-done.20.refs_1_, bf16[3,4096,512]{2,1,0:T(8,128)(2,1)S(1)} %bitcast.38), custom_call_target="tpu_custom_call" | custom-call | flops 1048576 | bytes 65536 | tf_op jit(solution)/shard_map/project/pallas_call | solution.py:79
  133.4 8.1 %collective-permute-done.19.refs_0_ = bf16[216,2048]{1,0:T(8,128)(2,1)S(1)} collective-permute-done((bf16[216,2048]{1,0:T(8,128)(2,1)S(1)}, bf16[216,2048]{1,0:T(8,128)(2,1)S(1)}, u32[]{:S(2)}, u32[]{:S(2)}) %collective-permute-start.19) | collective-permute-done | bytes 884768 | tf_op jit(solution)/shard_map/ppermute | solution.py:243
  141.8 2.8 %project.29 = bf16[3,256,256]{2,1,0:T(8,128)(2,1)S(1)} custom-call(s32[7]{0:T(128)S(1)} %stack.46.places, bf16[256,2048]{1,0:T(8,128)(2,1)S(1)} %collective-permute-done.13.refs_0_, bf16[256,2048]{1,0:T(8,128)(2,1)S(1)} %collective-permute-done.17.refs_1_, bf16[3,4096,512]{2,1,0:T(8,128)(2,1)S(1)} %bitcast.39), custom_call_target="tpu_custom_call" | custom-call | flops 1048576 | bytes 65536 | tf_op jit(solution)/shard_map/project/pallas_call | solution.py:79
  146.0 2.7 %project.28.refs_0_.refs_2_ = bf16[3,256,256]{2,1,0:T(8,128)(2,1)S(1)} custom-call(s32[7]{0:T(128)S(1)} %stack.46.places, bf16[256,2048]{1,0:T(8,128)(2,1)S(1)} %collective-permute-done.13.refs_0_, bf16[256,2048]{1,0:T(8,128)(2,1)S(1)} %collective-permute-done.17.refs_1_, bf16[3,4096,512]{2,1,0:T(8,128)(2,1)S(1)} %bitcast.40), custom_call_target="tpu_custom_call" | custom-call | flops 1048576 | bytes 65536 | tf_op jit(solution)/shard_map/project/pallas_call | solution.py:79
  150.9 2.1 %project.33 = bf16[3,208,256]{2,1,0:T(8,128)(2,1)S(1)} custom-call(s32[7]{0:T(128)S(1)} %stack.46.places, bf16[216,2048]{1,0:T(8,128)(2,1)S(1)} %collective-permute-done.19.refs_0_, bf16[216,2048]{1,0:T(8,128)(2,1)S(1)} %collective-permute-done.25.refs_1_, bf16[3,4096,512]{2,1,0:T(8,128)(2,1)S(1)} %bitcast.41), custom_call_target="tpu_custom_call" | custom-call | flops 1048576 | bytes 65536 | tf_op jit(solution)/shard_map/project/pallas_call | solution.py:79
  159.0 2.7 %filter.7 = bf16[512,256]{1,0:T(8,128)(2,1)S(1)} custom-call(s32[7]{0:T(128)S(1)} %stack.46.places, bf16[3,256,256]{2,1,0:T(8,128)(2,1)S(1)} %project.28.refs_0_.refs_2_, bf16[3,256,256]{2,1,0:T(8,128)(2,1)S(1)} %collective-permute-done.22.refs_1_.refs_3_, bf16[3,256,256]{2,1,0:T(8,128)(2,1)S(1)} %project.31.refs_2_, ...), custom_call_target="tpu_custom_call" | custom-call | flops 1048576 | bytes 65536 | tf_op jit(solution)/shard_map/filter/pallas_call | solution.py:187
  162.4 5.1 %collective-permute-start.24 = (bf16[512,256]{1,0:T(8,128)(2,1)S(1)}, bf16[512,256]{1,0:T(8,128)(2,1)S(1)}, u32[]{:S(2)}, u32[]{:S(2)}) collective-permute-start(bf16[512,256]{1,0:T(8,128)(2,1)S(1)} %get-tuple-element.98), channel_id=1, source_target_pairs={{0,8},{2,0},{4,12},{6,4},{8,10},{10,2},{12,14},{14,6},{1,9},{3,1},... | collective-permute-start | bytes 786440 | tf_op jit(solution)/shard_map/ppermute | solution.py:414
  169.3 2.2 %filter.8 = bf16[320,256]{1,0:T(8,128)(2,1)S(1)} custom-call(s32[7]{0:T(128)S(1)} %stack.46.places, bf16[3,208,256]{2,1,0:T(8,128)(2,1)S(1)} %project.32.refs_0_.refs_4_, bf16[3,208,256]{2,1,0:T(8,128)(2,1)S(1)} %collective-permute-done.26.refs_1_.refs_5_, bf16[3,256,256]{2,1,0:T(8,128)(2,1)S(1)} %project.28.refs_0_.refs_2_, ...), custom_call_target="tpu_custom_call" | custom-call | flops 1048576 | bytes 65536 | tf_op jit(solution)/shard_map/filter/pallas_call | solution.py:187
  177.6 11.1 %collective-permute-done.30.refs_4_ = bf16[192,256]{1,0:T(8,128)(2,1)S(1)} collective-permute-done((bf16[192,256]{1,0:T(8,128)(2,1)S(1)}, bf16[192,256]{1,0:T(8,128)(2,1)S(1)}, u32[]{:S(2)}, u32[]{:S(2)}) %collective-permute-start.30) | collective-permute-done | bytes 98336 | tf_op jit(solution)/shard_map/ppermute | solution.py:414
  (107 shorter events, 41.9 us)
Async XLA Ops:
  3.0 29.1 %collective-permute-start.2 = (bf16[256,2048]{1,0:T(8,128)(2,1)S(1)}, bf16[256,2048]{1,0:T(8,128)(2,1)S(1)}, u32[]{:S(2)}, u32[]{:S(2)}) collective-permute-start(bf16[256,2048]{1,0:T(8,128)(2,1)S(1)} %multiply_convert_fusion.3.refs_0_), channel_id=1, source_target_pairs={{0,4},{4,8},{8,12},{12,0},{1,5},{5,9},{9,13},{13,1},{2,6},{6,10},{... | collective-permute-start | bytes 3145736 | tf_op jit(solution)/shard_map/ppermute | solution.py:243
  17.7 9.6 %collective-permute-start.4 = (f32[128,256]{1,0:T(8,128)S(1)}, f32[128,256]{1,0:T(8,128)S(1)}, u32[]{:S(2)}, u32[]{:S(2)}) collective-permute-start(f32[128,256]{1,0:T(8,128)S(1)} %bitcast.45), channel_id=1, source_target_pairs={{0,2},{2,0},{1,3},{3,1},{4,6},{6,4},{5,7},{7,5},{8,10},{10,8},{9,1... | collective-permute-start | bytes 393224 | tf_op jit(solution)/shard_map/ppermute | solution.py:246
  19.3 8.0 %collective-permute-start.3 = (f32[3,3,256]{2,1,0:T(4,128)S(1)}, f32[3,3,256]{2,1,0:T(4,128)S(1)}, u32[]{:S(2)}, u32[]{:S(2)}) collective-permute-start(f32[3,3,256]{2,1,0:T(4,128)S(1)} %bitcast.46), channel_id=1, source_target_pairs={{0,2},{2,0},{1,3},{3,1},{4,6},{6,4},{5,7},{7,5},{8,10},{10,8},{9,1... | collective-permute-start | bytes 27656 | tf_op jit(solution)/shard_map/ppermute | solution.py:246
  21.3 4.2 %collective-permute-start = (f32[8,512]{1,0:T(8,128)S(1)}, f32[8,512]{1,0:T(8,128)S(1)}, u32[]{:S(2)}, u32[]{:S(2)}) collective-permute-start(f32[8,512]{1,0:T(8,128)S(1)} %power.1), channel_id=1, source_target_pairs={{0,2},{2,0},{1,3},{3,1},{4,6},{6,4},{5,7},{7,5},{8,10},{10,8},{9,1... | collective-permute-start | bytes 49160 | tf_op jit(solution)/shard_map/ppermute | solution.py:246
  25.7 29.5 %collective-permute-start.1 = (bf16[264,2048]{1,0:T(8,128)(2,1)S(1)}, bf16[264,2048]{1,0:T(8,128)(2,1)S(1)}, u32[]{:S(2)}, u32[]{:S(2)}) collective-permute-start(bf16[264,2048]{1,0:T(8,128)(2,1)S(1)} %fusion.1.refs_0_), channel_id=1, source_target_pairs={{0,4},{4,8},{8,12},{12,0},{1,5},{5,9},{9,13},{13,1},{2,6},{6,10},{... | collective-permute-start | bytes 3244040 | tf_op jit(solution)/shard_map/ppermute | solution.py:243
  32.1 24.9 %collective-permute-start.8 = (bf16[256,2048]{1,0:T(8,128)(2,1)S(1)}, bf16[256,2048]{1,0:T(8,128)(2,1)S(1)}, u32[]{:S(2)}, u32[]{:S(2)}) collective-permute-start(bf16[256,2048]{1,0:T(8,128)(2,1)S(1)} %collective-permute-done.2.refs_0_), channel_id=1, source_target_pairs={{1,0},{0,1},{3,2},{2,3},{5,4},{4,5},{7,6},{6,7},{9,8},{8,9},{11,10... | collective-permute-start | bytes 3145736 | tf_op jit(solution)/shard_map/ppermute | solution.py:250
  32.1 45.6 %collective-permute-start.11 = (bf16[256,2048]{1,0:T(8,128)(2,1)S(1)}, bf16[256,2048]{1,0:T(8,128)(2,1)S(1)}, u32[]{:S(2)}, u32[]{:S(2)}) collective-permute-start(bf16[256,2048]{1,0:T(8,128)(2,1)S(1)} %collective-permute-done.2.refs_0_), channel_id=1, source_target_pairs={{0,4},{4,8},{8,12},{12,0},{1,5},{5,9},{9,13},{13,1},{2,6},{6,10},{... | collective-permute-start | bytes 3145736 | tf_op jit(solution)/shard_map/ppermute | solution.py:243
  32.1 11.5 %collective-permute-start.5 = (bf16[3,256,256]{2,1,0:T(8,128)(2,1)S(1)}, bf16[3,256,256]{2,1,0:T(8,128)(2,1)S(1)}, u32[]{:S(2)}, u32[]{:S(2)}) collective-permute-start(bf16[3,256,256]{2,1,0:T(8,128)(2,1)S(1)} %project.18), channel_id=1, source_target_pairs={{0,2},{2,0},{1,3},{3,1},{4,6},{6,4},{5,7},{7,5},{8,10},{10,8},{9,1... | collective-permute-start | bytes 1179656 | tf_op jit(solution)/shard_map/ppermute | solution.py:246
  55.2 24.2 %collective-permute-start.7 = (bf16[264,2048]{1,0:T(8,128)(2,1)S(1)}, bf16[264,2048]{1,0:T(8,128)(2,1)S(1)}, u32[]{:S(2)}, u32[]{:S(2)}) collective-permute-start(bf16[264,2048]{1,0:T(8,128)(2,1)S(1)} %collective-permute-done.1.refs_0_), channel_id=1, source_target_pairs={{1,0},{0,1},{3,2},{2,3},{5,4},{4,5},{7,6},{6,7},{9,8},{8,9},{11,10... | collective-permute-start | bytes 3244040 | tf_op jit(solution)/shard_map/ppermute | solution.py:250
  55.2 45.6 %collective-permute-start.6 = (bf16[264,2048]{1,0:T(8,128)(2,1)S(1)}, bf16[264,2048]{1,0:T(8,128)(2,1)S(1)}, u32[]{:S(2)}, u32[]{:S(2)}) collective-permute-start(bf16[264,2048]{1,0:T(8,128)(2,1)S(1)} %collective-permute-done.1.refs_0_), channel_id=1, source_target_pairs={{0,4},{4,8},{8,12},{12,0},{1,5},{5,9},{9,13},{13,1},{2,6},{6,10},{... | collective-permute-start | bytes 3244040 | tf_op jit(solution)/shard_map/ppermute | solution.py:243
  55.3 11.5 %collective-permute-start.12 = (bf16[3,256,256]{2,1,0:T(8,128)(2,1)S(1)}, bf16[3,256,256]{2,1,0:T(8,128)(2,1)S(1)}, u32[]{:S(2)}, u32[]{:S(2)}) collective-permute-start(bf16[3,256,256]{2,1,0:T(8,128)(2,1)S(1)} %project.21), channel_id=1, source_target_pairs={{0,2},{2,0},{1,3},{3,1},{4,6},{6,4},{5,7},{7,5},{8,10},{10,8},{9,1... | collective-permute-start | bytes 1179656 | tf_op jit(solution)/shard_map/ppermute | solution.py:246
  77.7 25.4 %collective-permute-start.14 = (bf16[256,2048]{1,0:T(8,128)(2,1)S(1)}, bf16[256,2048]{1,0:T(8,128)(2,1)S(1)}, u32[]{:S(2)}, u32[]{:S(2)}) collective-permute-start(bf16[256,2048]{1,0:T(8,128)(2,1)S(1)} %collective-permute-done.11.refs_0_), channel_id=1, source_target_pairs={{1,0},{0,1},{3,2},{2,3},{5,4},{4,5},{7,6},{6,7},{9,8},{8,9},{11,10... | collective-permute-start | bytes 3145736 | tf_op jit(solution)/shard_map/ppermute | solution.py:250
  77.7 23.2 %collective-permute-start.9 = (bf16[3,256,256]{2,1,0:T(8,128)(2,1)S(1)}, bf16[3,256,256]{2,1,0:T(8,128)(2,1)S(1)}, u32[]{:S(2)}, u32[]{:S(2)}) collective-permute-start(bf16[3,256,256]{2,1,0:T(8,128)(2,1)S(1)} %project.25), channel_id=1, source_target_pairs={{0,2},{2,0},{1,3},{3,1},{4,6},{6,4},{5,7},{7,5},{8,10},{10,8},{9,1... | collective-permute-start | bytes 1179656 | tf_op jit(solution)/shard_map/ppermute | solution.py:246
  79.4 43.9 %collective-permute-start.13 = (bf16[256,2048]{1,0:T(8,128)(2,1)S(1)}, bf16[256,2048]{1,0:T(8,128)(2,1)S(1)}, u32[]{:S(2)}, u32[]{:S(2)}) collective-permute-start(bf16[256,2048]{1,0:T(8,128)(2,1)S(1)} %collective-permute-done.11.refs_0_), channel_id=1, source_target_pairs={{0,4},{4,8},{8,12},{12,0},{1,5},{5,9},{9,13},{13,1},{2,6},{6,10},{... | collective-permute-start | bytes 3145736 | tf_op jit(solution)/shard_map/ppermute | solution.py:243
  100.9 22.5 %collective-permute-start.20 = (bf16[264,2048]{1,0:T(8,128)(2,1)S(1)}, bf16[264,2048]{1,0:T(8,128)(2,1)S(1)}, u32[]{:S(2)}, u32[]{:S(2)}) collective-permute-start(bf16[264,2048]{1,0:T(8,128)(2,1)S(1)} %collective-permute-done.6.refs_0_), channel_id=1, source_target_pairs={{1,0},{0,1},{3,2},{2,3},{5,4},{4,5},{7,6},{6,7},{9,8},{8,9},{11,10... | collective-permute-start | bytes 3244040 | tf_op jit(solution)/shard_map/ppermute | solution.py:250
  101.0 40.4 %collective-permute-start.19 = (bf16[216,2048]{1,0:T(8,128)(2,1)S(1)}, bf16[216,2048]{1,0:T(8,128)(2,1)S(1)}, u32[]{:S(2)}, u32[]{:S(2)}) collective-permute-start(bf16[216,2048]{1,0:T(8,128)(2,1)S(1)} %slice.34), channel_id=1, source_target_pairs={{0,4},{4,8},{8,12},{12,0},{1,5},{5,9},{9,13},{13,1},{2,6},{6,10},{... | collective-permute-start | bytes 2654216 | tf_op jit(solution)/shard_map/ppermute | solution.py:243
  101.3 12.0 %collective-permute-start.15 = (bf16[3,256,256]{2,1,0:T(8,128)(2,1)S(1)}, bf16[3,256,256]{2,1,0:T(8,128)(2,1)S(1)}, u32[]{:S(2)}, u32[]{:S(2)}) collective-permute-start(bf16[3,256,256]{2,1,0:T(8,128)(2,1)S(1)} %project.23), channel_id=1, source_target_pairs={{0,2},{2,0},{1,3},{3,1},{4,6},{6,4},{5,7},{7,5},{8,10},{10,8},{9,1... | collective-permute-start | bytes 1179656 | tf_op jit(solution)/shard_map/ppermute | solution.py:246
  105.9 17.5 %collective-permute-start.16 = (bf16[3,256,256]{2,1,0:T(8,128)(2,1)S(1)}, bf16[3,256,256]{2,1,0:T(8,128)(2,1)S(1)}, u32[]{:S(2)}, u32[]{:S(2)}) collective-permute-start(bf16[3,256,256]{2,1,0:T(8,128)(2,1)S(1)} %project.26), channel_id=1, source_target_pairs={{0,2},{2,0},{1,3},{3,1},{4,6},{6,4},{5,7},{7,5},{8,10},{10,8},{9,1... | collective-permute-start | bytes 1179656 | tf_op jit(solution)/shard_map/ppermute | solution.py:246
  123.4 18.4 %collective-permute-start.17 = (bf16[256,2048]{1,0:T(8,128)(2,1)S(1)}, bf16[256,2048]{1,0:T(8,128)(2,1)S(1)}, u32[]{:S(2)}, u32[]{:S(2)}) collective-permute-start(bf16[256,2048]{1,0:T(8,128)(2,1)S(1)} %collective-permute-done.13.refs_0_), channel_id=1, source_target_pairs={{1,0},{0,1},{3,2},{2,3},{5,4},{4,5},{7,6},{6,7},{9,8},{8,9},{11,10... | collective-permute-start | bytes 3145736 | tf_op jit(solution)/shard_map/ppermute | solution.py:250
  126.1 15.3 %collective-permute-start.21 = (bf16[3,256,256]{2,1,0:T(8,128)(2,1)S(1)}, bf16[3,256,256]{2,1,0:T(8,128)(2,1)S(1)}, u32[]{:S(2)}, u32[]{:S(2)}) collective-permute-start(bf16[3,256,256]{2,1,0:T(8,128)(2,1)S(1)} %project.30), channel_id=1, source_target_pairs={{0,2},{2,0},{1,3},{3,1},{4,6},{6,4},{5,7},{7,5},{8,10},{10,8},{9,1... | collective-permute-start | bytes 1179656 | tf_op jit(solution)/shard_map/ppermute | solution.py:246
  141.4 9.4 %collective-permute-start.25 = (bf16[216,2048]{1,0:T(8,128)(2,1)S(1)}, bf16[216,2048]{1,0:T(8,128)(2,1)S(1)}, u32[]{:S(2)}, u32[]{:S(2)}) collective-permute-start(bf16[216,2048]{1,0:T(8,128)(2,1)S(1)} %collective-permute-done.19.refs_0_), channel_id=1, source_target_pairs={{1,0},{0,1},{3,2},{2,3},{5,4},{4,5},{7,6},{6,7},{9,8},{8,9},{11,10... | collective-permute-start | bytes 2654216 | tf_op jit(solution)/shard_map/ppermute | solution.py:250
  141.5 9.4 %collective-permute-start.10 = (bf16[48,2048]{1,0:T(8,128)(2,1)S(1)}, bf16[48,2048]{1,0:T(8,128)(2,1)S(1)}, u32[]{:S(2)}, u32[]{:S(2)}) collective-permute-start(bf16[48,2048]{1,0:T(8,128)(2,1)S(1)} %slice.32), channel_id=1, source_target_pairs={{0,4},{4,8},{8,12},{12,0},{1,5},{5,9},{9,13},{13,1},{2,6},{6,10},{... | collective-permute-start | bytes 589832 | tf_op jit(solution)/shard_map/ppermute | solution.py:243
  144.6 14.4 %collective-permute-start.22 = (bf16[3,256,256]{2,1,0:T(8,128)(2,1)S(1)}, bf16[3,256,256]{2,1,0:T(8,128)(2,1)S(1)}, u32[]{:S(2)}, u32[]{:S(2)}) collective-permute-start(bf16[3,256,256]{2,1,0:T(8,128)(2,1)S(1)} %project.29), channel_id=1, source_target_pairs={{0,2},{2,0},{1,3},{3,1},{4,6},{6,4},{5,7},{7,5},{8,10},{10,8},{9,1... | collective-permute-start | bytes 1179656 | tf_op jit(solution)/shard_map/ppermute | solution.py:246
  150.9 3.6 %collective-permute-start.18 = (bf16[48,2048]{1,0:T(8,128)(2,1)S(1)}, bf16[48,2048]{1,0:T(8,128)(2,1)S(1)}, u32[]{:S(2)}, u32[]{:S(2)}) collective-permute-start(bf16[48,2048]{1,0:T(8,128)(2,1)S(1)} %collective-permute-done.10.refs_0_), channel_id=1, source_target_pairs={{1,0},{0,1},{3,2},{2,3},{5,4},{4,5},{7,6},{6,7},{9,8},{8,9},{11,10... | collective-permute-start | bytes 589832 | tf_op jit(solution)/shard_map/ppermute | solution.py:250
  153.0 16.3 %collective-permute-start.26 = (bf16[3,208,256]{2,1,0:T(8,128)(2,1)S(1)}, bf16[3,208,256]{2,1,0:T(8,128)(2,1)S(1)}, u32[]{:S(2)}, u32[]{:S(2)}) collective-permute-start(bf16[3,208,256]{2,1,0:T(8,128)(2,1)S(1)} %project.33), channel_id=1, source_target_pairs={{0,2},{2,0},{1,3},{3,1},{4,6},{6,4},{5,7},{7,5},{8,10},{10,8},{9,1... | collective-permute-start | bytes 958472 | tf_op jit(solution)/shard_map/ppermute | solution.py:246
  156.2 17.5 %collective-permute-start.29 = (bf16[3,48,256]{2,1,0:T(8,128)(2,1)S(1)}, bf16[3,48,256]{2,1,0:T(8,128)(2,1)S(1)}, u32[]{:S(2)}, u32[]{:S(2)}) collective-permute-start(bf16[3,48,256]{2,1,0:T(8,128)(2,1)S(1)} %project.35), channel_id=1, source_target_pairs={{0,2},{2,0},{1,3},{3,1},{4,6},{6,4},{5,7},{7,5},{8,10},{10,8},{9,1... | collective-permute-start | bytes 221192 | tf_op jit(solution)/shard_map/ppermute | solution.py:246
  161.7 14.1 %collective-permute-start.23 = (bf16[512,256]{1,0:T(8,128)(2,1)S(1)}, bf16[512,256]{1,0:T(8,128)(2,1)S(1)}, u32[]{:S(2)}, u32[]{:S(2)}) collective-permute-start(bf16[512,256]{1,0:T(8,128)(2,1)S(1)} %get-tuple-element.99), channel_id=1, source_target_pairs={{0,0},{2,8},{4,4},{6,12},{8,2},{10,10},{12,6},{14,14},{1,1},{3,9},... | collective-permute-start | bytes 786440 | tf_op jit(solution)/shard_map/ppermute | solution.py:414
  162.4 15.2 %collective-permute-start.24 = (bf16[512,256]{1,0:T(8,128)(2,1)S(1)}, bf16[512,256]{1,0:T(8,128)(2,1)S(1)}, u32[]{:S(2)}, u32[]{:S(2)}) collective-permute-start(bf16[512,256]{1,0:T(8,128)(2,1)S(1)} %get-tuple-element.98), channel_id=1, source_target_pairs={{0,8},{2,0},{4,12},{6,4},{8,10},{10,2},{12,14},{14,6},{1,9},{3,1},... | collective-permute-start | bytes 786440 | tf_op jit(solution)/shard_map/ppermute | solution.py:414
  171.6 17.1 %collective-permute-start.27 = (bf16[320,256]{1,0:T(8,128)(2,1)S(1)}, bf16[320,256]{1,0:T(8,128)(2,1)S(1)}, u32[]{:S(2)}, u32[]{:S(2)}) collective-permute-start(bf16[320,256]{1,0:T(8,128)(2,1)S(1)} %get-tuple-element.103), channel_id=1, source_target_pairs={{0,12},{2,4},{4,0},{6,8},{8,14},{10,6},{12,2},{14,10},{1,13},{3,5}... | collective-permute-start | bytes 491528 | tf_op jit(solution)/shard_map/ppermute | solution.py:414
  171.7 17.0 %collective-permute-start.28 = (bf16[320,256]{1,0:T(8,128)(2,1)S(1)}, bf16[320,256]{1,0:T(8,128)(2,1)S(1)}, u32[]{:S(2)}, u32[]{:S(2)}) collective-permute-start(bf16[320,256]{1,0:T(8,128)(2,1)S(1)} %get-tuple-element.102), channel_id=1, source_target_pairs={{0,4},{2,12},{4,8},{6,0},{8,6},{10,14},{12,10},{14,2},{1,5},{3,13}... | collective-permute-start | bytes 491528 | tf_op jit(solution)/shard_map/ppermute | solution.py:414
  175.5 13.2 %collective-permute-start.30 = (bf16[192,256]{1,0:T(8,128)(2,1)S(1)}, bf16[192,256]{1,0:T(8,128)(2,1)S(1)}, u32[]{:S(2)}, u32[]{:S(2)}) collective-permute-start(bf16[192,256]{1,0:T(8,128)(2,1)S(1)} %get-tuple-element.105), channel_id=1, source_target_pairs={{0,12},{2,4},{4,0},{6,8},{8,14},{10,6},{12,2},{14,10},{1,13},{3,5}... | collective-permute-start | bytes 294920 | tf_op jit(solution)/shard_map/ppermute | solution.py:414
  175.9 12.8 %collective-permute-start.31 = (bf16[192,256]{1,0:T(8,128)(2,1)S(1)}, bf16[192,256]{1,0:T(8,128)(2,1)S(1)}, u32[]{:S(2)}, u32[]{:S(2)}) collective-permute-start(bf16[192,256]{1,0:T(8,128)(2,1)S(1)} %get-tuple-element.104), channel_id=1, source_target_pairs={{0,4},{2,12},{4,8},{6,0},{8,6},{10,14},{12,10},{14,2},{1,5},{3,13}... | collective-permute-start | bytes 294920 | tf_op jit(solution)/shard_map/ppermute | solution.py:414
  (12 other events, 79.3 us)
